TPU v7x, 32 devices: a whole 2x2x4 slice. The times are simulated.
32 devices in a mesh: rows: 8 (over y, x, core), cols: 4 (over z).
Axes of the slice: x: 2, y: 2, z: 4, core: 2. Of those that a mesh axis runs over, the one named last changes fastest.
Arguments:
- up_a: bfloat16 [28672, 4096], P('rows', 'cols'), may hold values from -6 to 6
- gate_a: bfloat16 [28672, 4096], P('rows', 'cols'), may hold values from -6 to 6
- down_a: bfloat16 [28672, 4096], P('rows', 'cols'), may hold values from -6 to 6
- up_b: bfloat16 [28672, 4096], P('rows', 'cols'), may hold values from -6 to 6
- gate_b: bfloat16 [28672, 4096], P('rows', 'cols'), may hold values from -6 to 6
- down_b: bfloat16 [28672, 4096], P('rows', 'cols'), may hold values from -6 to 6
- perm: int32 [28672], P('rows'), may hold values from 0 to 28671, as said below
Outputs:
- costs: float32 [28672, 256], P('rows', 'cols')
- up_mean: bfloat16 [28672, 4096], P('rows', 'cols')
- gate_mean: bfloat16 [28672, 4096], P('rows', 'cols')
- down_mean: bfloat16 [28672, 4096], P('rows', 'cols')
Inputs may be any that keep to these rules, and one draw needn't show every extreme that they name: perm is a permutation of the hidden units. Split positions and values alike into aligned blocks of 3584: the positions of one block take at most 448 values from any one block, and exactly 448 from some block.
All inputs are finite; a program needn't handle non-finite values.
Results may differ from a plain program's by a relative error of at most 0.001.
Values may be sent and summed in bfloat16 or wider, within the bound.
A program may use at most 192 MiB of HBM per device.

v0:
```python
import jax
import jax.numpy as jnp
from jax import lax
from jax.sharding import PartitionSpec as P

D = 4096
A_DEV = 32


def cols_reduce(parts):
    count = lax.axis_size("cols")
    me = lax.axis_index("cols")
    moved = [lax.dynamic_index_in_dim(parts, me, 0, keepdims=False)]
    for shift in range(1, count):
        piece = lax.dynamic_index_in_dim(parts, (me + shift) % count, 0, keepdims=False)
        moved.append(lax.ppermute(piece, "cols", [(c, (c + shift) % count) for c in range(count)]))
    return moved


def pick(array, index):
    return array.at[index].get(mode="promise_in_bounds")


def mix(initial, picked):
    return ((initial.astype(jnp.float32) + picked.astype(jnp.float32)) * 0.5).astype(jnp.bfloat16)


def local(up_a, gate_a, down_a, up_b, gate_b, down_b, perm):
    row_count = up_a.shape[0]
    features = up_a.shape[1]
    stride = row_count // A_DEV
    cost_scale = (2.0 * D) ** (-0.5)
    peers = lax.axis_size("rows")
    cols = lax.axis_size("cols")
    capacity = max(2, (row_count + peers - 1) // peers)

    source = perm // row_count
    local_row = perm % row_count
    blocks = jnp.arange(peers, dtype=jnp.int32)
    matches = (source[None, :] == blocks[:, None]).astype(jnp.int32)
    arrival_rank = jnp.sum(jnp.cumsum(matches, axis=1) * matches, axis=0) - 1
    high = (local_row // 256).astype(jnp.bfloat16)
    low = (local_row % 256).astype(jnp.bfloat16)
    halves = jnp.stack([high, low])[:, None, :] * matches.astype(jnp.bfloat16)[None]
    at_rank = (arrival_rank[None, :] == jnp.arange(capacity, dtype=jnp.int32)[:, None]).astype(jnp.bfloat16)
    found = jnp.einsum("hsi,ri->hsr", halves, at_rank, preferred_element_type=jnp.float32)
    wanted = found[0].astype(jnp.int32) * 256 + found[1].astype(jnp.int32)
    wanted, up_held, gate_held = lax.optimization_barrier((wanted, up_a, gate_a))
    window = jnp.concatenate([up_held[::stride], gate_held[::stride]], axis=0)
    asked_rows = lax.all_to_all(wanted, "rows", split_axis=0, concat_axis=0, tiled=True)

    def exchange(rows):
        moved = rows.reshape(peers, -1, rows.shape[1])
        moved = lax.all_to_all(moved, "rows", split_axis=0, concat_axis=0, tiled=True)
        return moved.reshape(-1, rows.shape[1])

    asked = asked_rows.reshape(-1)
    slot = source * capacity + arrival_rank

    asked, window = lax.optimization_barrier((asked, window))
    sent = jnp.broadcast_to(window[None], (peers,) + window.shape)
    pieces = lax.all_to_all(sent, "rows", split_axis=0, concat_axis=0, tiled=True)
    up_rows = pick(up_b, asked)
    up_rows, pieces = lax.optimization_barrier((up_rows, pieces))
    up_moved = exchange(up_rows)
    pieces = pieces.reshape(peers, 2, A_DEV, features)
    wide = pieces.transpose(1, 2, 0, 3).reshape(2, A_DEV * peers, features)

    partial_value = jnp.einsum("kd,jd->kj", wide[0], up_b, preferred_element_type=jnp.float32)
    partial_value = partial_value + jnp.einsum(
        "kd,jd->kj", wide[1], gate_b, preferred_element_type=jnp.float32
    )
    gate_rows = pick(gate_b, asked)
    gate_rows, partial_value = lax.optimization_barrier((gate_rows, partial_value))
    terms = cols_reduce(partial_value.reshape(cols, -1, row_count))

    cut = features * 3 // 4 // 128 * 128
    left_rows = pick(down_b[:, :cut], asked)
    right_rows = pick(down_b[:, cut:], asked)

    gate_moved = exchange(gate_rows)
    up_mean = mix(up_a, pick(up_moved, slot))
    tied = lax.optimization_barrier((left_rows, right_rows, up_mean) + tuple(terms[1::2]))
    left_rows, right_rows, up_mean = tied[:3]
    terms[1::2] = tied[3:]
    left = exchange(left_rows)
    gate_mean = mix(gate_a, pick(gate_moved, slot))
    total = terms[0]
    for term in terms[1:]:
        total = total + term
    costs_out = (total * cost_scale).T
    right_rows, gate_mean, costs_out = lax.optimization_barrier((right_rows, gate_mean, costs_out))
    right = exchange(right_rows)
    left_mean = mix(down_a[:, :cut], pick(left, slot))
    down_mean = lax.pad(left_mean, jnp.zeros((), left_mean.dtype), ((0, 0, 0), (0, features - cut, 0)))
    right, down_mean = lax.optimization_barrier((right, down_mean))
    right_mean = mix(down_a[:, cut:], pick(right, slot))
    down_mean = lax.dynamic_update_slice(down_mean, right_mean, (0, cut))
    return (costs_out, up_mean, gate_mean, down_mean)


def solution(mesh):
    placed = (P("rows", "cols"),) * 6 + (P("rows"),)
    return jax.shard_map(
        local,
        mesh=mesh,
        in_specs=placed,
        out_specs=(P("rows", "cols"),) * 4,
        check_vma=False,
    )
```

profile of v0, /device:TPU:0, one launch (start us, length us, event | category | flops | bytes accessed | tf_op | source)
XLA Modules:
  0.0 333.1 jit_solution(16120420972539285700)
XLA Ops:
  7.0 5.2 %all-to-all-start = ((s32[8,1,448]{2,1,0:T(1,128)}), s32[8,1,448]{2,1,0:T(1,128)S(1)}, u32[]{:S(2)}, u32[]{:S(2)}) async-start(s32[8,1,448]{2,1,0:T(1,128)} %copy.11), calls=%async_computation | async-start | bytes 32768 | tf_op jit(solution)/shard_map/all_to_all | solution.py:50
  19.8 4.2 %all-to-all-start.1 = ((bf16[8,64,1024]{2,1,0:T(8,128)(2,1)}), bf16[8,64,1024]{2,1,0:T(8,128)(2,1)S(1)}, u32[]{:S(2)}, u32[]{:S(2)}) async-start(bf16[8,64,1024]{2,1,0:T(8,128)(2,1)} %broadcast_in_dim.7), calls=%async_computation.1 | async-start | bytes 2097152 | tf_op jit(solution)/shard_map/all_to_all | solution.py:62
  24.0 20.4 %gather_fusion.2 = bf16[3584,1024]{1,0:T(8,128)(2,1)} fusion(bf16[3584,1024]{1,0:T(8,128)(2,1)} %param.10, s32[4096]{0:T(1024)S(1)} %pad_clamp_fusion.1), kind=kCustom, calls=%fused_computation.2 | custom fusion | bytes 14694400 | tf_op jit(solution)/shard_map/gather | solution.py:21
  44.4 4.9 %all-to-all-start.2 = ((bf16[8,448,1024]{2,1,0:T(8,128)(2,1)}), bf16[8,448,1024]{2,1,0:T(8,128)(2,1)}, u32[]{:S(2)}, u32[]{:S(2)}) async-start(bf16[8,448,1024]{2,1,0:T(8,128)(2,1)} %bitcast.55), calls=%async_computation.2 | async-start | bytes 14680064 | tf_op jit(solution)/shard_map/all_to_all | solution.py:54
  49.3 20.4 %gather_fusion.4 = bf16[3584,1024]{1,0:T(8,128)(2,1)} fusion(bf16[3584,1024]{1,0:T(8,128)(2,1)} %param.11, s32[4096]{0:T(1024)S(1)} %pad_clamp_fusion.1), kind=kCustom, calls=%fused_computation.4 | custom fusion | bytes 14694400 | tf_op jit(solution)/shard_map/gather | solution.py:21
  70.3 5.5 %fusion.9 = f32[256,3584]{1,0:T(8,128)S(1)} fusion(bf16[3584,1024]{1,0:T(8,128)(2,1)} %param.10, bf16[2,32,8,1024]{3,2,1,0:T(8,128)(2,1)S(1)} %bitcast.60), kind=kOutput, calls=%fused_computation.28 | convolution fusion | flops 1879048192 | bytes 11534336 | tf_op jit(solution)/shard_map/kd,jd->kj/dot_general | solution.py:69
  75.8 4.0 %convolution_add_fusion = f32[256,3584]{1,0:T(8,128)} fusion(f32[256,3584]{1,0:T(8,128)S(1)} %fusion.9, bf16[3584,1024]{1,0:T(8,128)(2,1)S(1)} %bitcast.52, bf16[2,32,8,1024]{3,2,1,0:T(8,128)(2,1)S(1)} %bitcast.61), kind=kOutput, calls=%fused_computation.14 | convolution fusion | flops 1879965696 | bytes 15204352 | tf_op jit(solution)/shard_map/kd,jd->kj/dot_general | solution.py:70
  79.8 52.4 %all-to-all-done.2 = bf16[8,448,1024]{2,1,0:T(8,128)(2,1)} async-done(((bf16[8,448,1024]{2,1,0:T(8,128)(2,1)}), bf16[8,448,1024]{2,1,0:T(8,128)(2,1)}, u32[]{:S(2)}, u32[]{:S(2)}) %all-to-all-start.2) | async-done | bytes 7340064 | tf_op jit(solution)/shard_map/all_to_all | solution.py:54
  132.1 5.0 %all-to-all-start.3 = ((bf16[8,448,1024]{2,1,0:T(8,128)(2,1)}), bf16[8,448,1024]{2,1,0:T(8,128)(2,1)}, u32[]{:S(2)}, u32[]{:S(2)}) async-start(bf16[8,448,1024]{2,1,0:T(8,128)(2,1)} %bitcast.54), calls=%async_computation.3 | async-start | bytes 14680064 | tf_op jit(solution)/shard_map/all_to_all | solution.py:54
  137.2 5.5 %slice.38 = bf16[3584,768]{1,0:T(8,128)(2,1)} slice(bf16[3584,1024]{1,0:T(8,128)(2,1)} %param.12), slice={[0:3584], [0:768]} | slice | bytes 11010048 | tf_op jit(solution)/shard_map/slice | solution.py:78
  142.7 10.9 %gather_fusion.1 = bf16[3584,256]{1,0:T(8,128)(2,1)} fusion(bf16[3584,256]{1,0:T(8,128)(2,1)S(1)} %slice-done.2, s32[4096]{0:T(1024)S(1)} %pad_clamp_fusion.1), kind=kCustom, calls=%fused_computation.1 | custom fusion | bytes 3684352 | tf_op jit(solution)/shard_map/gather | solution.py:21
  153.7 17.2 %gather_fusion = bf16[3584,768]{1,0:T(8,128)(2,1)} fusion(bf16[3584,768]{1,0:T(8,128)(2,1)} %slice.38, s32[4096]{0:T(1024)S(1)} %pad_clamp_fusion.1), kind=kCustom, calls=%fused_computation | custom fusion | bytes 11024384 | tf_op jit(solution)/shard_map/gather | solution.py:21
  177.6 20.4 %gather_fusion.3 = bf16[3584,1024]{1,0:T(8,128)(2,1)} fusion(bf16[3584,1024]{1,0:T(8,128)(2,1)} %bitcast.6, s32[4096]{0:T(1024)S(1)} %pad_clamp_fusion), kind=kCustom, calls=%fused_computation.3 | custom fusion | bytes 14694400 | tf_op jit(solution)/shard_map/gather | solution.py:21
  198.0 12.0 %multiply_convert_fusion.1 = bf16[3584,1024]{1,0:T(8,128)(2,1)} fusion(bf16[3584,1024]{1,0:T(8,128)(2,1)} %gather_fusion.3, bf16[3584,1024]{1,0:T(8,128)(2,1)} %param.7), kind=kLoop, calls=%fused_computation.9 | loop fusion | flops 18350080 | bytes 22020096 | tf_op jit(solution)/shard_map/convert_element_type | solution.py:25
  210.1 8.2 %collective-permute-done = f32[64,3584]{1,0:T(8,128)S(1)} collective-permute-done((f32[64,3584]{1,0:T(8,128)}, f32[64,3584]{1,0:T(8,128)S(1)}, u32[]{:S(2)}, u32[]{:S(2)}) %collective-permute-start) | collective-permute-done | bytes 917536 | tf_op jit(solution)/shard_map/ppermute | solution.py:16
  219.8 4.9 %all-to-all-start.5 = ((bf16[8,448,768]{2,1,0:T(8,128)(2,1)}), bf16[8,448,768]{2,1,0:T(8,128)(2,1)}, u32[]{:S(2)}, u32[]{:S(2)}) async-start(bf16[8,448,768]{2,1,0:T(8,128)(2,1)} %bitcast.56), calls=%async_computation.5 | async-start | bytes 11010048 | tf_op jit(solution)/shard_map/all_to_all | solution.py:54
  227.4 20.4 %gather_fusion.5 = bf16[3584,1024]{1,0:T(8,128)(2,1)} fusion(bf16[3584,1024]{1,0:T(8,128)(2,1)} %bitcast.16, s32[4096]{0:T(1024)S(1)} %pad_clamp_fusion), kind=kCustom, calls=%fused_computation.5 | custom fusion | bytes 14694400 | tf_op jit(solution)/shard_map/gather | solution.py:21
  247.8 20.0 %collective-permute-done.2 = f32[64,3584]{1,0:T(8,128)} collective-permute-done((f32[64,3584]{1,0:T(8,128)S(1)}, f32[64,3584]{1,0:T(8,128)}, u32[]{:S(2)}, u32[]{:S(2)}) %collective-permute-start.2) | collective-permute-done | bytes 917536 | tf_op jit(solution)/shard_map/ppermute | solution.py:16
  270.4 12.0 %multiply_convert_fusion = bf16[3584,1024]{1,0:T(8,128)(2,1)} fusion(bf16[3584,1024]{1,0:T(8,128)(2,1)} %gather_fusion.5, bf16[3584,1024]{1,0:T(8,128)(2,1)} %param.8), kind=kLoop, calls=%fused_computation.8 | loop fusion | flops 18350080 | bytes 22020096 | tf_op jit(solution)/shard_map/convert_element_type | solution.py:25
  282.4 5.3 %all-to-all-done.5 = bf16[8,448,768]{2,1,0:T(8,128)(2,1)} async-done(((bf16[8,448,768]{2,1,0:T(8,128)(2,1)}), bf16[8,448,768]{2,1,0:T(8,128)(2,1)}, u32[]{:S(2)}, u32[]{:S(2)}) %all-to-all-start.5) | async-done | bytes 5505056 | tf_op jit(solution)/shard_map/all_to_all | solution.py:54
  291.3 17.2 %gather_fusion.6 = bf16[3584,768]{1,0:T(8,128)(2,1)} fusion(bf16[3584,768]{1,0:T(8,128)(2,1)} %bitcast.23, s32[4096]{0:T(1024)S(1)} %pad_clamp_fusion), kind=kCustom, calls=%fused_computation.6 | custom fusion | bytes 11024384 | tf_op jit(solution)/shard_map/gather | solution.py:21
  308.5 5.9 %multiply_convert_fusion.2 = bf16[3584,768]{1,0:T(8,128)(2,1)S(1)} fusion(bf16[3584,768]{1,0:T(8,128)(2,1)} %gather_fusion.6, bf16[3584,1024]{1,0:T(8,128)(2,1)} %param.9), kind=kLoop, calls=%fused_computation.10 | loop fusion | flops 13762560 | bytes 16515072 | tf_op jit(solution)/shard_map/convert_element_type | solution.py:25
  314.3 4.1 %pad.3 = bf16[3584,1024]{1,0:T(8,128)(2,1)} pad(bf16[3584,768]{1,0:T(8,128)(2,1)S(1)} %multiply_convert_fusion.2, bf16[]{:T(256)} %constant.98.clone.1), padding=0_0x0_256 | pad | bytes 12845058 | tf_op jit(solution)/shard_map/pad | solution.py:95
  318.4 10.9 %gather_fusion.7 = bf16[3584,256]{1,0:T(8,128)(2,1)} fusion(bf16[3584,256]{1,0:T(8,128)(2,1)S(1)} %bitcast.53, s32[4096]{0:T(1024)S(1)} %pad_clamp_fusion), kind=kCustom, calls=%fused_computation.7 | custom fusion | bytes 3684352 | tf_op jit(solution)/shard_map/gather | solution.py:21
  (44 shorter events, 35.5 us)
Async XLA Ops:
  7.0 11.6 %all-to-all-start = ((s32[8,1,448]{2,1,0:T(1,128)}), s32[8,1,448]{2,1,0:T(1,128)S(1)}, u32[]{:S(2)}, u32[]{:S(2)}) async-start(s32[8,1,448]{2,1,0:T(1,128)} %copy.11), calls=%async_computation | async-start | bytes 32768 | tf_op jit(solution)/shard_map/all_to_all | solution.py:50
  19.8 24.6 %all-to-all-start.1 = ((bf16[8,64,1024]{2,1,0:T(8,128)(2,1)}), bf16[8,64,1024]{2,1,0:T(8,128)(2,1)S(1)}, u32[]{:S(2)}, u32[]{:S(2)}) async-start(bf16[8,64,1024]{2,1,0:T(8,128)(2,1)} %broadcast_in_dim.7), calls=%async_computation.1 | async-start | bytes 2097152 | tf_op jit(solution)/shard_map/all_to_all | solution.py:62
  44.4 87.7 %all-to-all-start.2 = ((bf16[8,448,1024]{2,1,0:T(8,128)(2,1)}), bf16[8,448,1024]{2,1,0:T(8,128)(2,1)}, u32[]{:S(2)}, u32[]{:S(2)}) async-start(bf16[8,448,1024]{2,1,0:T(8,128)(2,1)} %bitcast.55), calls=%async_computation.2 | async-start | bytes 14680064 | tf_op jit(solution)/shard_map/all_to_all | solution.py:54
  69.7 6.1 %slice-start = ((s8[7340032]{0:T(1024)(128)(4,1)}), s8[4194304]{0:T(1024)(128)(4,1)S(1)}, s32[]{:S(2)}) async-start(s8[7340032]{0:T(1024)(128)(4,1)} %bitcast.51), calls=%async_computation.6 | async-start | bytes 8388608
  70.3 5.5 %slice-start.1 = ((s8[7340032]{0:T(1024)(128)(4,1)}), s8[3145728]{0:T(1024)(128)(4,1)S(1)}, s32[]{:S(2)}) async-start(s8[7340032]{0:T(1024)(128)(4,1)} %bitcast.51), calls=%async_computation.7 | async-start | bytes 6291456
  132.1 87.7 %all-to-all-start.3 = ((bf16[8,448,1024]{2,1,0:T(8,128)(2,1)}), bf16[8,448,1024]{2,1,0:T(8,128)(2,1)}, u32[]{:S(2)}, u32[]{:S(2)}) async-start(bf16[8,448,1024]{2,1,0:T(8,128)(2,1)} %bitcast.54), calls=%async_computation.3 | async-start | bytes 14680064 | tf_op jit(solution)/shard_map/all_to_all | solution.py:54
  137.2 5.5 %slice-start.2 = ((bf16[3584,1024]{1,0:T(8,128)(2,1)}), bf16[3584,256]{1,0:T(8,128)(2,1)S(1)}, s32[]{:S(2)}) async-start(bf16[3584,1024]{1,0:T(8,128)(2,1)} %param.12), calls=%async_computation.8 | async-start | bytes 3670016 | tf_op jit(solution)/shard_map/slice | solution.py:79
  174.0 36.1 %collective-permute-start.1 = (f32[64,3584]{1,0:T(8,128)}, f32[64,3584]{1,0:T(8,128)S(1)}, u32[]{:S(2)}, u32[]{:S(2)}) collective-permute-start(f32[64,3584]{1,0:T(8,128)} %get-tuple-element.43), channel_id=1, source_target_pairs={{0,3},{1,0},{2,1},{3,2},{4,7},{5,4},{6,5},{7,6},{8,11},{9,8},{10,9... | collective-permute-start | bytes 2752520 | tf_op jit(solution)/shard_map/ppermute | solution.py:16
  177.6 40.7 %collective-permute-start = (f32[64,3584]{1,0:T(8,128)}, f32[64,3584]{1,0:T(8,128)S(1)}, u32[]{:S(2)}, u32[]{:S(2)}) collective-permute-start(f32[64,3584]{1,0:T(8,128)} %get-tuple-element.44), channel_id=1, source_target_pairs={{0,1},{1,2},{2,3},{3,0},{4,5},{5,6},{6,7},{7,4},{8,9},{9,10},{10,1... | collective-permute-start | bytes 2752520 | tf_op jit(solution)/shard_map/ppermute | solution.py:16
  219.8 67.9 %all-to-all-start.5 = ((bf16[8,448,768]{2,1,0:T(8,128)(2,1)}), bf16[8,448,768]{2,1,0:T(8,128)(2,1)}, u32[]{:S(2)}, u32[]{:S(2)}) async-start(bf16[8,448,768]{2,1,0:T(8,128)(2,1)} %bitcast.56), calls=%async_computation.5 | async-start | bytes 11010048 | tf_op jit(solution)/shard_map/all_to_all | solution.py:54
  224.7 43.1 %collective-permute-start.2 = (f32[64,3584]{1,0:T(8,128)S(1)}, f32[64,3584]{1,0:T(8,128)}, u32[]{:S(2)}, u32[]{:S(2)}) collective-permute-start(f32[64,3584]{1,0:T(8,128)S(1)} %get-tuple-element.42), channel_id=1, source_target_pairs={{0,2},{1,3},{2,0},{3,1},{4,6},{5,7},{6,4},{7,5},{8,10},{9,11},{10,... | collective-permute-start | bytes 2752520 | tf_op jit(solution)/shard_map/ppermute | solution.py:16
  287.7 30.7 %all-to-all-start.4 = ((bf16[8,448,256]{2,1,0:T(8,128)(2,1)}), bf16[8,448,256]{2,1,0:T(8,128)(2,1)S(1)}, u32[]{:S(2)}, u32[]{:S(2)}) async-start(bf16[8,448,256]{2,1,0:T(8,128)(2,1)} %bitcast.59), calls=%async_computation.4 | async-start | bytes 3670016 | tf_op jit(solution)/shard_map/all_to_all | solution.py:54
where the time goes:
time: 334 us; the launch traced here: 333 us
  local copies, waits for them, and re-layouts  160 us (48%)
  waiting for transfers between devices  87.4 us (26%)
  other arithmetic  40.6 us (12%)
  starting transfers between devices  34 us (10%)
  matrix products  10.6 us (3%)
    gather x8, local copies, waits for them, and re-layouts, pick(): return array.at[index].get(mode='promise_in_bounds')  138 us
    all_to_all x4, waiting for transfers between devices, exchange(): lax.all_to_all(moved, 'rows', split_axis=0, concat_axis=0, tiled=True)  59.1 us
    convert_element_type x3, other arithmetic, mix(): ((initial.astype(jnp.float32) + picked.astype(jnp.float32)) * 0.5).astype...  29.9 us
    ppermute x3, waiting for transfers between devices, cols_reduce(): lax.ppermute(piece, 'cols', [(c, (c + shift) % count) for c in range(coun...  28.3 us
    all_to_all x4, starting transfers between devices, exchange(): lax.all_to_all(moved, 'rows', split_axis=0, concat_axis=0, tiled=True)  18.4 us
  transfers between devices with their start and end apart: 9, of which 5 were waited for; matrix products, arithmetic and copies ran while one was open for 57% of the time, Pallas kernels for 0%

commit v1 on v0

v1 whole, which is shorter than its diff:
```python
import functools

import jax
import jax.numpy as jnp
from jax import lax
from jax.experimental import pallas as pl
from jax.experimental.pallas import tpu as pltpu
from jax.sharding import PartitionSpec as P

D = 4096
A_DEV = 32
MESH = pl.DeviceIdType.MESH

PEERS = 8
LANES = 128
TILE = 256
SLOT = 64
CODE = 1024


def one_hot(hit):
    return jnp.where(hit, 1.0, 0.0).astype(jnp.bfloat16)


def matmul(a, b):
    return jnp.dot(a, b, preferred_element_type=jnp.float32)


def ask_kernel(count, perm_ref, asked_ref, code_ref, before_ref, hot, halves, counts, sent, got, send_sems, recv_sems, own_sem):
    me = lax.axis_index("rows")
    barrier = pltpu.get_barrier_semaphore()
    for k in range(1, PEERS):
        pl.semaphore_signal(barrier, inc=1, device_id={"rows": me ^ k}, device_id_type=MESH)

    pad = perm_ref.shape[0]
    used = count // LANES
    slots = count // PEERS
    perm = perm_ref[...]
    source = jnp.zeros_like(perm)
    for k in range(1, PEERS + 1):
        source = source + jnp.where(perm >= k * count, 1, 0)
    row = perm - source * count
    masks = jnp.concatenate([jnp.where(source == k, 1.0, 0.0) for k in range(PEERS)], axis=0)
    packed = masks.astype(jnp.bfloat16)
    shape = (LANES, LANES)
    lane_before = one_hot(lax.broadcasted_iota(jnp.int32, shape, 0) < lax.broadcasted_iota(jnp.int32, shape, 1))
    within = matmul(packed, lane_before)
    totals = matmul(packed, jnp.ones(shape, jnp.bfloat16)).astype(jnp.bfloat16)
    shape = (PEERS * pad, PEERS * pad)
    left, right = lax.broadcasted_iota(jnp.int32, shape, 0), lax.broadcasted_iota(jnp.int32, shape, 1)
    row_before = one_hot((right < left) & (right >= left - lax.rem(left, pad)))
    ahead = matmul(row_before, totals)
    counts[...] = ahead.astype(jnp.int32)
    ranked = masks * (within + ahead)
    rank = ranked[:pad]
    for k in range(1, PEERS):
        rank = rank + ranked[k * pad : (k + 1) * pad]
    rank = rank.astype(jnp.int32)
    code_ref[...] = (source ^ me) * CODE + rank
    for k in range(PEERS):
        before_ref[k] = counts[pl.ds(pl.multiple_of((me ^ k) * pad, pad), pad), :]

    high = lax.shift_right_logical(row, 8).astype(jnp.float32)
    low = (row & 255).astype(jnp.float32)
    block = lax.broadcasted_iota(jnp.int32, (PEERS, LANES), 0)
    slot = lax.broadcasted_iota(jnp.int32, (slots, LANES), 0)
    for j in range(used):
        at = slice(j * LANES, (j + 1) * LANES)
        one = slice(j, j + 1)
        mine = source[one] == block
        both = [jnp.where(mine, part[one], 0.0) for part in (high, low)]
        halves[:, at] = jnp.concatenate(both, axis=0).astype(jnp.bfloat16)
        hot[:, at] = one_hot(rank[one] == slot)
    found = lax.dot_general(halves[...], hot[...], (((1,), (1,)), ((), ())), preferred_element_type=jnp.float32)
    wanted = found[:PEERS] * 256.0 + found[PEERS:]
    for k in range(PEERS):
        sent[k, :, :slots] = jnp.broadcast_to(wanted[k : k + 1], (8, slots))
        sent[k, :, slots:] = jnp.zeros((8, sent.shape[2] - slots), jnp.float32)

    pl.semaphore_wait(barrier, PEERS - 1)
    copies = []
    for k in range(1, PEERS):
        peer = me ^ k
        copy = pltpu.make_async_remote_copy(
            src_ref=sent.at[peer],
            dst_ref=got.at[k],
            send_sem=send_sems.at[k],
            recv_sem=recv_sems.at[k],
            device_id={"rows": peer},
            device_id_type=MESH,
        )
        copy.start()
        copies.append(copy)
    own = pltpu.make_async_copy(sent.at[me], got.at[0], own_sem)
    own.start()
    own.wait()
    for copy in copies:
        copy.wait()
    table = jnp.concatenate([got[k, 0:1, :] for k in range(PEERS)], axis=0)
    table = jnp.concatenate([table] * (LANES // PEERS), axis=0)
    asked_ref[...] = table.T.astype(jnp.int32)


def ask(perm):
    count = perm.shape[0]
    used = count // LANES
    pad = -(-used // 8) * 8
    slots = count // PEERS
    wide = -(-slots // LANES) * LANES
    grid = jnp.pad(perm.reshape(used, LANES), ((0, pad - used), (0, 0)), constant_values=PEERS * count)
    vmem = pl.BlockSpec(memory_space=pltpu.VMEM)
    return pl.pallas_call(
        functools.partial(ask_kernel, count),
        out_shape=(
            jax.ShapeDtypeStruct((wide, LANES), jnp.int32),
            jax.ShapeDtypeStruct((pad, LANES), jnp.int32),
            jax.ShapeDtypeStruct((PEERS, pad, LANES), jnp.int32),
        ),
        in_specs=[vmem],
        out_specs=(vmem,) * 3,
        scratch_shapes=[
            pltpu.VMEM((slots, count), jnp.bfloat16),
            pltpu.VMEM((2 * PEERS, count), jnp.bfloat16),
            pltpu.VMEM((PEERS * pad, LANES), jnp.int32),
            pltpu.VMEM((PEERS, 8, wide), jnp.float32),
            pltpu.VMEM((PEERS, 8, wide), jnp.float32),
            pltpu.SemaphoreType.DMA((PEERS,)),
            pltpu.SemaphoreType.DMA((PEERS,)),
            pltpu.SemaphoreType.DMA,
        ],
        compiler_params=pltpu.CompilerParams(
            collective_id=0, has_side_effects=True, vmem_limit_bytes=32 * 1024 * 1024
        ),
    )(grid)


def window_kernel(stride, up_ref, gate_ref, out_ref, held, sems):
    copies = []
    for m, ref in enumerate((up_ref, gate_ref)):
        for i in range(A_DEV):
            at = m * A_DEV + i
            copy = pltpu.make_async_copy(ref.at[pl.ds(i * stride, 16)], held.at[pl.ds(at * 16, 16)], sems.at[at])
            copy.start()
            copies.append(copy)
    for copy in copies:
        copy.wait()
    shape = (2 * A_DEV, 32 * A_DEV)
    first = lax.broadcasted_iota(jnp.int32, shape, 0) * 16 == lax.broadcasted_iota(jnp.int32, shape, 1)
    out_ref[...] = matmul(one_hot(first), held[...]).astype(jnp.bfloat16)


def window_units(up_a, gate_a):
    features = up_a.shape[1]
    whole = pl.BlockSpec(memory_space=pl.ANY)
    return pl.pallas_call(
        functools.partial(window_kernel, up_a.shape[0] // A_DEV),
        out_shape=jax.ShapeDtypeStruct((2 * A_DEV, features), jnp.bfloat16),
        in_specs=[whole, whole],
        out_specs=pl.BlockSpec(memory_space=pltpu.VMEM),
        scratch_shapes=[
            pltpu.VMEM((32 * A_DEV, features), jnp.bfloat16),
            pltpu.SemaphoreType.DMA((2 * A_DEV,)),
        ],
    )(up_a, gate_a)


def collect_kernel(shifts, asked_ref, rows_ref, *refs):
    outs, total = refs[: len(shifts)], refs[-1]
    step = pl.program_id(1)
    depth = rows_ref.shape[0]
    slots = outs[0].shape[0]
    row = lax.broadcasted_iota(jnp.int32, (slots, depth), 1) + step * depth
    hot = jnp.concatenate([one_hot(asked_ref[:slots, k : k + 1] == row) for k in shifts], axis=0)
    part = matmul(hot, rows_ref[...])

    @pl.when(step == 0)
    def _():
        total[...] = part

    @pl.when(step > 0)
    def _():
        total[...] += part

    @pl.when(step == pl.num_programs(1) - 1)
    def _():
        for at, out in enumerate(outs):
            out[...] = total[at * slots : (at + 1) * slots].astype(out.dtype)


def collect(asked, rows, shifts, start, size):
    count = rows.shape[0]
    slots = count // PEERS
    depth = 512 if count % 512 == 0 else slots
    n = len(shifts)
    return pl.pallas_call(
        functools.partial(collect_kernel, shifts),
        out_shape=[jax.ShapeDtypeStruct((slots, size), rows.dtype)] * n,
        grid=(1, count // depth),
        in_specs=[
            pl.BlockSpec(asked.shape, lambda c, s: (0, 0)),
            pl.BlockSpec((depth, size), lambda c, s: (s, start // size)),
        ],
        out_specs=[pl.BlockSpec((slots, size), lambda c, s: (0, 0))] * n,
        scratch_shapes=[pltpu.VMEM((n * slots, size), jnp.float32)],
        compiler_params=pltpu.CompilerParams(vmem_limit_bytes=60 * 1024 * 1024),
        cost_estimate=pl.CostEstimate(
            flops=2 * n * slots * count * size, bytes_accessed=2 * (count + n * slots) * size, transcendentals=0
        ),
    )(asked, rows)


def place_kernel(before_ref, code_ref, initial_ref, *refs):
    *rest, out_ref, held, total = refs
    arrived = rest[-PEERS:]
    t = pl.program_id(0)
    pad = before_ref.shape[0] // PEERS
    last = arrived[0].shape[0] - SLOT
    per = TILE // LANES
    starts, rounds = [], jnp.int32(1)
    for k in range(PEERS):
        lo = before_ref[k * pad + t * per]
        hi = before_ref[k * pad + t * per + per]
        start = lax.shift_left(lax.shift_right_logical(lo, 4), 4)
        starts.append(start)
        rounds = jnp.maximum(rounds, lax.shift_right_logical(hi - start + SLOT - 1, 6))
    lane = lax.broadcasted_iota(jnp.int32, (1, PEERS * SLOT), 1)
    peer = lax.shift_right_logical(lane, 6)
    code = code_ref[...]
    code = code[:, :1]

    def gathered(j):
        first = jnp.zeros_like(lane)
        at = jnp.zeros_like(lane)
        for k in range(PEERS):
            begin = starts[k] + j * SLOT
            from_row = jnp.minimum(begin, last)
            held[k * SLOT : (k + 1) * SLOT, :] = arrived[k][pl.ds(pl.multiple_of(from_row, 16), SLOT), :]
            first = jnp.where(peer == k, begin, first)
            at = jnp.where(peer == k, from_row, at)
        at = at + (lane & (SLOT - 1))
        codes = jnp.where(at >= first, peer * CODE + at, -1)
        return matmul(one_hot(code == codes), held[...])

    total[...] = gathered(jnp.int32(0))

    def more(j, carry):
        total[...] += gathered(j)
        return carry

    lax.fori_loop(1, rounds, more, 0)
    out_ref[...] = ((initial_ref[...].astype(jnp.float32) + total[...]) * 0.5).astype(out_ref.dtype)


def place(before, code, initial, arrived, start, out=None):
    count, features = initial.shape
    slots, size = arrived[0].shape
    wide = lambda t, *_: (t, start // size)
    extra = [] if out is None else [out]
    return pl.pallas_call(
        place_kernel,
        out_shape=jax.ShapeDtypeStruct((count, features), initial.dtype),
        grid_spec=pltpu.PrefetchScalarGridSpec(
            num_scalar_prefetch=1,
            grid=(count // TILE,),
            in_specs=[
                pl.BlockSpec((TILE, LANES), lambda t, *_: (t, 0)),
                pl.BlockSpec((TILE, size), wide),
            ]
            + [pl.BlockSpec(memory_space=pl.ANY)] * len(extra)
            + [pl.BlockSpec((slots, size), lambda t, *_: (0, 0))] * PEERS,
            out_specs=pl.BlockSpec((TILE, size), wide),
            scratch_shapes=[
                pltpu.VMEM((PEERS * SLOT, size), jnp.bfloat16),
                pltpu.VMEM((TILE, size), jnp.float32),
            ],
        ),
        input_output_aliases={3: 0} if extra else {},
        compiler_params=pltpu.CompilerParams(vmem_limit_bytes=60 * 1024 * 1024),
        cost_estimate=pl.CostEstimate(
            flops=2 * count * PEERS * SLOT * size, bytes_accessed=6 * count * size, transcendentals=0
        ),
    )(before, code, initial, *extra, *arrived)


def balanced(up_a, gate_a, down_a, up_b, gate_b, down_b, perm):
    row_count, features = up_a.shape
    cols = lax.axis_size("cols")
    cost_scale = (2.0 * D) ** (-0.5)

    window = window_units(up_a, gate_a)
    perm, window = lax.optimization_barrier((perm, window))
    pieces = lax.all_gather(window, "rows")
    asked, code, before = ask(perm)
    before = before[:, :, 0].reshape(-1)
    code = jnp.broadcast_to(code.reshape(-1)[:row_count, None], (row_count, LANES))

    def after(value, *others):
        return lax.optimization_barrier((value,) + others)[0]

    def send(rows, start, size, group, *others):
        parts = collect(after(asked, *others), rows, group, start, size)
        return parts, {
            k: part if k == 0 else lax.ppermute(part, "rows", [(i, i ^ k) for i in range(PEERS)])
            for k, part in zip(group, parts)
        }

    def placed(initial, arrived, start, out, *others):
        return place(before, after(code, *others), initial, [arrived[k] for k in range(PEERS)], start, out)

    near, far, every = (6, 2, 4), (7, 3, 5, 1, 0), (6, 2, 4, 7, 3, 5, 1, 0)
    half, quarter = features // 2, features // 4
    parts, up_first = send(up_b, 0, features, near[:1])
    parts, up_second = send(up_b, 0, features, near[1:], *parts)
    up_first = {**up_first, **up_second}
    parts, up_last = send(up_b, 0, features, far, *parts)

    pieces = after(pieces, *parts)
    wide = pieces.reshape(PEERS, 2, A_DEV, features).transpose(1, 2, 0, 3).reshape(2, A_DEV * PEERS, features)
    partial_value = jnp.einsum("kd,jd->kj", wide[0], up_b, preferred_element_type=jnp.float32)
    partial_value = partial_value + jnp.einsum("kd,jd->kj", wide[1], gate_b, preferred_element_type=jnp.float32)
    total = lax.psum_scatter(partial_value.reshape(cols, -1, row_count), "cols", scatter_dimension=0)

    parts, gate_first = send(gate_b, 0, features, near, partial_value, *up_first.values())
    parts, gate_last = send(gate_b, 0, features, far, *parts, *up_last.values())
    up_mean = placed(up_a, {**up_first, **up_last}, 0, None, *parts)
    parts, down_first = send(down_b, 0, half, near, up_mean, *gate_first.values())
    parts, down_second = send(down_b, 0, half, far, *parts, *gate_last.values())
    gate_mean = placed(gate_a, {**gate_first, **gate_last}, 0, None, *parts)
    parts, down_third = send(down_b, half, quarter, every, gate_mean, *down_first.values())
    parts, down_fourth = send(down_b, half + quarter, quarter, every, *parts, *down_second.values())
    down_mean = placed(down_a, {**down_first, **down_second}, 0, None, *parts)
    down_mean = placed(down_a, down_third, half, down_mean)
    costs = (after(total, down_mean) * cost_scale).T
    down_mean = placed(down_a, down_fourth, half + quarter, down_mean, costs)
    return (costs, up_mean, gate_mean, down_mean)


def pick(array, index):
    rows = jnp.arange(array.shape[0], dtype=jnp.int32)
    hot = (index[:, None] == rows[None, :]).astype(array.dtype)
    return jnp.dot(hot, array, preferred_element_type=jnp.float32).astype(array.dtype)


def mix(initial, picked):
    return ((initial.astype(jnp.float32) + picked.astype(jnp.float32)) * 0.5).astype(jnp.bfloat16)


def general(up_a, gate_a, down_a, up_b, gate_b, down_b, perm):
    row_count, features = up_a.shape
    stride = row_count // A_DEV
    cost_scale = (2.0 * D) ** (-0.5)
    peers = lax.axis_size("rows")
    cols = lax.axis_size("cols")
    capacity = max(2, (row_count + peers - 1) // peers)

    source = perm // row_count
    local_row = perm % row_count
    blocks = jnp.arange(peers, dtype=jnp.int32)
    matches = (source[None, :] == blocks[:, None]).astype(jnp.int32)
    order = jnp.arange(row_count, dtype=jnp.int32)
    ahead = jnp.dot(
        matches.astype(jnp.bfloat16),
        (order[:, None] < order[None, :]).astype(jnp.bfloat16),
        preferred_element_type=jnp.float32,
    )
    arrival_rank = jnp.sum(ahead.astype(jnp.int32) * matches, axis=0)
    high = (local_row // 256).astype(jnp.bfloat16)
    low = (local_row % 256).astype(jnp.bfloat16)
    halves = jnp.stack([high, low])[:, None, :] * matches.astype(jnp.bfloat16)[None]
    at_rank = (arrival_rank[None, :] == jnp.arange(capacity, dtype=jnp.int32)[:, None]).astype(jnp.bfloat16)
    found = jnp.einsum("hsi,ri->hsr", halves, at_rank, preferred_element_type=jnp.float32)
    wanted = found[0].astype(jnp.int32) * 256 + found[1].astype(jnp.int32)
    asked = lax.all_to_all(wanted, "rows", split_axis=0, concat_axis=0, tiled=True).reshape(-1)
    slot = source * capacity + arrival_rank

    window = jnp.concatenate([up_a[::stride], gate_a[::stride]], axis=0)
    pieces = lax.all_gather(window, "rows").reshape(peers, 2, A_DEV, features)
    wide = pieces.transpose(1, 2, 0, 3).reshape(2, A_DEV * peers, features)
    partial_value = jnp.einsum("kd,jd->kj", wide[0], up_b, preferred_element_type=jnp.float32)
    partial_value = partial_value + jnp.einsum("kd,jd->kj", wide[1], gate_b, preferred_element_type=jnp.float32)
    total = lax.psum_scatter(partial_value.reshape(cols, -1, row_count), "cols", scatter_dimension=0)

    def averaged(initial, other):
        moved = pick(other, asked).reshape(peers, capacity, features)
        moved = lax.all_to_all(moved, "rows", split_axis=0, concat_axis=0, tiled=True)
        return mix(initial, pick(moved.reshape(-1, features), slot))

    return (
        (total * cost_scale).T,
        averaged(up_a, up_b),
        averaged(gate_a, gate_b),
        averaged(down_a, down_b),
    )


def solution(mesh):
    def local(up_a, *rest):
        row_count, features = up_a.shape
        even = mesh.shape["rows"] == PEERS and row_count % (PEERS * 16) == 0 and row_count % (A_DEV * 16) == 0
        even = even and row_count % TILE == 0 and SLOT <= row_count // PEERS < CODE and features % 512 == 0
        return (balanced if even else general)(up_a, *rest)

    placed = (P("rows", "cols"),) * 6 + (P("rows"),)
    return jax.shard_map(
        local,
        mesh=mesh,
        in_specs=placed,
        out_specs=(P("rows", "cols"),) * 4,
        check_vma=False,
    )
```

time: 334 us -> 384 us (1.15)
  Pallas kernels: 0 us -> 236 us
  local copies, waits for them, and re-layouts: 160 us -> 7.44 us
  other arithmetic: 40.6 us -> 2.18 us
  between operations: 0.89 us -> 14.5 us
  waiting for transfers between devices: 87.4 us -> 81 us
    pallas_call x0 -> x16, Pallas kernels: none -> 236 us  [the longest x9 151 us: collect(): pl.pallas_call(functools.partial(collect_kernel, shifts), out_shape=[jax....]
    gather x8 -> x0, local copies, waits for them, and re-layouts: 138 us -> none  [pick(): return array.at[index].get(mode='promise_in_bounds')]
    all_to_all x6 -> x0, waiting for transfers between devices: 59.1 us -> none  [the longest x4 59.1 us: exchange(): lax.all_to_all(moved, 'rows', split_axis=0, concat_axis=0, tiled=True)]
    ppermute x3 -> x35, waiting for transfers between devices: 28.3 us -> 80.9 us  [send(): lax.ppermute(part, 'rows', [(i, i ^ k) for i in range(PEERS)])]
    convert_element_type x5 -> x0, other arithmetic: 30 us -> none  [the longest x3 29.9 us: mix(): ((initial.astype(jnp.float32) + picked.astype(jnp.float32)) * 0.5).astype...]
    all_to_all x6 -> x0, starting transfers between devices: 27.8 us -> none  [the longest x4 18.4 us: exchange(): lax.all_to_all(moved, 'rows', split_axis=0, concat_axis=0, tiled=True)]
    ppermute x3 -> x35, starting transfers between devices: 6.26 us -> 31.7 us  [send(): lax.ppermute(part, 'rows', [(i, i ^ k) for i in range(PEERS)])]
    slice x6 -> x1, local copies, waits for them, and re-layouts: 12.2 us -> 0.21 us  [balanced(): before = before[:, :, 0].reshape(-1)]
  transfers between devices with their start and end apart: 9 -> 37, of which waited for: 5 -> 11; matrix products, arithmetic and copies ran while one was open for 57% -> 1% of each run, Pallas kernels for 0% -> 58%
where the time goes in v1:
time: 384 us; the launch traced here: 382 us
  Pallas kernels  236 us (61%)
  waiting for transfers between devices  81 us (21%)
  starting transfers between devices  31.8 us (8%)
  between operations  14.5 us (4%)
  matrix products  9.24 us (2%)
  local copies, waits for them, and re-layouts  7.44 us (2%)
    pallas_call x9, Pallas kernels, collect(): pl.pallas_call(functools.partial(collect_kernel, shifts), out_shape=[jax....  151 us
    ppermute x35, waiting for transfers between devices, send(): lax.ppermute(part, 'rows', [(i, i ^ k) for i in range(PEERS)])  80.9 us
    pallas_call x5, Pallas kernels, place(): pl.pallas_call(place_kernel, out_shape=jax.ShapeDtypeStruct((count, featu...  73.7 us
    ppermute x35, starting transfers between devices, send(): lax.ppermute(part, 'rows', [(i, i ^ k) for i in range(PEERS)])  31.7 us
    pallas_call x1, Pallas kernels, ask(): pl.pallas_call(functools.partial(ask_kernel, count), out_shape=(jax.Shape...  7.86 us
  transfers between devices with their start and end apart: 37, of which 11 were waited for; matrix products, arithmetic and copies ran while one was open for 1% of the time, Pallas kernels for 58%

profile of v1, /device:TPU:0, one launch (start us, length us, event | category | flops | bytes accessed | tf_op | source)
XLA Modules:
  0.0 382.2 jit_solution(12503770555148015547)
XLA Ops:
  10.5 7.9 %shard_map.103 = (s32[512,128]{1,0:T(8,128)S(1)}, s32[32,128]{1,0:T(8,128)S(1)}, s32[8,32,128]{2,1,0:T(8,128)S(1)}) custom-call(s32[32,128]{1,0:T(8,128)S(1)} %pad.4.perm_ref), custom_call_target="tpu_custom_call" | custom-call | tf_op jit(solution)/shard_map/pallas_call | solution.py:112
  19.1 9.6 %shard_map.104 = bf16[448,1024]{1,0:T(8,128)(2,1)} custom-call(s32[512,128]{1,0:T(8,128)} %copy-done, bf16[3584,1024]{1,0:T(8,128)(2,1)} %rows_ref.11), custom_call_target="tpu_custom_call" | custom-call | flops 3288334336 | bytes 8257536 | tf_op jit(solution)/shard_map/pallas_call | solution.py:195
  28.7 13.4 %shard_map.105 = (bf16[448,1024]{1,0:T(8,128)(2,1)}, bf16[448,1024]{1,0:T(8,128)(2,1)}) custom-call(s32[512,128]{1,0:T(8,128)} %copy-done, bf16[3584,1024]{1,0:T(8,128)(2,1)} %rows_ref.11), custom_call_target="tpu_custom_call" | custom-call | flops 6576668672 | bytes 9175040 | tf_op jit(solution)/shard_map/pallas_call | solution.py:195
  42.0 28.3 %shard_map.106 = (bf16[448,1024]{1,0:T(8,128)(2,1)}, bf16[448,1024]{1,0:T(8,128)(2,1)}, bf16[448,1024]{1,0:T(8,128)(2,1)}, bf16[448,1024]{1,0:T(8,128)(2,1)}, bf16[448,1024]{1,0:T(8,128)(2,1)}) custom-call(s32[512,128]{1,0:T(8,128)} %copy-done, bf16[3584,1024]{1,0:T(8,128)(2,1)} %rows_ref.11), custom_call_target="tpu_custom_call" | custom-call | flops 16441671680 | bytes 11927552 | tf_op jit(solution)/shard_map/pallas_call | solution.py:195
  72.3 5.3 %fusion = f32[256,3584]{1,0:T(8,128)S(1)} fusion(bf16[3584,1024]{1,0:T(8,128)(2,1)} %rows_ref.11, bf16[2,32,8,1024]{3,2,1,0:T(8,128)(2,1)S(1)} %bitcast.22), kind=kOutput, calls=%fused_computation.4 | convolution fusion | flops 1879048192 | bytes 11534336 | tf_op jit(solution)/shard_map/kd,jd->kj/dot_general | solution.py:319
  77.6 3.9 %convolution_add_fusion = f32[256,3584]{1,0:T(8,128)} fusion(f32[256,3584]{1,0:T(8,128)S(1)} %fusion, bf16[3584,1024]{1,0:T(8,128)(2,1)S(1)} %bitcast.21, bf16[2,32,8,1024]{3,2,1,0:T(8,128)(2,1)S(1)} %bitcast.23), kind=kOutput, calls=%fused_computation | convolution fusion | flops 1879965696 | bytes 15204352 | tf_op jit(solution)/shard_map/kd,jd->kj/dot_general | solution.py:320
  87.0 19.0 %collective-permute-done.refs_6_ = bf16[448,1024]{1,0:T(8,128)(2,1)S(1)} collective-permute-done((bf16[448,1024]{1,0:T(8,128)(2,1)}, bf16[448,1024]{1,0:T(8,128)(2,1)S(1)}, u32[]{:S(2)}, u32[]{:S(2)}) %collective-permute-start) | collective-permute-done | bytes 917536 | tf_op jit(solution)/shard_map/ppermute | solution.py:303
  106.0 18.8 %collective-permute-done.1.refs_2_ = bf16[448,1024]{1,0:T(8,128)(2,1)S(1)} collective-permute-done((bf16[448,1024]{1,0:T(8,128)(2,1)}, bf16[448,1024]{1,0:T(8,128)(2,1)S(1)}, u32[]{:S(2)}, u32[]{:S(2)}) %collective-permute-start.1) | collective-permute-done | bytes 917536 | tf_op jit(solution)/shard_map/ppermute | solution.py:303
  125.8 18.4 %shard_map.107 = (bf16[448,1024]{1,0:T(8,128)(2,1)}, bf16[448,1024]{1,0:T(8,128)(2,1)}, bf16[448,1024]{1,0:T(8,128)(2,1)}) custom-call(s32[512,128]{1,0:T(8,128)} %copy-done, bf16[3584,1024]{1,0:T(8,128)(2,1)} %rows_ref.13), custom_call_target="tpu_custom_call" | custom-call | flops 9865003008 | bytes 10092544 | tf_op jit(solution)/shard_map/pallas_call | solution.py:195
  146.5 16.7 %collective-permute-done.4.refs_3_ = bf16[448,1024]{1,0:T(8,128)(2,1)} collective-permute-done((bf16[448,1024]{1,0:T(8,128)(2,1)S(1)}, bf16[448,1024]{1,0:T(8,128)(2,1)}, u32[]{:S(2)}, u32[]{:S(2)}) %collective-permute-start.4) | collective-permute-done | bytes 917536 | tf_op jit(solution)/shard_map/ppermute | solution.py:303
  164.8 28.3 %shard_map.108 = (bf16[448,1024]{1,0:T(8,128)(2,1)}, bf16[448,1024]{1,0:T(8,128)(2,1)}, bf16[448,1024]{1,0:T(8,128)(2,1)}, bf16[448,1024]{1,0:T(8,128)(2,1)}, bf16[448,1024]{1,0:T(8,128)(2,1)}) custom-call(s32[512,128]{1,0:T(8,128)} %copy-done, bf16[3584,1024]{1,0:T(8,128)(2,1)} %rows_ref.13), custom_call_target="tpu_custom_call" | custom-call | flops 16441671680 | bytes 11927552 | tf_op jit(solution)/shard_map/pallas_call | solution.py:195
  196.4 7.2 %collective-permute-done.8.refs_2_ = bf16[448,1024]{1,0:T(8,128)(2,1)S(1)} collective-permute-done((bf16[448,1024]{1,0:T(8,128)(2,1)}, bf16[448,1024]{1,0:T(8,128)(2,1)S(1)}, u32[]{:S(2)}, u32[]{:S(2)}) %collective-permute-start.8) | collective-permute-done | bytes 917536 | tf_op jit(solution)/shard_map/ppermute | solution.py:303
  206.9 17.7 %shard_map.109 = bf16[3584,1024]{1,0:T(8,128)(2,1)} custom-call(s32[256]{0:T(256)} %reshape_squeeze.3.before_ref, s32[3584,128]{1,0:T(8,128)} %broadcast_in_dim.9.code_ref, bf16[3584,1024]{1,0:T(8,128)(2,1)} %initial_ref.5, bf16[448,1024]{1,0:T(8,128)(2,1)} %get-tuple-element.73.refs_0_, bf16[448,1024]{1,0:T(8,128)(2,1)} %collective-permute-done.6.refs_1_, ...), custom_call_target="tpu_custom_call" | custom-call | flops 3758096384 | bytes 22020096 | tf_op jit(solution)/shard_map/pallas_call | solution.py:259
  224.6 11.1 %shard_map.110 = (bf16[448,512]{1,0:T(8,128)(2,1)}, bf16[448,512]{1,0:T(8,128)(2,1)}, bf16[448,512]{1,0:T(8,128)(2,1)}) custom-call(s32[512,128]{1,0:T(8,128)} %copy-done, bf16[3584,1024]{1,0:T(8,128)(2,1)} %rows_ref.17), custom_call_target="tpu_custom_call" | custom-call | flops 4932501504 | bytes 5046272 | tf_op jit(solution)/shard_map/pallas_call | solution.py:195
  243.7 15.7 %shard_map.111 = (bf16[448,512]{1,0:T(8,128)(2,1)}, bf16[448,512]{1,0:T(8,128)(2,1)}, bf16[448,512]{1,0:T(8,128)(2,1)}, bf16[448,512]{1,0:T(8,128)(2,1)}, bf16[448,512]{1,0:T(8,128)(2,1)}) custom-call(s32[512,128]{1,0:T(8,128)} %copy-done, bf16[3584,1024]{1,0:T(8,128)(2,1)} %rows_ref.17), custom_call_target="tpu_custom_call" | custom-call | flops 8220835840 | bytes 5963776 | tf_op jit(solution)/shard_map/pallas_call | solution.py:195
  261.3 17.8 %shard_map.112 = bf16[3584,1024]{1,0:T(8,128)(2,1)} custom-call(s32[256]{0:T(256)} %reshape_squeeze.3.before_ref, s32[3584,128]{1,0:T(8,128)} %broadcast_in_dim.9.code_ref, bf16[3584,1024]{1,0:T(8,128)(2,1)} %initial_ref.6, bf16[448,1024]{1,0:T(8,128)(2,1)} %get-tuple-element.86.refs_0_, bf16[448,1024]{1,0:T(8,128)(2,1)} %collective-permute-done.13.refs_1_, ...), custom_call_target="tpu_custom_call" | custom-call | flops 3758096384 | bytes 22020096 | tf_op jit(solution)/shard_map/pallas_call | solution.py:259
  280.9 13.4 %shard_map.113 = (bf16[448,256]{1,0:T(8,128)(2,1)}, bf16[448,256]{1,0:T(8,128)(2,1)}, bf16[448,256]{1,0:T(8,128)(2,1)}, bf16[448,256]{1,0:T(8,128)(2,1)}, bf16[4...) custom-call(s32[512,128]{1,0:T(8,128)} %copy-done, ...), custom_call_target="tpu_custom_call" | custom-call | flops 6576668672 | bytes 3670016 | tf_op jit(solution)/shard_map/pallas_call | solution.py:195
  299.9 4.1 %collective-permute-done.26.refs_7_ = bf16[448,256]{1,0:T(8,128)(2,1)S(1)} collective-permute-done((bf16[448,256]{1,0:T(8,128)(2,1)}, bf16[448,256]{1,0:T(8,128)(2,1)S(1)}, u32[]{:S(2)}, u32[]{:S(2)}) %collective-permute-start.26) | collective-permute-done | bytes 229408 | tf_op jit(solution)/shard_map/ppermute | solution.py:303
  304.0 4.2 %collective-permute-done.22.refs_3_ = bf16[448,256]{1,0:T(8,128)(2,1)S(1)} collective-permute-done((bf16[448,256]{1,0:T(8,128)(2,1)}, bf16[448,256]{1,0:T(8,128)(2,1)S(1)}, u32[]{:S(2)}, u32[]{:S(2)}) %collective-permute-start.22) | collective-permute-done | bytes 229408 | tf_op jit(solution)/shard_map/ppermute | solution.py:303
  308.2 13.3 %shard_map.114 = (bf16[448,256]{1,0:T(8,128)(2,1)}, bf16[448,256]{1,0:T(8,128)(2,1)}, bf16[448,256]{1,0:T(8,128)(2,1)}, bf16[448,256]{1,0:T(8,128)(2,1)}, bf16[4...) custom-call(s32[512,128]{1,0:T(8,128)} %copy-done, ...), custom_call_target="tpu_custom_call" | custom-call | flops 6576668672 | bytes 3670016 | tf_op jit(solution)/shard_map/pallas_call | solution.py:195
  324.4 13.9 %shard_map.115.refs_0_ = bf16[3584,1024]{1,0:T(8,128)(2,1)} custom-call(s32[256]{0:T(256)} %reshape_squeeze.3.before_ref, s32[3584,128]{1,0:T(8,128)} %broadcast_in_dim.9.code_ref, bf16[3584,1024]{1,0:T(8,128)(2,1)} %initial_ref.9, bf16[448,512]{1,0:T(8,128)(2,1)} %get-tuple-element.97.refs_0_, bf16[448,512]{1,0:T(8,128)(2,1)} %copy-done.12, ...), custom_call_target="tpu_custom_call" | custom-call | flops 1879048192 | bytes 11010048 | tf_op jit(solution)/shard_map/pallas_call | solution.py:259
  341.8 12.1 %shard_map.116.refs_0_ = bf16[3584,1024]{1,0:T(8,128)(2,1)} custom-call(s32[256]{0:T(256)} %reshape_squeeze.3.before_ref, s32[3584,128]{1,0:T(8,128)} %broadcast_in_dim.9.code_ref, bf16[3584,1024]{1,0:T(8,128)(2,1)} %initial_ref.9, bf16[3584,1024]{1,0:T(8,128)(2,1)} %shard_map.115.refs_0_, ...), custom_call_target="tpu_custom_call", output_to_operand_aliasing={{}: (3, {})} | custom-call | flops 939524096 | bytes 5505024 | tf_op jit(solution)/shard_map/pallas_call | solution.py:259
  357.2 4.7 %collective-permute-done.32.refs_6_ = bf16[448,256]{1,0:T(8,128)(2,1)S(1)} collective-permute-done((bf16[448,256]{1,0:T(8,128)(2,1)S(1)}, bf16[448,256]{1,0:T(8,128)(2,1)S(1)}, u32[]{:S(2)}, u32[]{:S(2)}) %collective-permute-start.32) | collective-permute-done | bytes 229408 | tf_op jit(solution)/shard_map/ppermute | solution.py:303
  363.2 12.1 %shard_map.117 = bf16[3584,1024]{1,0:T(8,128)(2,1)} custom-call(s32[256]{0:T(256)} %reshape_squeeze.3.before_ref, s32[3584,128]{1,0:T(8,128)} %broadcast_in_dim.9.code_ref, bf16[3584,1024]{1,0:T(8,128)(2,1)} %initial_ref.9, bf16[3584,1024]{1,0:T(8,128)(2,1)} %shard_map.116.refs_0_, ...), custom_call_target="tpu_custom_call", output_to_operand_aliasing={{}: (3, {})} | custom-call | flops 939524096 | bytes 5505024 | tf_op jit(solution)/shard_map/pallas_call | solution.py:259
  (152 shorter events, 50.8 us)
Async XLA Ops:
  7.2 63.1 %all-gather.3.cloned.1.call-start = ((), (), s32[]{:S(2)}) async-start(), calls=%async_computation.2 | async-start | bytes 1179648 | tf_op jit(solution)/shard_map/all_gather | solution.py:292
  10.4 343.5 %reduce-scatter.2.cloned.1.call-start = ((), (), s32[]{:S(2)}) async-start(), calls=%async_computation.1 | async-start | bytes 4587520 | tf_op jit(solution)/shard_map/reduce_scatter | solution.py:321
  83.2 41.6 %collective-permute-start.1 = (bf16[448,1024]{1,0:T(8,128)(2,1)}, bf16[448,1024]{1,0:T(8,128)(2,1)S(1)}, u32[]{:S(2)}, u32[]{:S(2)}) collective-permute-start(bf16[448,1024]{1,0:T(8,128)(2,1)} %get-tuple-element.66), channel_id=1, source_target_pairs={{0,8},{4,12},{8,0},{12,4},{16,24},{20,28},{24,16},{28,20},{1,9},{5... | collective-permute-start | bytes 2752520 | tf_op jit(solution)/shard_map/ppermute | solution.py:303
  83.7 42.1 %collective-permute-start.2 = (bf16[448,1024]{1,0:T(8,128)(2,1)}, bf16[448,1024]{1,0:T(8,128)(2,1)}, u32[]{:S(2)}, u32[]{:S(2)}) collective-permute-start(bf16[448,1024]{1,0:T(8,128)(2,1)} %get-tuple-element.67), channel_id=1, source_target_pairs={{0,16},{4,20},{8,24},{12,28},{16,0},{20,4},{24,8},{28,12},{1,17},{... | collective-permute-start | bytes 2752520 | tf_op jit(solution)/shard_map/ppermute | solution.py:303
  85.1 60.7 %collective-permute-start.3 = (bf16[448,1024]{1,0:T(8,128)(2,1)}, bf16[448,1024]{1,0:T(8,128)(2,1)}, u32[]{:S(2)}, u32[]{:S(2)}) collective-permute-start(bf16[448,1024]{1,0:T(8,128)(2,1)} %get-tuple-element.69), channel_id=1, source_target_pairs={{0,28},{4,24},{8,20},{12,16},{16,12},{20,8},{24,4},{28,0},{1,29},{... | collective-permute-start | bytes 2752520 | tf_op jit(solution)/shard_map/ppermute | solution.py:303
  85.6 77.6 %collective-permute-start.4 = (bf16[448,1024]{1,0:T(8,128)(2,1)S(1)}, bf16[448,1024]{1,0:T(8,128)(2,1)}, u32[]{:S(2)}, u32[]{:S(2)}) collective-permute-start(bf16[448,1024]{1,0:T(8,128)(2,1)S(1)} %copy-done.28), channel_id=1, source_target_pairs={{0,12},{4,8},{8,4},{12,0},{16,28},{20,24},{24,20},{28,16},{1,13},{... | collective-permute-start | bytes 2752520 | tf_op jit(solution)/shard_map/ppermute | solution.py:303
  106.0 58.8 %collective-permute-start.5 = (bf16[448,1024]{1,0:T(8,128)(2,1)}, bf16[448,1024]{1,0:T(8,128)(2,1)}, u32[]{:S(2)}, u32[]{:S(2)}) collective-permute-start(bf16[448,1024]{1,0:T(8,128)(2,1)} %get-tuple-element.71), channel_id=1, source_target_pairs={{0,20},{4,16},{8,28},{12,24},{16,4},{20,0},{24,12},{28,8},{1,21},{... | collective-permute-start | bytes 2752520 | tf_op jit(solution)/shard_map/ppermute | solution.py:303
  124.8 39.9 %collective-permute-start.6 = (bf16[448,1024]{1,0:T(8,128)(2,1)}, bf16[448,1024]{1,0:T(8,128)(2,1)}, u32[]{:S(2)}, u32[]{:S(2)}) collective-permute-start(bf16[448,1024]{1,0:T(8,128)(2,1)} %get-tuple-element.72), channel_id=1, source_target_pairs={{0,4},{4,0},{8,12},{12,8},{16,20},{20,16},{24,28},{28,24},{1,5},{5... | collective-permute-start | bytes 2752520 | tf_op jit(solution)/shard_map/ppermute | solution.py:303
  144.3 50.6 %collective-permute-start.7 = (bf16[448,1024]{1,0:T(8,128)(2,1)}, bf16[448,1024]{1,0:T(8,128)(2,1)S(1)}, u32[]{:S(2)}, u32[]{:S(2)}) collective-permute-start(bf16[448,1024]{1,0:T(8,128)(2,1)} %get-tuple-element.78), channel_id=1, source_target_pairs={{0,24},{4,28},{8,16},{12,20},{16,8},{20,12},{24,0},{28,4},{1,25},{... | collective-permute-start | bytes 2752520 | tf_op jit(solution)/shard_map/ppermute | solution.py:303
  145.8 57.8 %collective-permute-start.8 = (bf16[448,1024]{1,0:T(8,128)(2,1)}, bf16[448,1024]{1,0:T(8,128)(2,1)S(1)}, u32[]{:S(2)}, u32[]{:S(2)}) collective-permute-start(bf16[448,1024]{1,0:T(8,128)(2,1)} %get-tuple-element.79), channel_id=1, source_target_pairs={{0,8},{4,12},{8,0},{12,4},{16,24},{20,28},{24,16},{28,20},{1,9},{5... | collective-permute-start | bytes 2752520 | tf_op jit(solution)/shard_map/ppermute | solution.py:303
  163.2 61.4 %collective-permute-start.9 = (bf16[448,1024]{1,0:T(8,128)(2,1)}, bf16[448,1024]{1,0:T(8,128)(2,1)S(1)}, u32[]{:S(2)}, u32[]{:S(2)}) collective-permute-start(bf16[448,1024]{1,0:T(8,128)(2,1)} %get-tuple-element.80), channel_id=1, source_target_pairs={{0,16},{4,20},{8,24},{12,28},{16,0},{20,4},{24,8},{28,12},{1,17},{... | collective-permute-start | bytes 2752520 | tf_op jit(solution)/shard_map/ppermute | solution.py:303
  193.1 44.1 %collective-permute-start.10 = (bf16[448,1024]{1,0:T(8,128)(2,1)}, bf16[448,1024]{1,0:T(8,128)(2,1)}, u32[]{:S(2)}, u32[]{:S(2)}) collective-permute-start(bf16[448,1024]{1,0:T(8,128)(2,1)} %get-tuple-element.82), channel_id=1, source_target_pairs={{0,28},{4,24},{8,20},{12,16},{16,12},{20,8},{24,4},{28,0},{1,29},{... | collective-permute-start | bytes 2752520 | tf_op jit(solution)/shard_map/ppermute | solution.py:303
  194.7 47.3 %collective-permute-start.11 = (bf16[448,1024]{1,0:T(8,128)(2,1)}, bf16[448,1024]{1,0:T(8,128)(2,1)}, u32[]{:S(2)}, u32[]{:S(2)}) collective-permute-start(bf16[448,1024]{1,0:T(8,128)(2,1)} %get-tuple-element.83), channel_id=1, source_target_pairs={{0,12},{4,8},{8,4},{12,0},{16,28},{20,24},{24,20},{28,16},{1,13},{... | collective-permute-start | bytes 2752520 | tf_op jit(solution)/shard_map/ppermute | solution.py:303
  194.9 48.8 %collective-permute-start.12 = (bf16[448,1024]{1,0:T(8,128)(2,1)}, bf16[448,1024]{1,0:T(8,128)(2,1)}, u32[]{:S(2)}, u32[]{:S(2)}) collective-permute-start(bf16[448,1024]{1,0:T(8,128)(2,1)} %get-tuple-element.84), channel_id=1, source_target_pairs={{0,20},{4,16},{8,28},{12,24},{16,4},{20,0},{24,12},{28,8},{1,21},{... | collective-permute-start | bytes 2752520 | tf_op jit(solution)/shard_map/ppermute | solution.py:303
  203.6 40.1 %collective-permute-start.13 = (bf16[448,1024]{1,0:T(8,128)(2,1)}, bf16[448,1024]{1,0:T(8,128)(2,1)}, u32[]{:S(2)}, u32[]{:S(2)}) collective-permute-start(bf16[448,1024]{1,0:T(8,128)(2,1)} %get-tuple-element.85), channel_id=1, source_target_pairs={{0,4},{4,0},{8,12},{12,8},{16,20},{20,16},{24,28},{28,24},{1,5},{5... | collective-permute-start | bytes 2752520 | tf_op jit(solution)/shard_map/ppermute | solution.py:303
  235.7 43.5 %collective-permute-start.14 = (bf16[448,512]{1,0:T(8,128)(2,1)}, bf16[448,512]{1,0:T(8,128)(2,1)S(1)}, u32[]{:S(2)}, u32[]{:S(2)}) collective-permute-start(bf16[448,512]{1,0:T(8,128)(2,1)} %get-tuple-element.89), channel_id=1, source_target_pairs={{0,24},{4,28},{8,16},{12,20},{16,8},{20,12},{24,0},{28,4},{1,25},{... | collective-permute-start | bytes 1376264 | tf_op jit(solution)/shard_map/ppermute | solution.py:303
  237.2 43.6 %collective-permute-start.15 = (bf16[448,512]{1,0:T(8,128)(2,1)}, bf16[448,512]{1,0:T(8,128)(2,1)S(1)}, u32[]{:S(2)}, u32[]{:S(2)}) collective-permute-start(bf16[448,512]{1,0:T(8,128)(2,1)} %get-tuple-element.90), channel_id=1, source_target_pairs={{0,8},{4,12},{8,0},{12,4},{16,24},{20,28},{24,16},{28,20},{1,9},{5... | collective-permute-start | bytes 1376264 | tf_op jit(solution)/shard_map/ppermute | solution.py:303
  242.0 38.9 %collective-permute-start.16 = (bf16[448,512]{1,0:T(8,128)(2,1)}, bf16[448,512]{1,0:T(8,128)(2,1)S(1)}, u32[]{:S(2)}, u32[]{:S(2)}) collective-permute-start(bf16[448,512]{1,0:T(8,128)(2,1)} %get-tuple-element.91), channel_id=1, source_target_pairs={{0,16},{4,20},{8,24},{12,28},{16,0},{20,4},{24,8},{28,12},{1,17},{... | collective-permute-start | bytes 1376264 | tf_op jit(solution)/shard_map/ppermute | solution.py:303
  259.4 36.6 %collective-permute-start.17 = (bf16[448,512]{1,0:T(8,128)(2,1)}, bf16[448,512]{1,0:T(8,128)(2,1)S(1)}, u32[]{:S(2)}, u32[]{:S(2)}) collective-permute-start(bf16[448,512]{1,0:T(8,128)(2,1)} %get-tuple-element.93), channel_id=1, source_target_pairs={{0,28},{4,24},{8,20},{12,16},{16,12},{20,8},{24,4},{28,0},{1,29},{... | collective-permute-start | bytes 1376264 | tf_op jit(solution)/shard_map/ppermute | solution.py:303
  261.2 35.4 %collective-permute-start.18 = (bf16[448,512]{1,0:T(8,128)(2,1)}, bf16[448,512]{1,0:T(8,128)(2,1)S(1)}, u32[]{:S(2)}, u32[]{:S(2)}) collective-permute-start(bf16[448,512]{1,0:T(8,128)(2,1)} %get-tuple-element.94), channel_id=1, source_target_pairs={{0,12},{4,8},{8,4},{12,0},{16,28},{20,24},{24,20},{28,16},{1,13},{... | collective-permute-start | bytes 1376264 | tf_op jit(solution)/shard_map/ppermute | solution.py:303
  298.7 39.7 %collective-permute-start.23 = (bf16[448,256]{1,0:T(8,128)(2,1)}, bf16[448,256]{1,0:T(8,128)(2,1)S(1)}, u32[]{:S(2)}, u32[]{:S(2)}) collective-permute-start(bf16[448,256]{1,0:T(8,128)(2,1)} %get-tuple-element.104), channel_id=1, source_target_pairs={{0,12},{4,8},{8,4},{12,0},{16,28},{20,24},{24,20},{28,16},{1,13},{... | collective-permute-start | bytes 688136 | tf_op jit(solution)/shard_map/ppermute | solution.py:303
  304.0 35.2 %collective-permute-start.25 = (bf16[448,256]{1,0:T(8,128)(2,1)}, bf16[448,256]{1,0:T(8,128)(2,1)S(1)}, u32[]{:S(2)}, u32[]{:S(2)}) collective-permute-start(bf16[448,256]{1,0:T(8,128)(2,1)} %get-tuple-element.105), channel_id=1, source_target_pairs={{0,20},{4,16},{8,28},{12,24},{16,4},{20,0},{24,12},{28,8},{1,21},{... | collective-permute-start | bytes 688136 | tf_op jit(solution)/shard_map/ppermute | solution.py:303
  308.2 31.7 %collective-permute-start.21 = (bf16[448,256]{1,0:T(8,128)(2,1)}, bf16[448,256]{1,0:T(8,128)(2,1)S(1)}, u32[]{:S(2)}, u32[]{:S(2)}) collective-permute-start(bf16[448,256]{1,0:T(8,128)(2,1)} %get-tuple-element.106), channel_id=1, source_target_pairs={{0,4},{4,0},{8,12},{12,8},{16,20},{20,16},{24,28},{28,24},{1,5},{5... | collective-permute-start | bytes 688136 | tf_op jit(solution)/shard_map/ppermute | solution.py:303
  321.6 32.3 %collective-permute-start.33 = (bf16[448,256]{1,0:T(8,128)(2,1)}, bf16[448,256]{1,0:T(8,128)(2,1)S(1)}, u32[]{:S(2)}, u32[]{:S(2)}) collective-permute-start(bf16[448,256]{1,0:T(8,128)(2,1)} %get-tuple-element.109), channel_id=1, source_target_pairs={{0,24},{4,28},{8,16},{12,20},{16,8},{20,12},{24,0},{28,4},{1,25},{... | collective-permute-start | bytes 688136 | tf_op jit(solution)/shard_map/ppermute | solution.py:303
  (50 other events, 722.1 us)
Sparse Core Ops, SparseCore 0:
  10.6 26.1 all-gather.2
  81.7 68.7 reduce-scatter.1

commit v2 on v1

v2 whole, which is shorter than its diff:
```python
import functools

import jax
import jax.numpy as jnp
from jax import lax
from jax.experimental import pallas as pl
from jax.experimental.pallas import tpu as pltpu
from jax.sharding import PartitionSpec as P

D = 4096
A_DEV = 32
MESH = pl.DeviceIdType.MESH

PEERS = 8
LANES = 128
TILE = 256
SLOT = 64
COST_ROWS = 512
OVER_LANES = (((1,), (1,)), ((), ()))
CODE = 1024


def one_hot(hit):
    return jnp.where(hit, 1.0, 0.0).astype(jnp.bfloat16)


def matmul(a, b):
    return jnp.dot(a, b, preferred_element_type=jnp.float32)


def count_ranks(count, me, perm_ref, code_ref, slot_ref, before_ref, hot, halves, counts, sent):
    pad = perm_ref.shape[0]
    used = count // LANES
    slots = count // PEERS
    perm = perm_ref[...]
    source = jnp.zeros_like(perm)
    for k in range(1, PEERS + 1):
        source = source + jnp.where(perm >= k * count, 1, 0)
    row = perm - source * count
    masks = jnp.concatenate([jnp.where(source == k, 1.0, 0.0) for k in range(PEERS)], axis=0)
    packed = masks.astype(jnp.bfloat16)
    shape = (LANES, LANES)
    lane_before = one_hot(lax.broadcasted_iota(jnp.int32, shape, 0) < lax.broadcasted_iota(jnp.int32, shape, 1))
    within = matmul(packed, lane_before)
    totals = matmul(packed, jnp.ones(shape, jnp.bfloat16)).astype(jnp.bfloat16)
    shape = (PEERS * pad, PEERS * pad)
    left, right = lax.broadcasted_iota(jnp.int32, shape, 0), lax.broadcasted_iota(jnp.int32, shape, 1)
    row_before = one_hot((right < left) & (right >= left - lax.rem(left, pad)))
    ahead = matmul(row_before, totals)
    counts[...] = ahead.astype(jnp.int32)
    ranked = masks * (within + ahead)
    rank = ranked[:pad]
    for k in range(1, PEERS):
        rank = rank + ranked[k * pad : (k + 1) * pad]
    rank = rank.astype(jnp.int32)
    code_ref[...] = (source ^ me) * CODE + rank
    slot_ref[...] = jnp.minimum((source ^ me) * slots + rank, count - 1)
    for k in range(PEERS):
        before_ref[k] = counts[pl.ds(pl.multiple_of((me ^ k) * pad, pad), pad), :]

    high = lax.shift_right_logical(row, 8).astype(jnp.float32)
    low = (row & 255).astype(jnp.float32)
    block = lax.broadcasted_iota(jnp.int32, (PEERS, LANES), 0)
    slot = lax.broadcasted_iota(jnp.int32, (slots, LANES), 0)
    for j in range(used):
        at = slice(j * LANES, (j + 1) * LANES)
        one = slice(j, j + 1)
        mine = source[one] == block
        both = [jnp.where(mine, part[one], 0.0) for part in (high, low)]
        halves[:, at] = jnp.concatenate(both, axis=0).astype(jnp.bfloat16)
        hot[:, at] = one_hot(rank[one] == slot)
    found = lax.dot_general(halves[...], hot[...], OVER_LANES, preferred_element_type=jnp.float32)
    wanted = found[:PEERS] * 256.0 + found[PEERS:]
    for k in range(PEERS):
        sent[k, :, :slots] = jnp.broadcast_to(wanted[k : k + 1], (8, slots)).astype(jnp.int32)
        sent[k, :, slots:] = jnp.zeros((8, sent.shape[2] - slots), jnp.int32)


def spread_out(rows_ref, spread, base=0):
    tall, width = rows_ref.shape
    tiles = width // LANES

    def step(m, carry):
        for c in range(tiles):
            v = rows_ref[pl.ds(pl.multiple_of(m * 16, 16), 16), c * LANES : (c + 1) * LANES].astype(jnp.float32)
            for h in range(2):
                to = base + (m * 2 + h) * 8 * tiles + c * 8
                spread[pl.ds(pl.multiple_of(to, 8), 8), :] = v[h * 8 : h * 8 + 8]
        return carry

    lax.fori_loop(0, tall // 16, step, 0)


def sixteen(index_of, spread, turn, tiles):
    for s in range(16):
        i = index_of(s)
        begin = lax.shift_right_logical(i, 3) * (8 * tiles) + (i & 7)
        turn[pl.ds((s // 8) * 8 * tiles + s % 8, tiles, stride=8), :] = spread[pl.ds(begin, tiles, stride=8), :]
    for c in range(tiles):
        yield c, jnp.concatenate([turn[(h * tiles + c) * 8 : (h * tiles + c + 1) * 8, :] for h in range(2)], axis=0)


def first_kernel(count, chunks, perm_ref, up_a, gate_a, up_b, gate_b, down_b, code_ref, slot_ref, before_ref, partial_ref, up_moved, up_sent, *refs):
    gate_rows, refs = refs[:PEERS], refs[PEERS:]
    down_rows = [refs[n * PEERS : (n + 1) * PEERS] for n in range(len(chunks))]
    refs = refs[len(chunks) * PEERS :]
    hot, halves, counts, sent, got, asked, held, window, windows, wide, rows, spread, turn, stage, part = refs[:15]
    ask_send, ask_recv, up_send, up_recv, win_send, win_recv, strip_sems, load_sems, stage_sems, own_sem, part_sem = refs[15:]
    me = lax.axis_index("rows")
    slots = count // PEERS
    stride = count // A_DEV
    barrier = pltpu.get_barrier_semaphore()
    for k in range(1, PEERS):
        pl.semaphore_signal(barrier, inc=1, device_id={"rows": me ^ k}, device_id_type=MESH)

    strips = []
    for m, ref in enumerate((up_a, gate_a)):
        for i in range(A_DEV):
            at = m * A_DEV + i
            strips.append(
                pltpu.make_async_copy(ref.at[pl.ds(i * stride, 16)], held.at[pl.ds(at * 16, 16)], strip_sems.at[at])
            )
    for copy in strips:
        copy.start()
    loads = [pltpu.make_async_copy(ref, rows.at[n], load_sems.at[n]) for n, ref in enumerate((up_b, gate_b))]
    for copy in loads:
        copy.start()

    for copy in strips:
        copy.wait()
    shape = (2 * A_DEV, 32 * A_DEV)
    first = lax.broadcasted_iota(jnp.int32, shape, 0) * 16 == lax.broadcasted_iota(jnp.int32, shape, 1)
    window[...] = matmul(one_hot(first), held[...]).astype(jnp.bfloat16)
    windows[0] = window[...]
    pl.semaphore_wait(barrier, PEERS - 1)

    def remote(src, dst, send, recv, peer):
        return pltpu.make_async_remote_copy(
            src_ref=src, dst_ref=dst, send_sem=send, recv_sem=recv, device_id={"rows": peer}, device_id_type=MESH
        )

    across = [
        remote(window, windows.at[k], win_send.at[k], win_recv.at[k], me ^ k) for k in (6, 2, 4)
    ]
    for copy in across:
        copy.start()

    count_ranks(count, me, perm_ref, code_ref, slot_ref, before_ref, hot, halves, counts, sent)
    asks = [remote(sent.at[me ^ k], got.at[k], ask_send.at[k], ask_recv.at[k], me ^ k) for k in (6, 7, 4, 5, 2, 3, 1)]
    for copy in asks:
        copy.start()
    own = pltpu.make_async_copy(sent.at[me], got.at[0], own_sem)
    own.start()
    loads[0].wait()
    spread_out(rows.at[0], spread)
    own.wait()
    for copy in asks:
        copy.wait()
    got[...] = jnp.clip(got[...], 0, count - 1)
    own = pltpu.make_async_copy(got, asked, own_sem)
    own.start()
    own.wait()

    def gather(k, buffer):
        def step(t, carry):
            for c, tile in sixteen(lambda s: asked[k, 0, t * 16 + s], spread, turn, 8):
                stage[buffer, pl.ds(pl.multiple_of(t * 16, 16), 16), c * LANES : (c + 1) * LANES] = tile.astype(
                    jnp.bfloat16
                )
            return carry

        lax.fori_loop(0, slots // 16, step, 0)

    def up_step(n, carry):
        k = n ^ 6
        gather(k, 0)

        @pl.when(k > 0)
        def _():
            copy = pltpu.make_async_copy(stage.at[0], up_sent.at[k], stage_sems.at[0])
            copy.start()
            copy.wait()
            remote(up_sent.at[k], up_moved.at[k], up_send.at[k], up_recv.at[k], me ^ k).start()

        @pl.when(k == 0)
        def _():
            copy = pltpu.make_async_copy(stage.at[0], up_moved.at[0], stage_sems.at[0])
            copy.start()
            copy.wait()

        return carry

    lax.fori_loop(0, PEERS, up_step, 0)

    for copy in across:
        copy.wait()
    beside = [remote(windows.at[k], windows.at[k + 1], win_send.at[k + 1], win_recv.at[k + 1], me ^ 1) for k in (0, 2, 4, 6)]
    for copy in beside:
        copy.start()

    def collect(outs):
        def copies(j, buffer):
            for n, (ref, begin, size) in enumerate(outs[j]):
                yield pltpu.make_async_copy(
                    stage.at[buffer, :, pl.ds(begin, size)], ref, stage_sems.at[n * 2 + buffer]
                )

        def step(n, carry):
            buffer = n & 1
            k = n ^ 6

            @pl.when(n >= 2)
            def _():
                for copy in copies(0, buffer):
                    copy.wait()

            gather(k, buffer)
            for j in range(PEERS):

                @pl.when(k == j)
                def _():
                    for copy in copies(j, buffer):
                        copy.start()

            return carry

        lax.fori_loop(0, PEERS, step, 0)
        for buffer in range(2):
            for copy in copies(0, buffer):
                copy.wait()

    loads[1].wait()
    spread_out(rows.at[1], spread)
    collect([[(ref, 0, ref.shape[1])] for ref in gate_rows])

    for copy in beside:
        copy.wait()
    for k in range(PEERS):
        for m in range(2):
            wide[m, k * A_DEV : (k + 1) * A_DEV, :] = windows[k, m * A_DEV : (m + 1) * A_DEV, :]
    depth = COST_ROWS
    group = part.shape[2]

    def cost(j, carry):
        at = pl.ds(pl.multiple_of(j * depth, depth), depth)
        both = [
            lax.dot_general(wide[m], rows[m, at, :], OVER_LANES, preferred_element_type=jnp.float32) for m in range(2)
        ]
        value = both[0] + both[1]
        for k in range(PEERS):
            for c in range(part.shape[0]):
                begin = k * A_DEV + c * group
                part[c, me ^ k, :, at] = value[begin : begin + group]
        return carry

    lax.fori_loop(0, count // depth, cost, 0)
    share = pltpu.make_async_copy(part, partial_ref, part_sem)
    share.start()
    load = pltpu.make_async_copy(down_b, rows.at[0], load_sems.at[0])
    load.start()
    load.wait()
    spread_out(rows.at[0], spread)
    starts = [sum(chunks[:n]) for n in range(len(chunks))]
    collect([[(down_rows[n][k], starts[n], chunks[n]) for n in range(len(chunks))] for k in range(PEERS)])
    share.wait()
    for k in range(1, PEERS):
        remote(up_sent.at[k], up_moved.at[k], up_send.at[k], up_recv.at[k], me ^ k).wait()


def first(up_a, gate_a, up_b, gate_b, down_b, perm, chunks):
    count, features = up_a.shape
    cols = lax.axis_size("cols")
    used = count // LANES
    pad = -(-used // 8) * 8
    slots = count // PEERS
    lanes = -(-slots // LANES) * LANES
    grid = jnp.pad(perm.reshape(used, LANES), ((0, pad - used), (0, 0)), constant_values=PEERS * count)
    vmem = pl.BlockSpec(memory_space=pltpu.VMEM)
    hbm = pl.BlockSpec(memory_space=pltpu.HBM)
    bf16, f32, i32 = jnp.bfloat16, jnp.float32, jnp.int32
    shapes = [
        jax.ShapeDtypeStruct((pad, LANES), i32),
        jax.ShapeDtypeStruct((pad, LANES), i32),
        jax.ShapeDtypeStruct((PEERS, pad, LANES), i32),
        jax.ShapeDtypeStruct((cols, PEERS, A_DEV // cols, count), f32),
        jax.ShapeDtypeStruct((PEERS, slots, features), bf16),
        jax.ShapeDtypeStruct((PEERS, slots, features), bf16),
    ]
    shapes += [jax.ShapeDtypeStruct((slots, size), bf16) for size in (features,) + chunks for _ in range(PEERS)]
    got = pl.pallas_call(
        functools.partial(first_kernel, count, chunks),
        out_shape=shapes,
        in_specs=[vmem] + [hbm] * 5,
        out_specs=[vmem] * 3 + [hbm] * (len(shapes) - 3),
        scratch_shapes=[
            pltpu.VMEM((slots, count), bf16),
            pltpu.VMEM((2 * PEERS, count), bf16),
            pltpu.VMEM((PEERS * pad, LANES), i32),
            pltpu.VMEM((PEERS, 8, lanes), i32),
            pltpu.VMEM((PEERS, 8, lanes), i32),
            pltpu.SMEM((PEERS, 8, lanes), i32),
            pltpu.VMEM((32 * A_DEV, features), bf16),
            pltpu.VMEM((2 * A_DEV, features), bf16),
            pltpu.VMEM((PEERS, 2 * A_DEV, features), bf16),
            pltpu.VMEM((2, A_DEV * PEERS, features), bf16),
            pltpu.VMEM((2, count, features), bf16),
            pltpu.VMEM((count * 8 + 8 * 8, LANES), f32),
            pltpu.VMEM((LANES + 8 * 8, LANES), f32),
            pltpu.VMEM((2, slots, features), bf16),
            pltpu.VMEM((cols, PEERS, A_DEV // cols, count), f32),
        ]
        + [pltpu.SemaphoreType.DMA((PEERS,))] * 6
        + [
            pltpu.SemaphoreType.DMA((2 * A_DEV,)),
            pltpu.SemaphoreType.DMA((2,)),
            pltpu.SemaphoreType.DMA((2 * len(chunks),)),
            pltpu.SemaphoreType.DMA,
            pltpu.SemaphoreType.DMA,
        ],
        compiler_params=pltpu.CompilerParams(
            collective_id=0, has_side_effects=True, vmem_limit_bytes=60 * 1024 * 1024
        ),
    )(grid, up_a, gate_a, up_b, gate_b, down_b)
    code, slot, before, partial_value, up_moved = got[:5]
    lists = [got[6 + n * PEERS : 6 + (n + 1) * PEERS] for n in range(1 + len(chunks))]
    return code, slot, before, partial_value, up_moved, lists


def place_kernel(before_ref, code_ref, initial_ref, *refs):
    *rest, out_ref, held, total = refs
    arrived = rest[-PEERS:]
    t = pl.program_id(0)
    pad = before_ref.shape[0] // PEERS
    last = arrived[0].shape[0] - SLOT
    per = TILE // LANES
    starts, rounds = [], jnp.int32(1)
    for k in range(PEERS):
        lo = before_ref[k * pad + t * per]
        hi = before_ref[k * pad + t * per + per]
        start = lax.shift_left(lax.shift_right_logical(lo, 4), 4)
        starts.append(start)
        rounds = jnp.maximum(rounds, lax.shift_right_logical(hi - start + SLOT - 1, 6))
    lane = lax.broadcasted_iota(jnp.int32, (1, PEERS * SLOT), 1)
    peer = lax.shift_right_logical(lane, 6)
    code = code_ref[...]
    code = code[:, :1]

    def gathered(j):
        first = jnp.zeros_like(lane)
        at = jnp.zeros_like(lane)
        for k in range(PEERS):
            begin = starts[k] + j * SLOT
            from_row = jnp.minimum(begin, last)
            held[k * SLOT : (k + 1) * SLOT, :] = arrived[k][pl.ds(pl.multiple_of(from_row, 16), SLOT), :]
            first = jnp.where(peer == k, begin, first)
            at = jnp.where(peer == k, from_row, at)
        at = at + (lane & (SLOT - 1))
        codes = jnp.where(at >= first, peer * CODE + at, -1)
        return matmul(one_hot(code == codes), held[...])

    total[...] = gathered(jnp.int32(0))

    def more(j, carry):
        total[...] += gathered(j)
        return carry

    lax.fori_loop(1, rounds, more, 0)
    out_ref[...] = ((initial_ref[...].astype(jnp.float32) + total[...]) * 0.5).astype(out_ref.dtype)


def place(before, code, initial, arrived, start, out=None):
    count, features = initial.shape
    slots, size = arrived[0].shape
    wide = lambda t, *_: (t, start // size)
    extra = [] if out is None else [out]
    return pl.pallas_call(
        place_kernel,
        out_shape=jax.ShapeDtypeStruct((count, features), initial.dtype),
        grid_spec=pltpu.PrefetchScalarGridSpec(
            num_scalar_prefetch=1,
            grid=(count // TILE,),
            in_specs=[
                pl.BlockSpec((TILE, LANES), lambda t, *_: (t, 0)),
                pl.BlockSpec((TILE, size), wide),
            ]
            + [pl.BlockSpec(memory_space=pl.ANY)] * len(extra)
            + [pl.BlockSpec((slots, size), lambda t, *_: (0, 0))] * PEERS,
            out_specs=pl.BlockSpec((TILE, size), wide),
            scratch_shapes=[
                pltpu.VMEM((PEERS * SLOT, size), jnp.bfloat16),
                pltpu.VMEM((TILE, size), jnp.float32),
            ],
        ),
        input_output_aliases={3: 0} if extra else {},
        compiler_params=pltpu.CompilerParams(vmem_limit_bytes=60 * 1024 * 1024),
        cost_estimate=pl.CostEstimate(
            flops=2 * count * PEERS * SLOT * size, bytes_accessed=6 * count * size, transcendentals=0
        ),
    )(before, code, initial, *extra, *arrived)


def place_rows_kernel(slot_ref, initial_ref, *refs):
    *arrived, out_ref, spread, turn = refs
    t = pl.program_id(0)
    tall, width = initial_ref.shape
    tiles = width // LANES

    @pl.when(t == 0)
    def _():
        for k in range(PEERS):
            spread_out(arrived[k], spread, k * arrived[k].shape[0] * tiles)

    def step(j, carry):
        at = pl.ds(pl.multiple_of(j * 16, 16), 16)
        for c, tile in sixteen(lambda s: slot_ref[t * tall + j * 16 + s], spread, turn, tiles):
            lanes = slice(c * LANES, (c + 1) * LANES)
            out_ref[at, lanes] = ((initial_ref[at, lanes].astype(jnp.float32) + tile) * 0.5).astype(out_ref.dtype)
        return carry

    lax.fori_loop(0, tall // 16, step, 0)


def place_rows(slot, initial, arrived):
    count, features = initial.shape
    slots = count // PEERS
    if isinstance(arrived, list):
        specs = [pl.BlockSpec((slots, features), lambda t, *_: (0, 0))] * PEERS
    else:
        specs = [pl.BlockSpec((None, slots, features), functools.partial(lambda k, t, *_: (k, 0, 0), k)) for k in range(PEERS)]
        arrived = [arrived] * PEERS
    tall = count // 7 if count % (7 * 16) == 0 else LANES
    return pl.pallas_call(
        place_rows_kernel,
        out_shape=jax.ShapeDtypeStruct((count, features), initial.dtype),
        grid_spec=pltpu.PrefetchScalarGridSpec(
            num_scalar_prefetch=1,
            grid=(count // tall,),
            in_specs=[pl.BlockSpec((tall, features), lambda t, *_: (t, 0))] + specs,
            out_specs=pl.BlockSpec((tall, features), lambda t, *_: (t, 0)),
            scratch_shapes=[
                pltpu.VMEM(((count + 8) * features // LANES, LANES), jnp.float32),
                pltpu.VMEM(((16 + 8) * features // LANES, LANES), jnp.float32),
            ],
        ),
        compiler_params=pltpu.CompilerParams(vmem_limit_bytes=60 * 1024 * 1024),
        cost_estimate=pl.CostEstimate(flops=0, bytes_accessed=6 * count * features, transcendentals=0),
    )(slot, initial, *arrived)


def balanced(up_a, gate_a, down_a, up_b, gate_b, down_b, perm):
    row_count, features = up_a.shape
    cost_scale = (2.0 * D) ** (-0.5)
    chunks = (features // 2, features // 4, features // 4)
    code, slot, before, partial_value, up_moved, lists = first(up_a, gate_a, up_b, gate_b, down_b, perm, chunks)
    before = before[:, :, 0].reshape(-1)
    slot = slot.reshape(-1)
    code = jnp.broadcast_to(code.reshape(-1)[:row_count, None], (row_count, LANES))

    def after(value, *others):
        return lax.optimization_barrier((value,) + others)[0]

    def exchange(rows, ks, *others):
        return {
            k: lax.ppermute(after(rows[k], *others), "rows", [(i, i ^ k) for i in range(PEERS)]) for k in ks
        }

    def parts(rows, *moved):
        got = {0: rows[0]}
        for some in moved:
            got.update(some)
        return [got[k] for k in range(PEERS)]

    gate, down = lists[0], lists[1:]
    gate_first = exchange(gate, (6, 7, 4, 5, 2))
    partial_value = after(partial_value, *(gate[k] for k in (6, 7, 4, 5, 2)))
    shares = lax.all_to_all(partial_value, "cols", split_axis=0, concat_axis=0, tiled=True)
    up_mean = place_rows(slot, up_a, up_moved)
    gate_last = exchange(gate, (3, 1), up_mean)
    left = exchange(down[0], (6, 7, 4, 5, 2, 3, 1), up_mean)
    gate_mean = place_rows(slot, gate_a, parts(gate, gate_first, gate_last))
    middle = exchange(down[1], (6, 7, 4, 5, 2, 3, 1), gate_mean)
    right = exchange(down[2], (6, 7, 4, 5, 2, 3, 1), gate_mean)
    down_mean = place(before, code, down_a, parts(down[0], left), 0)
    down_mean = place(before, code, down_a, parts(down[1], middle), chunks[0], down_mean)
    down_mean = place(before, code, down_a, parts(down[2], right), chunks[0] + chunks[1], down_mean)
    total = (shares[0] + shares[1]) + (shares[2] + shares[3])
    costs = (total.transpose(1, 0, 2).reshape(-1, row_count) * cost_scale).T
    return (costs, up_mean, gate_mean, down_mean)


def pick(array, index):
    rows = jnp.arange(array.shape[0], dtype=jnp.int32)
    hot = (index[:, None] == rows[None, :]).astype(array.dtype)
    return jnp.dot(hot, array, preferred_element_type=jnp.float32).astype(array.dtype)


def mix(initial, picked):
    return ((initial.astype(jnp.float32) + picked.astype(jnp.float32)) * 0.5).astype(jnp.bfloat16)


def general(up_a, gate_a, down_a, up_b, gate_b, down_b, perm):
    row_count, features = up_a.shape
    stride = row_count // A_DEV
    cost_scale = (2.0 * D) ** (-0.5)
    peers = lax.axis_size("rows")
    cols = lax.axis_size("cols")
    capacity = max(2, (row_count + peers - 1) // peers)

    source = perm // row_count
    local_row = perm % row_count
    blocks = jnp.arange(peers, dtype=jnp.int32)
    matches = (source[None, :] == blocks[:, None]).astype(jnp.int32)
    order = jnp.arange(row_count, dtype=jnp.int32)
    ahead = jnp.dot(
        matches.astype(jnp.bfloat16),
        (order[:, None] < order[None, :]).astype(jnp.bfloat16),
        preferred_element_type=jnp.float32,
    )
    arrival_rank = jnp.sum(ahead.astype(jnp.int32) * matches, axis=0)
    high = (local_row // 256).astype(jnp.bfloat16)
    low = (local_row % 256).astype(jnp.bfloat16)
    halves = jnp.stack([high, low])[:, None, :] * matches.astype(jnp.bfloat16)[None]
    at_rank = (arrival_rank[None, :] == jnp.arange(capacity, dtype=jnp.int32)[:, None]).astype(jnp.bfloat16)
    found = jnp.einsum("hsi,ri->hsr", halves, at_rank, preferred_element_type=jnp.float32)
    wanted = found[0].astype(jnp.int32) * 256 + found[1].astype(jnp.int32)
    asked = lax.all_to_all(wanted, "rows", split_axis=0, concat_axis=0, tiled=True).reshape(-1)
    slot = source * capacity + arrival_rank

    window = jnp.concatenate([up_a[::stride], gate_a[::stride]], axis=0)
    pieces = lax.all_gather(window, "rows").reshape(peers, 2, A_DEV, features)
    wide = pieces.transpose(1, 2, 0, 3).reshape(2, A_DEV * peers, features)
    partial_value = jnp.einsum("kd,jd->kj", wide[0], up_b, preferred_element_type=jnp.float32)
    partial_value = partial_value + jnp.einsum("kd,jd->kj", wide[1], gate_b, preferred_element_type=jnp.float32)
    total = lax.psum_scatter(partial_value.reshape(cols, -1, row_count), "cols", scatter_dimension=0)

    def averaged(initial, other):
        moved = pick(other, asked).reshape(peers, capacity, features)
        moved = lax.all_to_all(moved, "rows", split_axis=0, concat_axis=0, tiled=True)
        return mix(initial, pick(moved.reshape(-1, features), slot))

    return (
        (total * cost_scale).T,
        averaged(up_a, up_b),
        averaged(gate_a, gate_b),
        averaged(down_a, down_b),
    )


def solution(mesh):
    def local(up_a, *rest):
        row_count, features = up_a.shape
        even = mesh.shape["rows"] == PEERS and row_count % (PEERS * 16) == 0 and row_count % (A_DEV * 16) == 0
        even = even and row_count % COST_ROWS == 0 and SLOT <= row_count // PEERS < CODE
        even = even and features == 8 * LANES and mesh.shape["cols"] == A_DEV // 8
        return (balanced if even else general)(up_a, *rest)

    placed = (P("rows", "cols"),) * 6 + (P("rows"),)
    return jax.shard_map(
        local,
        mesh=mesh,
        in_specs=placed,
        out_specs=(P("rows", "cols"),) * 4,
        check_vma=False,
    )
```

time: 384 us -> 338 us (0.88)
  Pallas kernels: 236 us -> 179 us
  waiting for transfers between devices: 81 us -> 112 us
  between operations: 14.5 us -> 0.86 us
  matrix products: 9.24 us -> 0 us
    pallas_call x5 -> x3, Pallas kernels: 73.7 us -> 38.2 us  [place(): pl.pallas_call(place_kernel, out_shape=jax.ShapeDtypeStruct((count, featu...]
    ppermute x35 -> x28, waiting for transfers between devices: 80.9 us -> 112 us  [exchange(): lax.ppermute(after(rows[k], *others), 'rows', [(i, i ^ k) for i in range(...]
    pallas_call x11 -> x3, Pallas kernels: 162 us -> 141 us  [the longest x1 104 us: first(): pl.pallas_call(functools.partial(first_kernel, count, chunks), out_shape=...]
    dot_general x2 -> x0, matrix products: 9.24 us -> none  [the longest x1 5.33 us: balanced(): jnp.einsum('kd,jd->kj', wide[0], up_b, preferred_element_type=jnp.float32)]
    all_to_all x0 -> x1, starting transfers between devices: none -> 4.89 us  [balanced(): lax.all_to_all(partial_value, 'cols', split_axis=0, concat_axis=0, tiled=...]
    ppermute x35 -> x28, starting transfers between devices: 31.7 us -> 29 us  [exchange(): lax.ppermute(after(rows[k], *others), 'rows', [(i, i ^ k) for i in range(...]
  transfers between devices with their start and end apart: 37 -> 29, of which waited for: 11 -> 7; matrix products, arithmetic and copies ran while one was open for 1% -> 1% of each run, Pallas kernels for 58% -> 22%
where the time goes in v2:
time: 338 us; the launch traced here: 336 us
  Pallas kernels  179 us (53%)
  waiting for transfers between devices  112 us (33%)
  starting transfers between devices  33.9 us (10%)
  local copies, waits for them, and re-layouts  8.71 us (3%)
    ppermute x28, waiting for transfers between devices, exchange(): lax.ppermute(after(rows[k], *others), 'rows', [(i, i ^ k) for i in range(...  112 us
    pallas_call x1, Pallas kernels, first(): pl.pallas_call(functools.partial(first_kernel, count, chunks), out_shape=...  104 us
    pallas_call x3, Pallas kernels, place(): pl.pallas_call(place_kernel, out_shape=jax.ShapeDtypeStruct((count, featu...  38.2 us
    pallas_call x2, Pallas kernels, place_rows(): pl.pallas_call(place_rows_kernel, out_shape=jax.ShapeDtypeStruct((count,...  36.8 us
    ppermute x28, starting transfers between devices, exchange(): lax.ppermute(after(rows[k], *others), 'rows', [(i, i ^ k) for i in range(...  29 us
  transfers between devices with their start and end apart: 29, of which 7 were waited for; matrix products, arithmetic and copies ran while one was open for 1% of the time, Pallas kernels for 22%

profile of v2, /device:TPU:0, one launch (start us, length us, event | category | flops | bytes accessed | tf_op | source)
XLA Modules:
  0.0 336.3 jit_solution(15500668843900183618)
XLA Ops:
  2.0 103.9 %shard_map.102 = (s32[32,128]{1,0:T(8,128)}, s32[32,128]{1,0:T(8,128)}, s32[8,32,128]{2,1,0:T(8,128)}, f32[4,8,8,3584]{3,2,1,0:T(8,128)}, bf16[8,448,1024]{2,1,0...) custom-call(s32[32,128]{1,0:T(8,128)} %pad.4.perm_ref, ...), custom_call_target="tpu_custom_call" | custom-call | tf_op jit(solution)/shard_map/pallas_call | solution.py:290
  105.9 4.9 %all-to-all-start = ((f32[4,8,8,3584]{3,2,1,0:T(8,128)}), f32[4,8,8,3584]{3,2,1,0:T(8,128)}, u32[]{:S(2)}, u32[]{:S(2)}) async-start(f32[4,8,8,3584]{3,2,1,0:T(8,128)} %get-tuple-element.71), calls=%async_computation | async-start | bytes 7340032 | tf_op jit(solution)/shard_map/all_to_all | solution.py:476
  110.8 18.5 %shard_map.103 = bf16[3584,1024]{1,0:T(8,128)(2,1)} custom-call(s32[4096]{0:T(1024)} %bitcast.14, bf16[3584,1024]{1,0:T(8,128)(2,1)} %initial_ref.5, bf16[8,448,1024]{2,1,0:T(8,128)(2,1)} %get-tuple-element.73.refs_0_.refs_1_.refs_2_.refs_3_.refs_4_.refs_5_.refs_6_.refs_7_, ...), custom_call_target="tpu_custom_call" | custom-call | bytes 22020096 | tf_op jit(solution)/shard_map/pallas_call | solution.py:432
  129.3 1.5 collective-permute-start.2
  133.6 29.0 %collective-permute-done.8.refs_2_ = bf16[448,512]{1,0:T(8,128)(2,1)S(1)} collective-permute-done((bf16[448,512]{1,0:T(8,128)(2,1)}, bf16[448,512]{1,0:T(8,128)(2,1)S(1)}, u32[]{:S(2)}, u32[]{:S(2)}) %collective-permute-start.8) | collective-permute-done | bytes 458784 | tf_op jit(solution)/shard_map/ppermute | solution.py:464
  162.6 1.5 collective-permute-start.3
  164.1 1.5 collective-permute-start.5
  165.6 16.6 %collective-permute-done.1.refs_2_ = bf16[448,1024]{1,0:T(8,128)(2,1)S(1)} collective-permute-done((bf16[448,1024]{1,0:T(8,128)(2,1)}, bf16[448,1024]{1,0:T(8,128)(2,1)S(1)}, u32[]{:S(2)}, u32[]{:S(2)}) %collective-permute-start.1) | collective-permute-done | bytes 917536 | tf_op jit(solution)/shard_map/ppermute | solution.py:464
  183.9 41.1 %collective-permute-done.3.refs_4_ = bf16[448,1024]{1,0:T(8,128)(2,1)} collective-permute-done((bf16[448,1024]{1,0:T(8,128)(2,1)}, bf16[448,1024]{1,0:T(8,128)(2,1)}, u32[]{:S(2)}, u32[]{:S(2)}) %collective-permute-start.3) | collective-permute-done | bytes 917536 | tf_op jit(solution)/shard_map/ppermute | solution.py:464
  225.0 2.6 collective-permute-start.12
  227.6 1.8 collective-permute-start.13
  229.4 18.3 %shard_map.104 = bf16[3584,1024]{1,0:T(8,128)(2,1)} custom-call(s32[4096]{0:T(1024)} %bitcast.15, bf16[3584,1024]{1,0:T(8,128)(2,1)} %initial_ref.6, bf16[448,1024]{1,0:T(8,128)(2,1)} %get-tuple-element.74.refs_0_, bf16[448,1024]{1,0:T(8,128)(2,1)} %copy-done, bf16[448,1024]{1,0:T(8,128)(2,1)} %copy-done.2, bf16[448,1024]{1,0:T(8,128)(2,1)} %copy-done.1, ...), custom_call_target="tpu_custom_call" | custom-call | bytes 22020096 | tf_op jit(solution)/shard_map/pallas_call | solution.py:432
  247.8 6.7 %collective-permute-done.10.refs_4_ = bf16[448,512]{1,0:T(8,128)(2,1)} collective-permute-done((bf16[448,512]{1,0:T(8,128)(2,1)}, bf16[448,512]{1,0:T(8,128)(2,1)}, u32[]{:S(2)}, u32[]{:S(2)}) %collective-permute-start.10) | collective-permute-done | bytes 458784 | tf_op jit(solution)/shard_map/ppermute | solution.py:464
  254.5 1.9 collective-permute-start.15
  256.3 5.6 %collective-permute-done.11.refs_5_ = bf16[448,512]{1,0:T(8,128)(2,1)} collective-permute-done((bf16[448,512]{1,0:T(8,128)(2,1)}, bf16[448,512]{1,0:T(8,128)(2,1)}, u32[]{:S(2)}, u32[]{:S(2)}) %collective-permute-start.11) | collective-permute-done | bytes 458784 | tf_op jit(solution)/shard_map/ppermute | solution.py:464
  262.0 1.9 collective-permute-start.16
  266.2 2.1 collective-permute-start.20
  269.6 1.5 collective-permute-start.21
  271.1 11.3 %collective-permute-done.17.refs_5_ = bf16[448,256]{1,0:T(8,128)(2,1)S(1)} collective-permute-done((bf16[448,256]{1,0:T(8,128)(2,1)}, bf16[448,256]{1,0:T(8,128)(2,1)S(1)}, u32[]{:S(2)}, u32[]{:S(2)}) %collective-permute-start.17) | collective-permute-done | bytes 229408 | tf_op jit(solution)/shard_map/ppermute | solution.py:464
  290.8 2.5 broadcast_in_dim.9.code_ref
  293.4 13.9 %shard_map.105.refs_0_ = bf16[3584,1024]{1,0:T(8,128)(2,1)} custom-call(s32[256]{0:T(256)} %reshape_squeeze.3.before_ref, s32[3584,128]{1,0:T(8,128)} %broadcast_in_dim.9.code_ref, bf16[3584,1024]{1,0:T(8,128)(2,1)} %initial_ref.9, bf16[448,512]{1,0:T(8,128)(2,1)} %get-tuple-element.81.refs_0_, bf16[448,512]{1,0:T(8,128)(2,1)} %copy-done.4, ...), custom_call_target="tpu_custom_call" | custom-call | flops 1879048192 | bytes 11010048 | tf_op jit(solution)/shard_map/pallas_call | solution.py:376
  307.3 12.1 %shard_map.106.refs_0_ = bf16[3584,1024]{1,0:T(8,128)(2,1)} custom-call(s32[256]{0:T(256)} %reshape_squeeze.3.before_ref, s32[3584,128]{1,0:T(8,128)} %broadcast_in_dim.9.code_ref, bf16[3584,1024]{1,0:T(8,128)(2,1)} %initial_ref.9, bf16[3584,1024]{1,0:T(8,128)(2,1)} %shard_map.105.refs_0_, ...), custom_call_target="tpu_custom_call", output_to_operand_aliasing={{}: (3, {})} | custom-call | flops 939524096 | bytes 5505024 | tf_op jit(solution)/shard_map/pallas_call | solution.py:376
  320.5 12.1 %shard_map.107 = bf16[3584,1024]{1,0:T(8,128)(2,1)} custom-call(s32[256]{0:T(256)} %reshape_squeeze.3.before_ref, s32[3584,128]{1,0:T(8,128)} %broadcast_in_dim.9.code_ref, bf16[3584,1024]{1,0:T(8,128)(2,1)} %initial_ref.9, bf16[3584,1024]{1,0:T(8,128)(2,1)} %shard_map.106.refs_0_, ...), custom_call_target="tpu_custom_call", output_to_operand_aliasing={{}: (3, {})} | custom-call | flops 939524096 | bytes 5505024 | tf_op jit(solution)/shard_map/pallas_call | solution.py:376
  332.6 2.2 fusion.2
  (89 shorter events, 20.3 us)
Async XLA Ops:
  105.9 226.7 %all-to-all-start = ((f32[4,8,8,3584]{3,2,1,0:T(8,128)}), f32[4,8,8,3584]{3,2,1,0:T(8,128)}, u32[]{:S(2)}, u32[]{:S(2)}) async-start(f32[4,8,8,3584]{3,2,1,0:T(8,128)} %get-tuple-element.71), calls=%async_computation | async-start | bytes 7340032 | tf_op jit(solution)/shard_map/all_to_all | solution.py:476
  129.2 34.9 %collective-permute-start = (bf16[448,1024]{1,0:T(8,128)(2,1)}, bf16[448,1024]{1,0:T(8,128)(2,1)S(1)}, u32[]{:S(2)}, u32[]{:S(2)}) collective-permute-start(bf16[448,1024]{1,0:T(8,128)(2,1)} %get-tuple-element.76), channel_id=1, source_target_pairs={{0,4},{4,0},{8,12},{12,8},{16,20},{20,16},{24,28},{28,24},{1,5},{5... | collective-permute-start | bytes 2752520 | tf_op jit(solution)/shard_map/ppermute | solution.py:464
  129.3 34.8 %collective-permute-start.2 = (bf16[448,1024]{1,0:T(8,128)(2,1)}, bf16[448,1024]{1,0:T(8,128)(2,1)S(1)}, u32[]{:S(2)}, u32[]{:S(2)}) collective-permute-start(bf16[448,1024]{1,0:T(8,128)(2,1)} %get-tuple-element.78), channel_id=1, source_target_pairs={{0,12},{4,8},{8,4},{12,0},{16,28},{20,24},{24,20},{28,16},{1,13},{... | collective-permute-start | bytes 2752520 | tf_op jit(solution)/shard_map/ppermute | solution.py:464
  131.0 31.6 %collective-permute-start.8 = (bf16[448,512]{1,0:T(8,128)(2,1)}, bf16[448,512]{1,0:T(8,128)(2,1)S(1)}, u32[]{:S(2)}, u32[]{:S(2)}) collective-permute-start(bf16[448,512]{1,0:T(8,128)(2,1)} %get-tuple-element.85), channel_id=1, source_target_pairs={{0,8},{4,12},{8,0},{12,4},{16,24},{20,28},{24,16},{28,20},{1,9},{5... | collective-permute-start | bytes 1376264 | tf_op jit(solution)/shard_map/ppermute | solution.py:464
  131.5 50.8 %collective-permute-start.1 = (bf16[448,1024]{1,0:T(8,128)(2,1)}, bf16[448,1024]{1,0:T(8,128)(2,1)S(1)}, u32[]{:S(2)}, u32[]{:S(2)}) collective-permute-start(bf16[448,1024]{1,0:T(8,128)(2,1)} %get-tuple-element.70), channel_id=1, source_target_pairs={{0,8},{4,12},{8,0},{12,4},{16,24},{20,28},{24,16},{28,20},{1,9},{5... | collective-permute-start | bytes 2752520 | tf_op jit(solution)/shard_map/ppermute | solution.py:464
  133.0 49.5 %collective-permute-start.4 = (bf16[448,1024]{1,0:T(8,128)(2,1)}, bf16[448,1024]{1,0:T(8,128)(2,1)S(1)}, u32[]{:S(2)}, u32[]{:S(2)}) collective-permute-start(bf16[448,1024]{1,0:T(8,128)(2,1)} %get-tuple-element.69), channel_id=1, source_target_pairs={{0,20},{4,16},{8,28},{12,24},{16,4},{20,0},{24,12},{28,8},{1,21},{... | collective-permute-start | bytes 2752520 | tf_op jit(solution)/shard_map/ppermute | solution.py:464
  162.6 62.4 %collective-permute-start.3 = (bf16[448,1024]{1,0:T(8,128)(2,1)}, bf16[448,1024]{1,0:T(8,128)(2,1)}, u32[]{:S(2)}, u32[]{:S(2)}) collective-permute-start(bf16[448,1024]{1,0:T(8,128)(2,1)} %get-tuple-element.68), channel_id=1, source_target_pairs={{0,16},{4,20},{8,24},{12,28},{16,0},{20,4},{24,8},{28,12},{1,17},{... | collective-permute-start | bytes 2752520 | tf_op jit(solution)/shard_map/ppermute | solution.py:464
  164.1 60.9 %collective-permute-start.6 = (bf16[448,1024]{1,0:T(8,128)(2,1)}, bf16[448,1024]{1,0:T(8,128)(2,1)}, u32[]{:S(2)}, u32[]{:S(2)}) collective-permute-start(bf16[448,1024]{1,0:T(8,128)(2,1)} %get-tuple-element.67), channel_id=1, source_target_pairs={{0,28},{4,24},{8,20},{12,16},{16,12},{20,8},{24,4},{28,0},{1,29},{... | collective-permute-start | bytes 2752520 | tf_op jit(solution)/shard_map/ppermute | solution.py:464
  164.1 63.4 %collective-permute-start.5 = (bf16[448,1024]{1,0:T(8,128)(2,1)}, bf16[448,1024]{1,0:T(8,128)(2,1)}, u32[]{:S(2)}, u32[]{:S(2)}) collective-permute-start(bf16[448,1024]{1,0:T(8,128)(2,1)} %get-tuple-element.66), channel_id=1, source_target_pairs={{0,24},{4,28},{8,16},{12,20},{16,8},{20,12},{24,0},{28,4},{1,25},{... | collective-permute-start | bytes 2752520 | tf_op jit(solution)/shard_map/ppermute | solution.py:464
  182.3 65.5 %collective-permute-start.9 = (bf16[448,512]{1,0:T(8,128)(2,1)}, bf16[448,512]{1,0:T(8,128)(2,1)}, u32[]{:S(2)}, u32[]{:S(2)}) collective-permute-start(bf16[448,512]{1,0:T(8,128)(2,1)} %get-tuple-element.87), channel_id=1, source_target_pairs={{0,12},{4,8},{8,4},{12,0},{16,28},{20,24},{24,20},{28,16},{1,13},{... | collective-permute-start | bytes 1376264 | tf_op jit(solution)/shard_map/ppermute | solution.py:464
  182.5 72.0 %collective-permute-start.10 = (bf16[448,512]{1,0:T(8,128)(2,1)}, bf16[448,512]{1,0:T(8,128)(2,1)}, u32[]{:S(2)}, u32[]{:S(2)}) collective-permute-start(bf16[448,512]{1,0:T(8,128)(2,1)} %get-tuple-element.89), channel_id=1, source_target_pairs={{0,16},{4,20},{8,24},{12,28},{16,0},{20,4},{24,8},{28,12},{1,17},{... | collective-permute-start | bytes 1376264 | tf_op jit(solution)/shard_map/ppermute | solution.py:464
  225.0 37.0 %collective-permute-start.11 = (bf16[448,512]{1,0:T(8,128)(2,1)}, bf16[448,512]{1,0:T(8,128)(2,1)}, u32[]{:S(2)}, u32[]{:S(2)}) collective-permute-start(bf16[448,512]{1,0:T(8,128)(2,1)} %get-tuple-element.91), channel_id=1, source_target_pairs={{0,20},{4,16},{8,28},{12,24},{16,4},{20,0},{24,12},{28,8},{1,21},{... | collective-permute-start | bytes 1376264 | tf_op jit(solution)/shard_map/ppermute | solution.py:464
  225.0 38.9 %collective-permute-start.12 = (bf16[448,512]{1,0:T(8,128)(2,1)}, bf16[448,512]{1,0:T(8,128)(2,1)}, u32[]{:S(2)}, u32[]{:S(2)}) collective-permute-start(bf16[448,512]{1,0:T(8,128)(2,1)} %get-tuple-element.93), channel_id=1, source_target_pairs={{0,24},{4,28},{8,16},{12,20},{16,8},{20,12},{24,0},{28,4},{1,25},{... | collective-permute-start | bytes 1376264 | tf_op jit(solution)/shard_map/ppermute | solution.py:464
  227.6 37.4 %collective-permute-start.13 = (bf16[448,512]{1,0:T(8,128)(2,1)}, bf16[448,512]{1,0:T(8,128)(2,1)}, u32[]{:S(2)}, u32[]{:S(2)}) collective-permute-start(bf16[448,512]{1,0:T(8,128)(2,1)} %get-tuple-element.95), channel_id=1, source_target_pairs={{0,28},{4,24},{8,20},{12,16},{16,12},{20,8},{24,4},{28,0},{1,29},{... | collective-permute-start | bytes 1376264 | tf_op jit(solution)/shard_map/ppermute | solution.py:464
  263.8 18.6 %collective-permute-start.17 = (bf16[448,256]{1,0:T(8,128)(2,1)}, bf16[448,256]{1,0:T(8,128)(2,1)S(1)}, u32[]{:S(2)}, u32[]{:S(2)}) collective-permute-start(bf16[448,256]{1,0:T(8,128)(2,1)} %get-tuple-element.104), channel_id=1, source_target_pairs={{0,16},{4,20},{8,24},{12,28},{16,0},{20,4},{24,8},{28,12},{1,17},{... | collective-permute-start | bytes 688136 | tf_op jit(solution)/shard_map/ppermute | solution.py:464
  265.0 20.3 %collective-permute-start.18 = (bf16[448,256]{1,0:T(8,128)(2,1)}, bf16[448,256]{1,0:T(8,128)(2,1)S(1)}, u32[]{:S(2)}, u32[]{:S(2)}) collective-permute-start(bf16[448,256]{1,0:T(8,128)(2,1)} %get-tuple-element.106), channel_id=1, source_target_pairs={{0,20},{4,16},{8,28},{12,24},{16,4},{20,0},{24,12},{28,8},{1,21},{... | collective-permute-start | bytes 688136 | tf_op jit(solution)/shard_map/ppermute | solution.py:464
  265.0 21.4 %collective-permute-start.19 = (bf16[448,256]{1,0:T(8,128)(2,1)}, bf16[448,256]{1,0:T(8,128)(2,1)S(1)}, u32[]{:S(2)}, u32[]{:S(2)}) collective-permute-start(bf16[448,256]{1,0:T(8,128)(2,1)} %get-tuple-element.108), channel_id=1, source_target_pairs={{0,24},{4,28},{8,16},{12,20},{16,8},{20,12},{24,0},{28,4},{1,25},{... | collective-permute-start | bytes 688136 | tf_op jit(solution)/shard_map/ppermute | solution.py:464
  266.2 21.1 %collective-permute-start.20 = (bf16[448,256]{1,0:T(8,128)(2,1)}, bf16[448,256]{1,0:T(8,128)(2,1)S(1)}, u32[]{:S(2)}, u32[]{:S(2)}) collective-permute-start(bf16[448,256]{1,0:T(8,128)(2,1)} %get-tuple-element.110), channel_id=1, source_target_pairs={{0,28},{4,24},{8,20},{12,16},{16,12},{20,8},{24,4},{28,0},{1,29},{... | collective-permute-start | bytes 688136 | tf_op jit(solution)/shard_map/ppermute | solution.py:464
  269.6 18.8 %collective-permute-start.21 = (bf16[448,256]{1,0:T(8,128)(2,1)}, bf16[448,256]{1,0:T(8,128)(2,1)S(1)}, u32[]{:S(2)}, u32[]{:S(2)}) collective-permute-start(bf16[448,256]{1,0:T(8,128)(2,1)} %get-tuple-element.113), channel_id=1, source_target_pairs={{0,4},{4,0},{8,12},{12,8},{16,20},{20,16},{24,28},{28,24},{1,5},{5... | collective-permute-start | bytes 688136 | tf_op jit(solution)/shard_map/ppermute | solution.py:464
  285.2 34.2 %collective-permute-start.23 = (bf16[448,256]{1,0:T(8,128)(2,1)}, bf16[448,256]{1,0:T(8,128)(2,1)S(1)}, u32[]{:S(2)}, u32[]{:S(2)}) collective-permute-start(bf16[448,256]{1,0:T(8,128)(2,1)} %get-tuple-element.117), channel_id=1, source_target_pairs={{0,12},{4,8},{8,4},{12,0},{16,28},{20,24},{24,20},{28,16},{1,13},{... | collective-permute-start | bytes 688136 | tf_op jit(solution)/shard_map/ppermute | solution.py:464
  286.4 33.1 %collective-permute-start.24 = (bf16[448,256]{1,0:T(8,128)(2,1)}, bf16[448,256]{1,0:T(8,128)(2,1)S(1)}, u32[]{:S(2)}, u32[]{:S(2)}) collective-permute-start(bf16[448,256]{1,0:T(8,128)(2,1)} %get-tuple-element.119), channel_id=1, source_target_pairs={{0,16},{4,20},{8,24},{12,28},{16,0},{20,4},{24,8},{28,12},{1,17},{... | collective-permute-start | bytes 688136 | tf_op jit(solution)/shard_map/ppermute | solution.py:464
  287.3 32.2 %collective-permute-start.25 = (bf16[448,256]{1,0:T(8,128)(2,1)}, bf16[448,256]{1,0:T(8,128)(2,1)S(1)}, u32[]{:S(2)}, u32[]{:S(2)}) collective-permute-start(bf16[448,256]{1,0:T(8,128)(2,1)} %get-tuple-element.121), channel_id=1, source_target_pairs={{0,20},{4,16},{8,28},{12,24},{16,4},{20,0},{24,12},{28,8},{1,21},{... | collective-permute-start | bytes 688136 | tf_op jit(solution)/shard_map/ppermute | solution.py:464
  288.4 31.2 %collective-permute-start.26 = (bf16[448,256]{1,0:T(8,128)(2,1)}, bf16[448,256]{1,0:T(8,128)(2,1)S(1)}, u32[]{:S(2)}, u32[]{:S(2)}) collective-permute-start(bf16[448,256]{1,0:T(8,128)(2,1)} %get-tuple-element.123), channel_id=1, source_target_pairs={{0,24},{4,28},{8,16},{12,20},{16,8},{20,12},{24,0},{28,4},{1,25},{... | collective-permute-start | bytes 688136 | tf_op jit(solution)/shard_map/ppermute | solution.py:464
  289.9 29.7 %collective-permute-start.27 = (bf16[448,256]{1,0:T(8,128)(2,1)}, bf16[448,256]{1,0:T(8,128)(2,1)S(1)}, u32[]{:S(2)}, u32[]{:S(2)}) collective-permute-start(bf16[448,256]{1,0:T(8,128)(2,1)} %get-tuple-element.125), channel_id=1, source_target_pairs={{0,28},{4,24},{8,20},{12,16},{16,12},{20,8},{24,4},{28,0},{1,29},{... | collective-permute-start | bytes 688136 | tf_op jit(solution)/shard_map/ppermute | solution.py:464
  (26 other events, 720.5 us)

commit v3 on v2

--- a/solution.py
+++ b/solution.py
@@ -15,6 +15,10 @@
 LANES = 128
 TILE = 256
 SLOT = 64
+ORDER = (6, 7, 4, 5, 2, 3, 1)
+AHEAD = 5
+TALL = 512
+ROWS = 32
 COST_ROWS = 512
 OVER_LANES = (((1,), (1,)), ((), ()))
 CODE = 1024
@@ -54,7 +58,7 @@
         rank = rank + ranked[k * pad : (k + 1) * pad]
     rank = rank.astype(jnp.int32)
     code_ref[...] = (source ^ me) * CODE + rank
-    slot_ref[...] = jnp.minimum((source ^ me) * slots + rank, count - 1)
+    slot_ref[...] = first_of(jnp.minimum((source ^ me) * slots + rank, count - 1), 8)
     for k in range(PEERS):
         before_ref[k] = counts[pl.ds(pl.multiple_of((me ^ k) * pad, pad), pad), :]
 
@@ -91,13 +95,18 @@
     lax.fori_loop(0, tall // 16, step, 0)
 
 
-def sixteen(index_of, spread, turn, tiles):
-    for s in range(16):
-        i = index_of(s)
-        begin = lax.shift_right_logical(i, 3) * (8 * tiles) + (i & 7)
-        turn[pl.ds((s // 8) * 8 * tiles + s % 8, tiles, stride=8), :] = spread[pl.ds(begin, tiles, stride=8), :]
-    for c in range(tiles):
-        yield c, jnp.concatenate([turn[(h * tiles + c) * 8 : (h * tiles + c + 1) * 8, :] for h in range(2)], axis=0)
+def first_of(row, tiles):
+    return lax.shift_right_logical(row, 3) * (8 * tiles) + (row & 7)
+
+
+def rows_of(begin_of, spread, turn, tiles):
+    for s in range(ROWS):
+        to = (s // 8) * 8 * tiles + s % 8
+        turn[pl.ds(to, tiles, stride=8), :] = spread[pl.ds(begin_of(s), tiles, stride=8), :]
+    for h in range(ROWS // 16):
+        for c in range(tiles):
+            both = [turn[pl.ds(((2 * h + half) * tiles + c) * 8, 8), :] for half in range(2)]
+            yield h * 16, c, jnp.concatenate(both, axis=0)
 
 
 def first_kernel(count, chunks, perm_ref, up_a, gate_a, up_b, gate_b, down_b, code_ref, slot_ref, before_ref, partial_ref, up_moved, up_sent, *refs):
@@ -156,20 +165,19 @@
     own.wait()
     for copy in asks:
         copy.wait()
-    got[...] = jnp.clip(got[...], 0, count - 1)
+    got[...] = first_of(jnp.clip(got[...], 0, count - 1), 8)
     own = pltpu.make_async_copy(got, asked, own_sem)
     own.start()
     own.wait()
 
     def gather(k, buffer):
         def step(t, carry):
-            for c, tile in sixteen(lambda s: asked[k, 0, t * 16 + s], spread, turn, 8):
-                stage[buffer, pl.ds(pl.multiple_of(t * 16, 16), 16), c * LANES : (c + 1) * LANES] = tile.astype(
-                    jnp.bfloat16
-                )
+            for row, c, tile in rows_of(lambda s: asked[k, 0, t * ROWS + s], spread, turn, 8):
+                at = pl.ds(pl.multiple_of(t * ROWS + row, 16), 16)
+                stage[buffer, at, c * LANES : (c + 1) * LANES] = tile.astype(jnp.bfloat16)
             return carry
 
-        lax.fori_loop(0, slots // 16, step, 0)
+        lax.fori_loop(0, slots // ROWS, step, 0)
 
     def up_step(n, carry):
         k = n ^ 6
@@ -305,7 +313,7 @@
             pltpu.VMEM((2, A_DEV * PEERS, features), bf16),
             pltpu.VMEM((2, count, features), bf16),
             pltpu.VMEM((count * 8 + 8 * 8, LANES), f32),
-            pltpu.VMEM((LANES + 8 * 8, LANES), f32),
+            pltpu.VMEM(((ROWS + 8) * 8, LANES), f32),
             pltpu.VMEM((2, slots, features), bf16),
             pltpu.VMEM((cols, PEERS, A_DEV // cols, count), f32),
         ]
@@ -411,13 +419,13 @@
             spread_out(arrived[k], spread, k * arrived[k].shape[0] * tiles)
 
     def step(j, carry):
-        at = pl.ds(pl.multiple_of(j * 16, 16), 16)
-        for c, tile in sixteen(lambda s: slot_ref[t * tall + j * 16 + s], spread, turn, tiles):
+        for row, c, tile in rows_of(lambda s: slot_ref[t * tall + j * ROWS + s], spread, turn, tiles):
+            at = pl.ds(pl.multiple_of(j * ROWS + row, 16), 16)
             lanes = slice(c * LANES, (c + 1) * LANES)
             out_ref[at, lanes] = ((initial_ref[at, lanes].astype(jnp.float32) + tile) * 0.5).astype(out_ref.dtype)
         return carry
 
-    lax.fori_loop(0, tall // 16, step, 0)
+    lax.fori_loop(0, tall // ROWS, step, 0)
 
 
 def place_rows(slot, initial, arrived):
@@ -428,7 +436,7 @@
     else:
         specs = [pl.BlockSpec((None, slots, features), functools.partial(lambda k, t, *_: (k, 0, 0), k)) for k in range(PEERS)]
         arrived = [arrived] * PEERS
-    tall = count // 7 if count % (7 * 16) == 0 else LANES
+    tall = TALL
     return pl.pallas_call(
         place_rows_kernel,
         out_shape=jax.ShapeDtypeStruct((count, features), initial.dtype),
@@ -439,7 +447,7 @@
             out_specs=pl.BlockSpec((tall, features), lambda t, *_: (t, 0)),
             scratch_shapes=[
                 pltpu.VMEM(((count + 8) * features // LANES, LANES), jnp.float32),
-                pltpu.VMEM(((16 + 8) * features // LANES, LANES), jnp.float32),
+                pltpu.VMEM(((ROWS + 8) * features // LANES, LANES), jnp.float32),
             ],
         ),
         compiler_params=pltpu.CompilerParams(vmem_limit_bytes=60 * 1024 * 1024),
@@ -459,32 +467,38 @@
     def after(value, *others):
         return lax.optimization_barrier((value,) + others)[0]
 
-    def exchange(rows, ks, *others):
-        return {
-            k: lax.ppermute(after(rows[k], *others), "rows", [(i, i ^ k) for i in range(PEERS)]) for k in ks
-        }
-
-    def parts(rows, *moved):
-        got = {0: rows[0]}
-        for some in moved:
-            got.update(some)
+    gate, down = lists[0], lists[1:]
+    arrived = []
+
+    def travel(rows, ks, *others):
+        for k in ks:
+            before_it = arrived[-AHEAD:][:1] if len(arrived) >= AHEAD else []
+            sent = after(rows[k], *before_it, *others)
+            arrived.append(lax.ppermute(sent, "rows", [(i, i ^ k) for i in range(PEERS)]))
+
+    def taken(rows, at):
+        got = {0: rows[0], **dict(zip(ORDER, arrived[at : at + len(ORDER)]))}
         return [got[k] for k in range(PEERS)]
 
-    gate, down = lists[0], lists[1:]
-    gate_first = exchange(gate, (6, 7, 4, 5, 2))
-    partial_value = after(partial_value, *(gate[k] for k in (6, 7, 4, 5, 2)))
-    shares = lax.all_to_all(partial_value, "cols", split_axis=0, concat_axis=0, tiled=True)
-    up_mean = place_rows(slot, up_a, up_moved)
-    gate_last = exchange(gate, (3, 1), up_mean)
-    left = exchange(down[0], (6, 7, 4, 5, 2, 3, 1), up_mean)
-    gate_mean = place_rows(slot, gate_a, parts(gate, gate_first, gate_last))
-    middle = exchange(down[1], (6, 7, 4, 5, 2, 3, 1), gate_mean)
-    right = exchange(down[2], (6, 7, 4, 5, 2, 3, 1), gate_mean)
-    down_mean = place(before, code, down_a, parts(down[0], left), 0)
-    down_mean = place(before, code, down_a, parts(down[1], middle), chunks[0], down_mean)
-    down_mean = place(before, code, down_a, parts(down[2], right), chunks[0] + chunks[1], down_mean)
+    travel(gate, ORDER)
+    shares = lax.all_to_all(after(partial_value, arrived[2]), "cols", split_axis=0, concat_axis=0, tiled=True)
+    up_mean = place_rows(after(slot, arrived[2]), up_a, up_moved)
+    travel(down[0], ORDER[:1], up_mean)
+    travel(down[0], ORDER[1:AHEAD])
+    gate_mean = place_rows(slot, gate_a, taken(gate, 0))
+    travel(down[0], ORDER[AHEAD : AHEAD + 1], gate_mean)
+    travel(down[0], ORDER[AHEAD + 1 :])
+    travel(down[1], ORDER[:AHEAD])
+    down_mean = place(before, code, down_a, taken(down[0], 7), 0)
     total = (shares[0] + shares[1]) + (shares[2] + shares[3])
     costs = (total.transpose(1, 0, 2).reshape(-1, row_count) * cost_scale).T
+    travel(down[1], ORDER[AHEAD : AHEAD + 1], down_mean)
+    travel(down[1], ORDER[AHEAD + 1 :])
+    travel(down[2], ORDER[:AHEAD])
+    down_mean = place(before, code, down_a, taken(down[1], 14), chunks[0], down_mean)
+    travel(down[2], ORDER[AHEAD : AHEAD + 1], down_mean, costs)
+    travel(down[2], ORDER[AHEAD + 1 :])
+    down_mean = place(before, code, down_a, taken(down[2], 21), chunks[0] + chunks[1], down_mean)
     return (costs, up_mean, gate_mean, down_mean)
 
 
@@ -550,7 +564,8 @@
     def local(up_a, *rest):
         row_count, features = up_a.shape
         even = mesh.shape["rows"] == PEERS and row_count % (PEERS * 16) == 0 and row_count % (A_DEV * 16) == 0
-        even = even and row_count % COST_ROWS == 0 and SLOT <= row_count // PEERS < CODE
+        even = even and row_count % COST_ROWS == 0 and row_count % TALL == 0 and row_count % (PEERS * ROWS) == 0
+        even = even and SLOT <= row_count // PEERS < CODE
         even = even and features == 8 * LANES and mesh.shape["cols"] == A_DEV // 8
         return (balanced if even else general)(up_a, *rest)
 

time: 338 us -> 325 us (0.962)
  waiting for transfers between devices: 112 us -> 103 us
  Pallas kernels: 179 us -> 175 us
    ppermute x28, waiting for transfers between devices: 112 us -> 103 us  [travel(): lax.ppermute(sent, 'rows', [(i, i ^ k) for i in range(PEERS)])]
    pallas_call x2, Pallas kernels: 36.8 us -> 33 us  [place_rows(): pl.pallas_call(place_rows_kernel, out_shape=jax.ShapeDtypeStruct((count,...]
  transfers between devices with their start and end apart: 29 -> 29, of which waited for: 7 -> 10; matrix products, arithmetic and copies ran while one was open for 1% -> 2% of each run, Pallas kernels for 22% -> 18%
where the time goes in v3:
time: 325 us; the launch traced here: 323 us
  Pallas kernels  175 us (54%)
  waiting for transfers between devices  103 us (32%)
  starting transfers between devices  35.8 us (11%)
  local copies, waits for them, and re-layouts  6.89 us (2%)
    pallas_call x1, Pallas kernels, first(): pl.pallas_call(functools.partial(first_kernel, count, chunks), out_shape=...  103 us
    ppermute x28, waiting for transfers between devices, travel(): lax.ppermute(sent, 'rows', [(i, i ^ k) for i in range(PEERS)])  103 us
    pallas_call x3, Pallas kernels, place(): pl.pallas_call(place_kernel, out_shape=jax.ShapeDtypeStruct((count, featu...  38.3 us
    pallas_call x2, Pallas kernels, place_rows(): pl.pallas_call(place_rows_kernel, out_shape=jax.ShapeDtypeStruct((count,...  33 us
    ppermute x28, starting transfers between devices, travel(): lax.ppermute(sent, 'rows', [(i, i ^ k) for i in range(PEERS)])  31 us
  transfers between devices with their start and end apart: 29, of which 10 were waited for; matrix products, arithmetic and copies ran while one was open for 2% of the time, Pallas kernels for 18%

profile of v3, /device:TPU:0, one launch (start us, length us, event | category | flops | bytes accessed | tf_op | source)
XLA Modules:
  0.0 323.4 jit_solution(3001088569444150928)
XLA Ops:
  2.0 103.4 %shard_map.102 = (s32[32,128]{1,0:T(8,128)}, s32[32,128]{1,0:T(8,128)}, s32[8,32,128]{2,1,0:T(8,128)}, f32[4,8,8,3584]{3,2,1,0:T(8,128)}, bf16[8,448,1024]{2,1,0...) custom-call(s32[32,128]{1,0:T(8,128)} %pad.4.perm_ref, ...), custom_call_target="tpu_custom_call" | custom-call | tf_op jit(solution)/shard_map/pallas_call | solution.py:298
  106.9 21.1 %collective-permute-done.refs_4_ = bf16[448,1024]{1,0:T(8,128)(2,1)S(1)} collective-permute-done((bf16[448,1024]{1,0:T(8,128)(2,1)}, bf16[448,1024]{1,0:T(8,128)(2,1)S(1)}, u32[]{:S(2)}, u32[]{:S(2)}) %collective-permute-start) | collective-permute-done | bytes 917536 | tf_op jit(solution)/shard_map/ppermute | solution.py:477
  128.0 4.9 %all-to-all-start = ((f32[4,8,8,3584]{3,2,1,0:T(8,128)}), f32[4,8,8,3584]{3,2,1,0:T(8,128)}, u32[]{:S(2)}, u32[]{:S(2)}) async-start(f32[4,8,8,3584]{3,2,1,0:T(8,128)} %get-tuple-element.68), calls=%async_computation | async-start | bytes 7340032 | tf_op jit(solution)/shard_map/all_to_all | solution.py:484
  132.9 2.0 collective-permute-start.4
  134.9 2.1 collective-permute-start.6
  138.1 19.2 %collective-permute-done.4.refs_6_ = bf16[448,1024]{1,0:T(8,128)(2,1)S(1)} collective-permute-done((bf16[448,1024]{1,0:T(8,128)(2,1)}, bf16[448,1024]{1,0:T(8,128)(2,1)S(1)}, u32[]{:S(2)}, u32[]{:S(2)}) %collective-permute-start.4) | collective-permute-done | bytes 917536 | tf_op jit(solution)/shard_map/ppermute | solution.py:477
  157.4 18.4 %collective-permute-done.1.refs_7_ = bf16[448,1024]{1,0:T(8,128)(2,1)S(1)} collective-permute-done((bf16[448,1024]{1,0:T(8,128)(2,1)}, bf16[448,1024]{1,0:T(8,128)(2,1)S(1)}, u32[]{:S(2)}, u32[]{:S(2)}) %collective-permute-start.1) | collective-permute-done | bytes 917536 | tf_op jit(solution)/shard_map/ppermute | solution.py:477
  176.8 16.5 %shard_map.103 = bf16[3584,1024]{1,0:T(8,128)(2,1)} custom-call(s32[4096]{0:T(1024)} %bitcast.14, bf16[3584,1024]{1,0:T(8,128)(2,1)} %initial_ref.5, bf16[8,448,1024]{2,1,0:T(8,128)(2,1)} %get-tuple-element.71.refs_0_.refs_1_.refs_2_.refs_3_.refs_4_.refs_5_.refs_6_.refs_7_, ...), custom_call_target="tpu_custom_call" | custom-call | bytes 22020096 | tf_op jit(solution)/shard_map/pallas_call | solution.py:440
  193.3 2.1 collective-permute-start.10
  197.6 17.5 %collective-permute-done.5.refs_3_ = bf16[448,1024]{1,0:T(8,128)(2,1)} collective-permute-done((bf16[448,1024]{1,0:T(8,128)(2,1)}, bf16[448,1024]{1,0:T(8,128)(2,1)}, u32[]{:S(2)}, u32[]{:S(2)}) %collective-permute-start.5) | collective-permute-done | bytes 917536 | tf_op jit(solution)/shard_map/ppermute | solution.py:477
  216.4 16.5 %shard_map.104 = bf16[3584,1024]{1,0:T(8,128)(2,1)} custom-call(s32[4096]{0:T(1024)} %bitcast.15, bf16[3584,1024]{1,0:T(8,128)(2,1)} %initial_ref.6, bf16[448,1024]{1,0:T(8,128)(2,1)} %get-tuple-element.72.refs_0_, bf16[448,1024]{1,0:T(8,128)(2,1)} %collective-permute-done.2.refs_1_, bf16[448,1024]{1,0:T(8,128)(2,1)} %collective-permute-done.3.refs_2_, ...), custom_call_target="tpu_custom_call" | custom-call | bytes 22020096 | tf_op jit(solution)/shard_map/pallas_call | solution.py:440
  235.6 1.6 collective-permute-start.17
  237.3 6.7 %collective-permute-done.13.refs_5_ = bf16[448,512]{1,0:T(8,128)(2,1)S(1)} collective-permute-done((bf16[448,512]{1,0:T(8,128)(2,1)}, bf16[448,512]{1,0:T(8,128)(2,1)S(1)}, u32[]{:S(2)}, u32[]{:S(2)}) %collective-permute-start.13) | collective-permute-done | bytes 458784 | tf_op jit(solution)/shard_map/ppermute | solution.py:477
  243.9 1.9 collective-permute-start.14
  248.5 7.6 %collective-permute-done.9.refs_2_ = bf16[448,512]{1,0:T(8,128)(2,1)S(1)} collective-permute-done((bf16[448,512]{1,0:T(8,128)(2,1)}, bf16[448,512]{1,0:T(8,128)(2,1)S(1)}, u32[]{:S(2)}, u32[]{:S(2)}) %collective-permute-start.9) | collective-permute-done | bytes 458784 | tf_op jit(solution)/shard_map/ppermute | solution.py:477
  256.5 2.5 broadcast_in_dim.9.code_ref
  259.1 13.9 %shard_map.105.refs_0_ = bf16[3584,1024]{1,0:T(8,128)(2,1)} custom-call(s32[256]{0:T(256)} %reshape_squeeze.3.before_ref, s32[3584,128]{1,0:T(8,128)} %broadcast_in_dim.9.code_ref, bf16[3584,1024]{1,0:T(8,128)(2,1)} %initial_ref.9, bf16[448,512]{1,0:T(8,128)(2,1)} %get-tuple-element.83.refs_0_, bf16[448,512]{1,0:T(8,128)(2,1)} %copy-done.8, ...), custom_call_target="tpu_custom_call" | custom-call | flops 1879048192 | bytes 11010048 | tf_op jit(solution)/shard_map/pallas_call | solution.py:384
  278.4 2.3 collective-permute-done.18.refs_4_
  281.6 2.2 collective-permute-start.23
  283.7 3.5 %collective-permute-done.21.refs_8_ = bf16[448,256]{1,0:T(8,128)(2,1)S(1)} collective-permute-done((bf16[448,256]{1,0:T(8,128)(2,1)}, bf16[448,256]{1,0:T(8,128)(2,1)S(1)}, u32[]{:S(2)}, u32[]{:S(2)}) %collective-permute-start.21) | collective-permute-done | bytes 229408 | tf_op jit(solution)/shard_map/ppermute | solution.py:477
  287.3 12.3 %shard_map.106.refs_0_ = bf16[3584,1024]{1,0:T(8,128)(2,1)} custom-call(s32[256]{0:T(256)} %reshape_squeeze.3.before_ref, s32[3584,128]{1,0:T(8,128)} %broadcast_in_dim.9.code_ref, bf16[3584,1024]{1,0:T(8,128)(2,1)} %initial_ref.9, bf16[3584,1024]{1,0:T(8,128)(2,1)} %shard_map.105.refs_0_, ...), custom_call_target="tpu_custom_call", output_to_operand_aliasing={{}: (3, {})} | custom-call | flops 939524096 | bytes 5505024 | tf_op jit(solution)/shard_map/pallas_call | solution.py:384
  299.5 2.2 fusion.2
  304.0 6.6 %collective-permute-done.25.refs_4_ = bf16[448,256]{1,0:T(8,128)(2,1)S(1)} collective-permute-done((bf16[448,256]{1,0:T(8,128)(2,1)S(1)}, bf16[448,256]{1,0:T(8,128)(2,1)S(1)}, u32[]{:S(2)}, u32[]{:S(2)}) %collective-permute-start.25) | collective-permute-done | bytes 229408 | tf_op jit(solution)/shard_map/ppermute | solution.py:477
  311.2 12.1 %shard_map.107 = bf16[3584,1024]{1,0:T(8,128)(2,1)} custom-call(s32[256]{0:T(256)} %reshape_squeeze.3.before_ref, s32[3584,128]{1,0:T(8,128)} %broadcast_in_dim.9.code_ref, bf16[3584,1024]{1,0:T(8,128)(2,1)} %initial_ref.9, bf16[3584,1024]{1,0:T(8,128)(2,1)} %shard_map.106.refs_0_, ...), custom_call_target="tpu_custom_call", output_to_operand_aliasing={{}: (3, {})} | custom-call | flops 939524096 | bytes 5505024 | tf_op jit(solution)/shard_map/pallas_call | solution.py:384
  (99 shorter events, 23.6 us)
Async XLA Ops:
  105.3 22.7 %collective-permute-start = (bf16[448,1024]{1,0:T(8,128)(2,1)}, bf16[448,1024]{1,0:T(8,128)(2,1)S(1)}, u32[]{:S(2)}, u32[]{:S(2)}) collective-permute-start(bf16[448,1024]{1,0:T(8,128)(2,1)} %get-tuple-element.67), channel_id=1, source_target_pairs={{0,16},{4,20},{8,24},{12,28},{16,0},{20,4},{24,8},{28,12},{1,17},{... | collective-permute-start | bytes 2752520 | tf_op jit(solution)/shard_map/ppermute | solution.py:477
  128.0 171.5 %all-to-all-start = ((f32[4,8,8,3584]{3,2,1,0:T(8,128)}), f32[4,8,8,3584]{3,2,1,0:T(8,128)}, u32[]{:S(2)}, u32[]{:S(2)}) async-start(f32[4,8,8,3584]{3,2,1,0:T(8,128)} %get-tuple-element.68), calls=%async_computation | async-start | bytes 7340032 | tf_op jit(solution)/shard_map/all_to_all | solution.py:484
  132.9 24.5 %collective-permute-start.4 = (bf16[448,1024]{1,0:T(8,128)(2,1)}, bf16[448,1024]{1,0:T(8,128)(2,1)S(1)}, u32[]{:S(2)}, u32[]{:S(2)}) collective-permute-start(bf16[448,1024]{1,0:T(8,128)(2,1)} %get-tuple-element.78), channel_id=1, source_target_pairs={{0,24},{4,28},{8,16},{12,20},{16,8},{20,12},{24,0},{28,4},{1,25},{... | collective-permute-start | bytes 2752520 | tf_op jit(solution)/shard_map/ppermute | solution.py:477
  134.9 40.8 %collective-permute-start.1 = (bf16[448,1024]{1,0:T(8,128)(2,1)}, bf16[448,1024]{1,0:T(8,128)(2,1)S(1)}, u32[]{:S(2)}, u32[]{:S(2)}) collective-permute-start(bf16[448,1024]{1,0:T(8,128)(2,1)} %get-tuple-element.74), channel_id=1, source_target_pairs={{0,28},{4,24},{8,20},{12,16},{16,12},{20,8},{24,4},{28,0},{1,29},{... | collective-permute-start | bytes 2752520 | tf_op jit(solution)/shard_map/ppermute | solution.py:477
  134.9 60.5 %collective-permute-start.6 = (bf16[448,1024]{1,0:T(8,128)(2,1)}, bf16[448,1024]{1,0:T(8,128)(2,1)}, u32[]{:S(2)}, u32[]{:S(2)}) collective-permute-start(bf16[448,1024]{1,0:T(8,128)(2,1)} %get-tuple-element.80), channel_id=1, source_target_pairs={{0,20},{4,16},{8,28},{12,24},{16,4},{20,0},{24,12},{28,8},{1,21},{... | collective-permute-start | bytes 2752520 | tf_op jit(solution)/shard_map/ppermute | solution.py:477
  137.0 59.8 %collective-permute-start.3 = (bf16[448,1024]{1,0:T(8,128)(2,1)}, bf16[448,1024]{1,0:T(8,128)(2,1)}, u32[]{:S(2)}, u32[]{:S(2)}) collective-permute-start(bf16[448,1024]{1,0:T(8,128)(2,1)} %get-tuple-element.76), channel_id=1, source_target_pairs={{0,8},{4,12},{8,0},{12,4},{16,24},{20,28},{24,16},{28,20},{1,9},{5... | collective-permute-start | bytes 2752520 | tf_op jit(solution)/shard_map/ppermute | solution.py:477
  157.4 57.7 %collective-permute-start.5 = (bf16[448,1024]{1,0:T(8,128)(2,1)}, bf16[448,1024]{1,0:T(8,128)(2,1)}, u32[]{:S(2)}, u32[]{:S(2)}) collective-permute-start(bf16[448,1024]{1,0:T(8,128)(2,1)} %get-tuple-element.79), channel_id=1, source_target_pairs={{0,12},{4,8},{8,4},{12,0},{16,28},{20,24},{24,20},{28,16},{1,13},{... | collective-permute-start | bytes 2752520 | tf_op jit(solution)/shard_map/ppermute | solution.py:477
  175.8 40.6 %collective-permute-start.2 = (bf16[448,1024]{1,0:T(8,128)(2,1)}, bf16[448,1024]{1,0:T(8,128)(2,1)}, u32[]{:S(2)}, u32[]{:S(2)}) collective-permute-start(bf16[448,1024]{1,0:T(8,128)(2,1)} %get-tuple-element.75), channel_id=1, source_target_pairs={{0,4},{4,0},{8,12},{12,8},{16,20},{20,16},{24,28},{28,24},{1,5},{5... | collective-permute-start | bytes 2752520 | tf_op jit(solution)/shard_map/ppermute | solution.py:477
  193.3 39.6 %collective-permute-start.10 = (bf16[448,512]{1,0:T(8,128)(2,1)}, bf16[448,512]{1,0:T(8,128)(2,1)S(1)}, u32[]{:S(2)}, u32[]{:S(2)}) collective-permute-start(bf16[448,512]{1,0:T(8,128)(2,1)} %get-tuple-element.92), channel_id=1, source_target_pairs={{0,24},{4,28},{8,16},{12,20},{16,8},{20,12},{24,0},{28,4},{1,25},{... | collective-permute-start | bytes 1376264 | tf_op jit(solution)/shard_map/ppermute | solution.py:477
  195.4 38.1 %collective-permute-start.7 = (bf16[448,512]{1,0:T(8,128)(2,1)S(1)}, bf16[448,512]{1,0:T(8,128)(2,1)S(1)}, u32[]{:S(2)}, u32[]{:S(2)}) collective-permute-start(bf16[448,512]{1,0:T(8,128)(2,1)S(1)} %copy-done.24), channel_id=1, source_target_pairs={{0,28},{4,24},{8,20},{12,16},{16,12},{20,8},{24,4},{28,0},{1,29},{... | collective-permute-start | bytes 1376264 | tf_op jit(solution)/shard_map/ppermute | solution.py:477
  196.8 38.8 %collective-permute-start.12 = (bf16[448,512]{1,0:T(8,128)(2,1)}, bf16[448,512]{1,0:T(8,128)(2,1)S(1)}, u32[]{:S(2)}, u32[]{:S(2)}) collective-permute-start(bf16[448,512]{1,0:T(8,128)(2,1)} %get-tuple-element.95), channel_id=1, source_target_pairs={{0,16},{4,20},{8,24},{12,28},{16,0},{20,4},{24,8},{28,12},{1,17},{... | collective-permute-start | bytes 1376264 | tf_op jit(solution)/shard_map/ppermute | solution.py:477
  215.1 28.9 %collective-permute-start.13 = (bf16[448,512]{1,0:T(8,128)(2,1)}, bf16[448,512]{1,0:T(8,128)(2,1)S(1)}, u32[]{:S(2)}, u32[]{:S(2)}) collective-permute-start(bf16[448,512]{1,0:T(8,128)(2,1)} %get-tuple-element.97), channel_id=1, source_target_pairs={{0,20},{4,16},{8,28},{12,24},{16,4},{20,0},{24,12},{28,8},{1,21},{... | collective-permute-start | bytes 1376264 | tf_op jit(solution)/shard_map/ppermute | solution.py:477
  233.6 13.9 %collective-permute-start.8 = (bf16[448,512]{1,0:T(8,128)(2,1)}, bf16[448,512]{1,0:T(8,128)(2,1)S(1)}, u32[]{:S(2)}, u32[]{:S(2)}) collective-permute-start(bf16[448,512]{1,0:T(8,128)(2,1)} %get-tuple-element.87), channel_id=1, source_target_pairs={{0,4},{4,0},{8,12},{12,8},{16,20},{20,16},{24,28},{28,24},{1,5},{5... | collective-permute-start | bytes 1376264 | tf_op jit(solution)/shard_map/ppermute | solution.py:477
  234.6 21.5 %collective-permute-start.9 = (bf16[448,512]{1,0:T(8,128)(2,1)}, bf16[448,512]{1,0:T(8,128)(2,1)S(1)}, u32[]{:S(2)}, u32[]{:S(2)}) collective-permute-start(bf16[448,512]{1,0:T(8,128)(2,1)} %get-tuple-element.89), channel_id=1, source_target_pairs={{0,8},{4,12},{8,0},{12,4},{16,24},{20,28},{24,16},{28,20},{1,9},{5... | collective-permute-start | bytes 1376264 | tf_op jit(solution)/shard_map/ppermute | solution.py:477
  235.6 37.4 %collective-permute-start.17 = (bf16[448,256]{1,0:T(8,128)(2,1)}, bf16[448,256]{1,0:T(8,128)(2,1)S(1)}, u32[]{:S(2)}, u32[]{:S(2)}) collective-permute-start(bf16[448,256]{1,0:T(8,128)(2,1)} %get-tuple-element.107), channel_id=1, source_target_pairs={{0,24},{4,28},{8,16},{12,20},{16,8},{20,12},{24,0},{28,4},{1,25},{... | collective-permute-start | bytes 688136 | tf_op jit(solution)/shard_map/ppermute | solution.py:477
  243.9 30.5 %collective-permute-start.14 = (bf16[448,256]{1,0:T(8,128)(2,1)}, bf16[448,256]{1,0:T(8,128)(2,1)}, u32[]{:S(2)}, u32[]{:S(2)}) collective-permute-start(bf16[448,256]{1,0:T(8,128)(2,1)} %get-tuple-element.101), channel_id=1, source_target_pairs={{0,28},{4,24},{8,20},{12,16},{16,12},{20,8},{24,4},{28,0},{1,29},{... | collective-permute-start | bytes 688136 | tf_op jit(solution)/shard_map/ppermute | solution.py:477
  245.8 28.7 %collective-permute-start.20 = (bf16[448,256]{1,0:T(8,128)(2,1)}, bf16[448,256]{1,0:T(8,128)(2,1)}, u32[]{:S(2)}, u32[]{:S(2)}) collective-permute-start(bf16[448,256]{1,0:T(8,128)(2,1)} %get-tuple-element.112), channel_id=1, source_target_pairs={{0,20},{4,16},{8,28},{12,24},{16,4},{20,0},{24,12},{28,8},{1,21},{... | collective-permute-start | bytes 688136 | tf_op jit(solution)/shard_map/ppermute | solution.py:477
  247.5 28.5 %collective-permute-start.16 = (bf16[448,256]{1,0:T(8,128)(2,1)}, bf16[448,256]{1,0:T(8,128)(2,1)S(1)}, u32[]{:S(2)}, u32[]{:S(2)}) collective-permute-start(bf16[448,256]{1,0:T(8,128)(2,1)} %get-tuple-element.104), channel_id=1, source_target_pairs={{0,8},{4,12},{8,0},{12,4},{16,24},{20,28},{24,16},{28,20},{1,9},{5... | collective-permute-start | bytes 688136 | tf_op jit(solution)/shard_map/ppermute | solution.py:477
  256.1 20.7 %collective-permute-start.19 = (bf16[448,256]{1,0:T(8,128)(2,1)}, bf16[448,256]{1,0:T(8,128)(2,1)S(1)}, u32[]{:S(2)}, u32[]{:S(2)}) collective-permute-start(bf16[448,256]{1,0:T(8,128)(2,1)} %get-tuple-element.110), channel_id=1, source_target_pairs={{0,16},{4,20},{8,24},{12,28},{16,0},{20,4},{24,8},{28,12},{1,17},{... | collective-permute-start | bytes 688136 | tf_op jit(solution)/shard_map/ppermute | solution.py:477
  276.0 28.0 %collective-permute-start.26 = (bf16[448,256]{1,0:T(8,128)(2,1)}, bf16[448,256]{1,0:T(8,128)(2,1)S(1)}, u32[]{:S(2)}, u32[]{:S(2)}) collective-permute-start(bf16[448,256]{1,0:T(8,128)(2,1)} %get-tuple-element.125), channel_id=1, source_target_pairs={{0,16},{4,20},{8,24},{12,28},{16,0},{20,4},{24,8},{28,12},{1,17},{... | collective-permute-start | bytes 688136 | tf_op jit(solution)/shard_map/ppermute | solution.py:477
  276.8 26.4 %collective-permute-start.24 = (bf16[448,256]{1,0:T(8,128)(2,1)}, bf16[448,256]{1,0:T(8,128)(2,1)S(1)}, u32[]{:S(2)}, u32[]{:S(2)}) collective-permute-start(bf16[448,256]{1,0:T(8,128)(2,1)} %get-tuple-element.122), channel_id=1, source_target_pairs={{0,24},{4,28},{8,16},{12,20},{16,8},{20,12},{24,0},{28,4},{1,25},{... | collective-permute-start | bytes 688136 | tf_op jit(solution)/shard_map/ppermute | solution.py:477
  280.7 23.2 %collective-permute-start.27 = (bf16[448,256]{1,0:T(8,128)(2,1)}, bf16[448,256]{1,0:T(8,128)(2,1)S(1)}, u32[]{:S(2)}, u32[]{:S(2)}) collective-permute-start(bf16[448,256]{1,0:T(8,128)(2,1)} %get-tuple-element.127), channel_id=1, source_target_pairs={{0,20},{4,16},{8,28},{12,24},{16,4},{20,0},{24,12},{28,8},{1,21},{... | collective-permute-start | bytes 688136 | tf_op jit(solution)/shard_map/ppermute | solution.py:477
  281.6 22.4 %collective-permute-start.23 = (bf16[448,256]{1,0:T(8,128)(2,1)}, bf16[448,256]{1,0:T(8,128)(2,1)S(1)}, u32[]{:S(2)}, u32[]{:S(2)}) collective-permute-start(bf16[448,256]{1,0:T(8,128)(2,1)} %get-tuple-element.119), channel_id=1, source_target_pairs={{0,8},{4,12},{8,0},{12,4},{16,24},{20,28},{24,16},{28,20},{1,9},{5... | collective-permute-start | bytes 688136 | tf_op jit(solution)/shard_map/ppermute | solution.py:477
  287.2 16.8 %collective-permute-start.22 = (bf16[448,256]{1,0:T(8,128)(2,1)}, bf16[448,256]{1,0:T(8,128)(2,1)S(1)}, u32[]{:S(2)}, u32[]{:S(2)}) collective-permute-start(bf16[448,256]{1,0:T(8,128)(2,1)} %get-tuple-element.117), channel_id=1, source_target_pairs={{0,4},{4,0},{8,12},{12,8},{16,20},{20,16},{24,28},{28,24},{1,5},{5... | collective-permute-start | bytes 688136 | tf_op jit(solution)/shard_map/ppermute | solution.py:477
  (31 other events, 463.5 us)

commit v4 on v3

v4 whole, which is shorter than its diff:
```python
import functools

import jax
import jax.numpy as jnp
from jax import lax
from jax.experimental import pallas as pl
from jax.experimental.pallas import tpu as pltpu
from jax.sharding import PartitionSpec as P

D = 4096
A_DEV = 32
MESH = pl.DeviceIdType.MESH

PEERS = 8
LANES = 128
ORDER = (6, 7, 4, 5, 2, 3, 1)
LATER = (2, 4, 3, 5, 1, 6, 7)
AHEAD = 9
ROWS = 32
COST_ROWS = 512
PARTS = 4
OVER_LANES = (((1,), (1,)), ((), ()))


def one_hot(hit):
    return jnp.where(hit, 1.0, 0.0).astype(jnp.bfloat16)


def matmul(a, b):
    return jnp.dot(a, b, preferred_element_type=jnp.float32)


def count_ranks(count, me, perm_ref, slot_ref, hot, halves, padded, sent):
    used, pad = perm_ref.shape[0], padded.shape[0]
    slots = count // PEERS
    padded[...] = jnp.full(padded.shape, PEERS * count, jnp.int32)
    padded[:used] = perm_ref[...]
    perm = padded[...]
    source = jnp.zeros_like(perm)
    for k in range(1, PEERS + 1):
        source = source + jnp.where(perm >= k * count, 1, 0)
    row = perm - source * count
    masks = jnp.concatenate([jnp.where(source == k, 1.0, 0.0) for k in range(PEERS)], axis=0)
    packed = masks.astype(jnp.bfloat16)
    shape = (LANES, LANES)
    lane_before = one_hot(lax.broadcasted_iota(jnp.int32, shape, 0) < lax.broadcasted_iota(jnp.int32, shape, 1))
    within = matmul(packed, lane_before)
    totals = matmul(packed, jnp.ones(shape, jnp.bfloat16)).astype(jnp.bfloat16)
    shape = (PEERS * pad, PEERS * pad)
    left, right = lax.broadcasted_iota(jnp.int32, shape, 0), lax.broadcasted_iota(jnp.int32, shape, 1)
    row_before = one_hot((right < left) & (right >= left - lax.rem(left, pad)))
    ahead = matmul(row_before, totals)
    ranked = masks * (within + ahead)
    rank = ranked[:pad]
    for k in range(1, PEERS):
        rank = rank + ranked[k * pad : (k + 1) * pad]
    rank = rank.astype(jnp.int32)
    slot_ref[...] = jnp.clip((source ^ me) * slots + rank, 0, count - 1)

    high = lax.shift_right_logical(row, 8).astype(jnp.float32)
    low = (row & 255).astype(jnp.float32)
    block = lax.broadcasted_iota(jnp.int32, (PEERS, LANES), 0)
    slot = lax.broadcasted_iota(jnp.int32, (slots, LANES), 0)
    for j in range(used):
        at = slice(j * LANES, (j + 1) * LANES)
        one = slice(j, j + 1)
        mine = source[one] == block
        both = [jnp.where(mine, part[one], 0.0) for part in (high, low)]
        halves[:, at] = jnp.concatenate(both, axis=0).astype(jnp.bfloat16)
        hot[:, at] = one_hot(rank[one] == slot)
    found = lax.dot_general(halves[...], hot[...], OVER_LANES, preferred_element_type=jnp.float32)
    wanted = found[:PEERS] * 256.0 + found[PEERS:]
    for k in range(PEERS):
        sent[k, :, :slots] = jnp.broadcast_to(wanted[k : k + 1], (8, slots)).astype(jnp.int32)
        sent[k, :, slots:] = jnp.zeros((8, sent.shape[2] - slots), jnp.int32)


def spread_out(rows_ref, spread, tiles=None):
    tall, width = rows_ref.shape
    tiles = tiles or width // LANES

    def step(m, carry):
        for c in range(tiles):
            v = rows_ref[pl.ds(pl.multiple_of(m * 16, 16), 16), c * LANES : (c + 1) * LANES].astype(jnp.float32)
            for h in range(2):
                to = (m * 2 + h) * 8 * tiles + c * 8
                spread[pl.ds(pl.multiple_of(to, 8), 8), :] = v[h * 8 : h * 8 + 8]
        return carry

    lax.fori_loop(0, tall // 16, step, 0)


def first_of(row, tiles):
    return lax.shift_right_logical(row, 3) * (8 * tiles) + (row & 7)


def rows_of(begin_of, spread, turn, tiles):
    for s in range(ROWS):
        to = (s // 8) * 8 * tiles + s % 8
        turn[pl.ds(to, tiles, stride=8), :] = spread[pl.ds(begin_of(s), tiles, stride=8), :]
    for h in range(ROWS // 16):
        for c in range(tiles):
            both = [turn[pl.ds(((2 * h + half) * tiles + c) * 8, 8), :] for half in range(2)]
            yield h * 16, c, jnp.concatenate(both, axis=0)


def table_reader(table):
    per = LANES // ROWS

    def read(j, s):
        return table[lax.div(j, per), lax.rem(j, per) * ROWS + s]

    return read


def main_kernel(count, cut, perm_ref, up_a, gate_a, down_a, up_b, gate_b, down_b, *refs):
    begin_ref, means, costs_ref, refs = refs[0], refs[1:4], refs[4], refs[5:]
    sent, moved, refs = refs[:4], refs[4:8], refs[8:]
    hot, halves, padded, slot, table, begins, ask, got, asked, held, window, windows, wide, rows, spread, turn, stage = refs[:17]
    part, shares, refs = refs[17], refs[18], refs[19:]
    ask_send, ask_recv, win_send, win_recv, item_send, item_recv, share_send, share_recv, strip_sems, load_sems, stage_sems, own_sem = refs
    me, column = lax.axis_index("rows"), lax.axis_index("cols")
    slots = count // PEERS
    stride = count // A_DEV
    cols = part.shape[0]
    features = up_a.shape[1]
    widths = (features, features, cut, features - cut)
    barrier = pltpu.get_barrier_semaphore()
    for k in range(1, PEERS):
        pl.semaphore_signal(barrier, inc=1, device_id={"rows": me ^ k}, device_id_type=MESH)
    for k in range(1, cols):
        pl.semaphore_signal(barrier, inc=1, device_id={"cols": column ^ k}, device_id_type=MESH)

    strips = []
    for m, ref in enumerate((up_a, gate_a)):
        for i in range(A_DEV):
            at = m * A_DEV + i
            strips.append(
                pltpu.make_async_copy(ref.at[pl.ds(i * stride, 16)], held.at[pl.ds(at * 16, 16)], strip_sems.at[at])
            )
    for copy in strips:
        copy.start()
    loads = [pltpu.make_async_copy(ref, rows.at[n], load_sems.at[n]) for n, ref in enumerate((up_b, gate_b))]
    for copy in loads:
        copy.start()

    for copy in strips:
        copy.wait()
    shape = (2 * A_DEV, 32 * A_DEV)
    first = lax.broadcasted_iota(jnp.int32, shape, 0) * 16 == lax.broadcasted_iota(jnp.int32, shape, 1)
    window[...] = matmul(one_hot(first), held[...]).astype(jnp.bfloat16)
    windows[0] = window[...]
    pl.semaphore_wait(barrier, PEERS - 1 + cols - 1)

    def remote(src, dst, send, recv, peer, axis="rows"):
        return pltpu.make_async_remote_copy(
            src_ref=src, dst_ref=dst, send_sem=send, recv_sem=recv, device_id={axis: peer}, device_id_type=MESH
        )

    across = [remote(window, windows.at[k], win_send.at[k], win_recv.at[k], me ^ k) for k in (6, 2, 4)]
    for copy in across:
        copy.start()

    count_ranks(count, me, perm_ref, slot, hot, halves, padded, ask)
    asks = [remote(ask.at[me ^ k], got.at[k], ask_send.at[k], ask_recv.at[k], me ^ k) for k in ORDER]
    for copy in asks:
        copy.start()
    own = pltpu.make_async_copy(ask.at[me], got.at[0], own_sem)
    own.start()
    begin_ref[...] = first_of(slot[...], widths[3] // LANES)
    loads[0].wait()
    spread_out(rows.at[0], spread)
    own.wait()
    for copy in asks:
        copy.wait()
    got[...] = first_of(jnp.clip(got[...], 0, count - 1), features // LANES)
    own = pltpu.make_async_copy(got, asked, own_sem)
    own.start()
    own.wait()

    def gather(k, buffer):
        def step(t, carry):
            for row, c, tile in rows_of(lambda s: asked[k, 0, t * ROWS + s], spread, turn, features // LANES):
                at = pl.ds(pl.multiple_of(t * ROWS + row, 16), 16)
                stage[buffer, at, c * LANES : (c + 1) * LANES] = tile.astype(jnp.bfloat16)
            return carry

        lax.fori_loop(0, slots // ROWS, step, 0)

    items = [(a, k) for a in range(4) for k in (ORDER if a < 2 else LATER)]

    def item(a, k):
        return remote(sent[a].at[k], moved[a].at[k], item_send.at[a, k], item_recv.at[a, k], me ^ k)

    def up_step(n, carry):
        k = n ^ 6
        gather(k, 0)
        copy = pltpu.make_async_copy(stage.at[0], sent[0].at[k], stage_sems.at[0])
        copy.start()
        copy.wait()

        @pl.when(k > 0)
        def _():
            item(0, k).start()

        return carry

    lax.fori_loop(0, PEERS, up_step, 0)
    done = {"sent": len(ORDER), "here": 0}

    def push(count_of):
        while done["sent"] < count_of:
            item(*items[done["sent"]]).start()
            done["sent"] += 1

    def receive(until, last=None):
        while done["here"] < until:
            item(*items[done["here"]]).wait_recv()
            done["here"] += 1
            push(min(done["here"] + AHEAD, last or len(items)))

    for copy in across:
        copy.wait()
    beside = [remote(windows.at[k], windows.at[k + 1], win_send.at[k + 1], win_recv.at[k + 1], me ^ 1) for k in (0, 2, 4, 6)]
    for copy in beside:
        copy.start()

    def collect(*arrays):
        def copies(k, buffer):
            begin = 0
            for n, a in enumerate(arrays):
                src = stage.at[buffer, :, pl.ds(begin, widths[a])]
                begin += widths[a]
                yield pltpu.make_async_copy(src, sent[a].at[k], stage_sems.at[2 * n + buffer])

        def step(n, carry):
            buffer = n & 1

            @pl.when(n >= 2)
            def _():
                for copy in copies(0, buffer):
                    copy.wait()

            gather(n ^ 6, buffer)
            for copy in copies(n ^ 6, buffer):
                copy.start()
            return carry

        lax.fori_loop(0, PEERS, step, 0)
        for buffer in range(2):
            for copy in copies(0, buffer):
                copy.wait()

    loads[1].wait()
    spread_out(rows.at[1], spread)
    collect(1)
    push(AHEAD)

    for copy in beside:
        copy.wait()
    for k in range(PEERS):
        for m in range(2):
            wide[m, k * A_DEV : (k + 1) * A_DEV, :] = windows[k, m * A_DEV : (m + 1) * A_DEV, :]
    group = part.shape[2]

    def cost(j, carry):
        at = pl.ds(pl.multiple_of(j * COST_ROWS, COST_ROWS), COST_ROWS)
        both = [
            lax.dot_general(wide[m], rows[m, at, :], OVER_LANES, preferred_element_type=jnp.float32) for m in range(2)
        ]
        value = both[0] + both[1]
        for k in range(PEERS):
            for c in range(cols):
                begin = k * A_DEV + c * group
                part[c, me ^ k, :, at] = value[begin : begin + group]
        return carry

    lax.fori_loop(0, count // COST_ROWS, cost, 0)
    exchanged = [
        remote(part.at[column ^ k], shares.at[k - 1], share_send.at[k], share_recv.at[k], column ^ k, "cols")
        for k in range(1, cols)
    ]
    for copy in exchanged:
        copy.start()
    load = pltpu.make_async_copy(down_b, rows.at[0], load_sems.at[0])
    load.start()
    load.wait()
    spread_out(rows.at[0], spread)
    collect(2, 3)

    def place(a, initial, out):
        width = widths[a]
        tiles = width // LANES
        lanes = pl.ds(0, width)
        table[...] = first_of(slot[...], tiles)
        to_table = pltpu.make_async_copy(table, begins, own_sem)
        to_table.start()
        ours = pltpu.make_async_copy(initial.at[:, lanes], rows.at[1, :, lanes], load_sems.at[1])
        ours.start()
        own_rows = pltpu.make_async_copy(sent[a].at[0], rows.at[0, pl.ds(0, slots), lanes], stage_sems.at[0])
        own_rows.start()
        fetched = [
            pltpu.make_async_copy(moved[a].at[k], rows.at[0, pl.ds(k * slots, slots), lanes], strip_sems.at[k])
            for k in range(1, PEERS)
        ]
        for copy in fetched:
            copy.start()
        own_rows.wait()
        for copy in fetched:
            copy.wait()
        spread_out(rows.at[0], spread, tiles)
        to_table.wait()
        ours.wait()
        read = table_reader(begins)

        def step(j, carry):
            for row, c, tile in rows_of(lambda s: read(j, s), spread, turn, tiles):
                at = pl.ds(pl.multiple_of(j * ROWS + row, 16), 16)
                columns = slice(c * LANES, (c + 1) * LANES)
                mean = (rows[1, at, columns].astype(jnp.float32) + tile) * 0.5
                rows[1, at, columns] = mean.astype(jnp.bfloat16)
            return carry

        lax.fori_loop(0, count // ROWS, step, 0)
        written = pltpu.make_async_copy(rows.at[1, :, lanes], out, load_sems.at[1])
        written.start()
        written.wait()

    held_back = 3 * len(ORDER)
    receive(len(ORDER), held_back)
    place(0, up_a, means[0])
    receive(2 * len(ORDER), held_back)
    place(1, gate_a, means[1])
    for copy in exchanged:
        copy.wait()
    for block in range(PEERS):
        value = part[column, block]
        for k in range(1, cols):
            value = value + shares[k - 1, block]
        value = value * (2.0 * D) ** (-0.5)
        for m in range(group):
            costs_ref[m * PEERS + block : m * PEERS + block + 1, :] = value[m : m + 1]
    receive(held_back - 3, held_back)
    push(len(items))
    receive(held_back)
    place(2, down_a, means[2])
    receive(len(items))
    for a, k in items:
        item(a, k).wait_send()


def last_kernel(cut, begins, up_ref, gate_ref, down_ref, costs_ref, own_ref, moved_ref, initial, *refs):
    up_out, gate_out, down_out, costs_out, rows, ours, spread, turn, sems = refs
    count, features = initial.shape
    slots = count // PEERS
    width = features - cut
    tiles = width // LANES
    left, right = pl.ds(0, cut), pl.ds(cut, width)
    fetched = [pltpu.make_async_copy(own_ref.at[0], rows.at[pl.ds(0, slots)], sems.at[0])]
    fetched += [
        pltpu.make_async_copy(moved_ref.at[k], rows.at[pl.ds(k * slots, slots)], sems.at[k]) for k in range(1, PEERS)
    ]
    fetched.append(pltpu.make_async_copy(initial.at[:, right], ours, sems.at[PEERS]))
    handed = []
    piece = count // PARTS
    for n in range(PARTS):
        at = pl.ds(n * piece, piece)
        pairs = ((up_ref, up_out.at[at]), (gate_ref, gate_out.at[at]), (down_ref, down_out.at[at, left]))
        for m, (src, dst) in enumerate(pairs):
            handed.append(pltpu.make_async_copy(src.at[at], dst, sems.at[PEERS + 1 + 3 * n + m]))
    handed.append(pltpu.make_async_copy(costs_ref, costs_out, sems.at[PEERS + 1 + 3 * PARTS]))
    for copy in fetched + handed:
        copy.start()
    for copy in fetched:
        copy.wait()
    spread_out(rows, spread)
    read = table_reader(begins)

    def step(j, carry):
        for row, c, tile in rows_of(lambda s: read(j, s), spread, turn, tiles):
            at = pl.ds(pl.multiple_of(j * ROWS + row, 16), 16)
            columns = slice(c * LANES, (c + 1) * LANES)
            ours[at, columns] = ((ours[at, columns].astype(jnp.float32) + tile) * 0.5).astype(jnp.bfloat16)
        return carry

    lax.fori_loop(0, count // ROWS, step, 0)
    written = pltpu.make_async_copy(ours, down_out.at[:, right], sems.at[0])
    written.start()
    for copy in handed:
        copy.wait()
    written.wait()


def balanced(up_a, gate_a, down_a, up_b, gate_b, down_b, perm):
    count, features = up_a.shape
    cols = lax.axis_size("cols")
    cut = features * 3 // 4
    used = count // LANES
    pad = -(-used // 8) * 8
    slots = count // PEERS
    lanes = -(-slots // LANES) * LANES
    tiles = features // LANES
    vmem, smem = pl.BlockSpec(memory_space=pltpu.VMEM), pl.BlockSpec(memory_space=pltpu.SMEM)
    hbm = pl.BlockSpec(memory_space=pltpu.HBM)
    bf16, f32, i32 = jnp.bfloat16, jnp.float32, jnp.int32
    group = A_DEV // cols
    whole = jax.ShapeDtypeStruct((count, features), bf16)
    costs_shape = jax.ShapeDtypeStruct((group * PEERS, count), f32)
    lists = [jax.ShapeDtypeStruct((PEERS, slots, size), bf16) for size in (features, features, cut, features - cut)]
    begins, *parts = pl.pallas_call(
        functools.partial(main_kernel, count, cut),
        out_shape=[jax.ShapeDtypeStruct((pad, LANES), i32), whole, whole, jax.ShapeDtypeStruct((count, cut), bf16), costs_shape]
        + lists * 2,
        in_specs=[vmem] + [hbm] * 6,
        out_specs=[vmem] + [hbm] * 3 + [vmem] + [hbm] * 8,
        scratch_shapes=[
            pltpu.VMEM((slots, count), bf16),
            pltpu.VMEM((2 * PEERS, count), bf16),
            pltpu.VMEM((pad, LANES), i32),
            pltpu.VMEM((pad, LANES), i32),
            pltpu.VMEM((pad, LANES), i32),
            pltpu.SMEM((pad, LANES), i32),
            pltpu.VMEM((PEERS, 8, lanes), i32),
            pltpu.VMEM((PEERS, 8, lanes), i32),
            pltpu.SMEM((PEERS, 8, lanes), i32),
            pltpu.VMEM((32 * A_DEV, features), bf16),
            pltpu.VMEM((2 * A_DEV, features), bf16),
            pltpu.VMEM((PEERS, 2 * A_DEV, features), bf16),
            pltpu.VMEM((2, A_DEV * PEERS, features), bf16),
            pltpu.VMEM((2, count, features), bf16),
            pltpu.VMEM(((count + 8) * tiles, LANES), f32),
            pltpu.VMEM(((ROWS + 8) * tiles, LANES), f32),
            pltpu.VMEM((2, slots, features), bf16),
            pltpu.VMEM((cols, PEERS, group, count), f32),
            pltpu.VMEM((cols - 1, PEERS, group, count), f32),
        ]
        + [pltpu.SemaphoreType.DMA((PEERS,))] * 4
        + [pltpu.SemaphoreType.DMA((4, PEERS))] * 2
        + [pltpu.SemaphoreType.DMA((cols,))] * 2
        + [
            pltpu.SemaphoreType.DMA((2 * A_DEV,)),
            pltpu.SemaphoreType.DMA((2,)),
            pltpu.SemaphoreType.DMA((4,)),
            pltpu.SemaphoreType.DMA,
        ],
        compiler_params=pltpu.CompilerParams(
            collective_id=0, has_side_effects=True, vmem_limit_bytes=62 * 1024 * 1024
        ),
    )(perm.reshape(used, LANES), up_a, gate_a, down_a, up_b, gate_b, down_b)
    up_part, gate_part, down_part, costs_part = parts[:4]
    own, moved = parts[7], parts[11]
    width = features - cut
    up_mean, gate_mean, down_mean, costs = pl.pallas_call(
        functools.partial(last_kernel, cut),
        out_shape=[whole, whole, whole, costs_shape],
        in_specs=[smem] + [hbm] * 7,
        out_specs=[hbm] * 4,
        scratch_shapes=[
            pltpu.VMEM((count, width), bf16),
            pltpu.VMEM((count, width), bf16),
            pltpu.VMEM(((count + 8) * width // LANES, LANES), f32),
            pltpu.VMEM(((ROWS + 8) * width // LANES, LANES), f32),
            pltpu.SemaphoreType.DMA((PEERS + 2 + 3 * PARTS,)),
        ],
        compiler_params=pltpu.CompilerParams(vmem_limit_bytes=62 * 1024 * 1024),
    )(begins, up_part, gate_part, down_part, costs_part, own, moved, down_a)
    return (costs.T, up_mean, gate_mean, down_mean)


def pick(array, index):
    rows = jnp.arange(array.shape[0], dtype=jnp.int32)
    hot = (index[:, None] == rows[None, :]).astype(array.dtype)
    return jnp.dot(hot, array, preferred_element_type=jnp.float32).astype(array.dtype)


def mix(initial, picked):
    return ((initial.astype(jnp.float32) + picked.astype(jnp.float32)) * 0.5).astype(jnp.bfloat16)


def general(up_a, gate_a, down_a, up_b, gate_b, down_b, perm):
    row_count, features = up_a.shape
    stride = row_count // A_DEV
    cost_scale = (2.0 * D) ** (-0.5)
    peers = lax.axis_size("rows")
    cols = lax.axis_size("cols")
    capacity = max(2, (row_count + peers - 1) // peers)

    source = perm // row_count
    local_row = perm % row_count
    blocks = jnp.arange(peers, dtype=jnp.int32)
    matches = (source[None, :] == blocks[:, None]).astype(jnp.int32)
    order = jnp.arange(row_count, dtype=jnp.int32)
    ahead = jnp.dot(
        matches.astype(jnp.bfloat16),
        (order[:, None] < order[None, :]).astype(jnp.bfloat16),
        preferred_element_type=jnp.float32,
    )
    arrival_rank = jnp.sum(ahead.astype(jnp.int32) * matches, axis=0)
    high = (local_row // 256).astype(jnp.bfloat16)
    low = (local_row % 256).astype(jnp.bfloat16)
    halves = jnp.stack([high, low])[:, None, :] * matches.astype(jnp.bfloat16)[None]
    at_rank = (arrival_rank[None, :] == jnp.arange(capacity, dtype=jnp.int32)[:, None]).astype(jnp.bfloat16)
    found = jnp.einsum("hsi,ri->hsr", halves, at_rank, preferred_element_type=jnp.float32)
    wanted = found[0].astype(jnp.int32) * 256 + found[1].astype(jnp.int32)
    asked = lax.all_to_all(wanted, "rows", split_axis=0, concat_axis=0, tiled=True).reshape(-1)
    slot = source * capacity + arrival_rank

    window = jnp.concatenate([up_a[::stride], gate_a[::stride]], axis=0)
    pieces = lax.all_gather(window, "rows").reshape(peers, 2, A_DEV, features)
    wide = pieces.transpose(1, 2, 0, 3).reshape(2, A_DEV * peers, features)
    partial_value = jnp.einsum("kd,jd->kj", wide[0], up_b, preferred_element_type=jnp.float32)
    partial_value = partial_value + jnp.einsum("kd,jd->kj", wide[1], gate_b, preferred_element_type=jnp.float32)
    total = lax.psum_scatter(partial_value.reshape(cols, -1, row_count), "cols", scatter_dimension=0)

    def averaged(initial, other):
        moved = pick(other, asked).reshape(peers, capacity, features)
        moved = lax.all_to_all(moved, "rows", split_axis=0, concat_axis=0, tiled=True)
        return mix(initial, pick(moved.reshape(-1, features), slot))

    return (
        (total * cost_scale).T,
        averaged(up_a, up_b),
        averaged(gate_a, gate_b),
        averaged(down_a, down_b),
    )


def solution(mesh):
    def local(up_a, *rest):
        row_count, features = up_a.shape
        even = mesh.shape["rows"] == PEERS and row_count % (PEERS * 16) == 0 and row_count % (A_DEV * 16) == 0
        even = even and row_count % COST_ROWS == 0 and row_count % (16 * PARTS) == 0 and row_count % (PEERS * ROWS) == 0
        even = even and features == 8 * LANES and mesh.shape["cols"] == A_DEV // 8
        return (balanced if even else general)(up_a, *rest)

    placed = (P("rows", "cols"),) * 6 + (P("rows"),)
    return jax.shard_map(
        local,
        mesh=mesh,
        in_specs=placed,
        out_specs=(P("rows", "cols"),) * 4,
        check_vma=False,
    )
```

time: 325 us -> 904 us (2.78)
  Pallas kernels: 175 us -> 903 us
  waiting for transfers between devices: 103 us -> 0 us
  starting transfers between devices: 35.8 us -> 0 us
    pallas_call x6 -> x2, Pallas kernels: 175 us -> 903 us  [the longest x1 641 us: balanced(): pl.pallas_call(functools.partial(last_kernel, cut), out_shape=[whole, who...]
    ppermute x28 -> x0, waiting for transfers between devices: 103 us -> none  [travel(): lax.ppermute(sent, 'rows', [(i, i ^ k) for i in range(PEERS)])]
    ppermute x28 -> x0, starting transfers between devices: 31 us -> none  [travel(): lax.ppermute(sent, 'rows', [(i, i ^ k) for i in range(PEERS)])]
  transfers between devices with their start and end apart: 29 -> 0, of which waited for: 10 -> 0; matrix products, arithmetic and copies ran while one was open for 2% -> 0% of each run, Pallas kernels for 18% -> 0%
where the time goes in v4:
time: 904 us; the launch traced here: 903 us
  Pallas kernels  903 us (100%)
    pallas_call x1, Pallas kernels, balanced(): pl.pallas_call(functools.partial(last_kernel, cut), out_shape=[whole, who...  641 us
    pallas_call x1, Pallas kernels, balanced(): pl.pallas_call(functools.partial(main_kernel, count, cut), out_shape=[jax...  261 us

profile of v4, /device:TPU:0, one launch (start us, length us, event | category | flops | bytes accessed | tf_op | source)
XLA Modules:
  0.0 903.4 jit_solution(12807460194042786679)
XLA Ops:
  0.6 261.3 %shard_map.102 = (s32[32,128]{1,0:T(8,128)}, bf16[3584,1024]{1,0:T(8,128)(2,1)}, bf16[3584,1024]{1,0:T(8,128)(2,1)}, bf16[3584,768]{1,0:T(8,128)(2,1)}, f32[64,3...) custom-call(s32[28,128]{1,0:T(8,128)} %bitcast.2, ...), custom_call_target="tpu_custom_call" | custom-call | tf_op jit(solution)/shard_map/pallas_call | solution.py:410
  261.9 641.5 %shard_map.103 = (bf16[3584,1024]{1,0:T(8,128)(2,1)}, bf16[3584,1024]{1,0:T(8,128)(2,1)}, bf16[3584,1024]{1,0:T(8,128)(2,1)}, f32[64,3584]{1,0:T(8,128)}) custom-call(s32[32,128]{1,0:T(8,128)} %get-tuple-element.15.begins, bf16[3584,1024]{1,0:T(8,128)(2,1)} %get-tuple-element.16.up_ref, bf16[3584,1024]{1,0:T(8,128)(2,1)} %get-tuple-element.17.gate_ref, ...), custom_call_target="tpu_custom_call" | custom-call | tf_op jit(solution)/shard_map/pallas_call | solution.py:453

commit v5 on v4

--- a/solution.py
+++ b/solution.py
@@ -350,7 +350,7 @@
 
 
 def last_kernel(cut, begins, up_ref, gate_ref, down_ref, costs_ref, own_ref, moved_ref, initial, *refs):
-    up_out, gate_out, down_out, costs_out, rows, ours, spread, turn, sems = refs
+    up_out, gate_out, down_out, costs_out, rows, ours, spread, turn, up, gate, down, costs, sems, in_sems, out_sems = refs
     count, features = initial.shape
     slots = count // PEERS
     width = features - cut
@@ -361,16 +361,20 @@
         pltpu.make_async_copy(moved_ref.at[k], rows.at[pl.ds(k * slots, slots)], sems.at[k]) for k in range(1, PEERS)
     ]
     fetched.append(pltpu.make_async_copy(initial.at[:, right], ours, sems.at[PEERS]))
-    handed = []
     piece = count // PARTS
+    read_in, handed = [], []
     for n in range(PARTS):
         at = pl.ds(n * piece, piece)
-        pairs = ((up_ref, up_out.at[at]), (gate_ref, gate_out.at[at]), (down_ref, down_out.at[at, left]))
-        for m, (src, dst) in enumerate(pairs):
-            handed.append(pltpu.make_async_copy(src.at[at], dst, sems.at[PEERS + 1 + 3 * n + m]))
-    handed.append(pltpu.make_async_copy(costs_ref, costs_out, sems.at[PEERS + 1 + 3 * PARTS]))
-    for copy in fetched + handed:
-        copy.start()
+        ways = ((up_ref.at[at], up.at[at], up_out.at[at]), (gate_ref.at[at], gate.at[at], gate_out.at[at]))
+        ways += ((down_ref.at[at], down.at[at], down_out.at[at, left]),)
+        ways += ((costs_ref, costs, costs_out),) if n == 0 else ()
+        read_in.append([pltpu.make_async_copy(w[0], w[1], in_sems.at[n, m]) for m, w in enumerate(ways)])
+        handed.append([pltpu.make_async_copy(w[1], w[2], out_sems.at[n, m]) for m, w in enumerate(ways)])
+    for copy in fetched:
+        copy.start()
+    for copies in read_in:
+        for copy in copies:
+            copy.start()
     for copy in fetched:
         copy.wait()
     spread_out(rows, spread)
@@ -383,12 +387,21 @@
             ours[at, columns] = ((ours[at, columns].astype(jnp.float32) + tile) * 0.5).astype(jnp.bfloat16)
         return carry
 
-    lax.fori_loop(0, count // ROWS, step, 0)
-    written = pltpu.make_async_copy(ours, down_out.at[:, right], sems.at[0])
-    written.start()
-    for copy in handed:
-        copy.wait()
-    written.wait()
+    steps = piece // ROWS
+    written = []
+    for n in range(PARTS):
+        for come, go in zip(read_in[n], handed[n]):
+            come.wait()
+            go.start()
+        lax.fori_loop(n * steps, (n + 1) * steps, step, 0)
+        at = pl.ds(n * piece, piece)
+        written.append(pltpu.make_async_copy(ours.at[at], down_out.at[at, right], sems.at[n]))
+        written[n].start()
+    for copies in handed:
+        for copy in copies:
+            copy.wait()
+    for copy in written:
+        copy.wait()
 
 
 def balanced(up_a, gate_a, down_a, up_b, gate_b, down_b, perm):
@@ -460,7 +473,13 @@
             pltpu.VMEM((count, width), bf16),
             pltpu.VMEM(((count + 8) * width // LANES, LANES), f32),
             pltpu.VMEM(((ROWS + 8) * width // LANES, LANES), f32),
-            pltpu.SemaphoreType.DMA((PEERS + 2 + 3 * PARTS,)),
+            pltpu.VMEM((count, features), bf16),
+            pltpu.VMEM((count, features), bf16),
+            pltpu.VMEM((count, cut), bf16),
+            pltpu.VMEM(costs_shape.shape, f32),
+            pltpu.SemaphoreType.DMA((PEERS + 1,)),
+            pltpu.SemaphoreType.DMA((PARTS, 4)),
+            pltpu.SemaphoreType.DMA((PARTS, 4)),
         ],
         compiler_params=pltpu.CompilerParams(vmem_limit_bytes=62 * 1024 * 1024),
     )(begins, up_part, gate_part, down_part, costs_part, own, moved, down_a)
@@ -529,7 +548,7 @@
     def local(up_a, *rest):
         row_count, features = up_a.shape
         even = mesh.shape["rows"] == PEERS and row_count % (PEERS * 16) == 0 and row_count % (A_DEV * 16) == 0
-        even = even and row_count % COST_ROWS == 0 and row_count % (16 * PARTS) == 0 and row_count % (PEERS * ROWS) == 0
+        even = even and row_count % COST_ROWS == 0 and row_count % (ROWS * PARTS) == 0 and row_count % (PEERS * ROWS) == 0
         even = even and features == 8 * LANES and mesh.shape["cols"] == A_DEV // 8
         return (balanced if even else general)(up_a, *rest)
 

time: 904 us -> 283 us (0.31)
  Pallas kernels: 903 us -> 282 us
    pallas_call x1, Pallas kernels: 641 us -> 20.4 us  [balanced(): pl.pallas_call(functools.partial(last_kernel, cut), out_shape=[whole, who...]
where the time goes in v5:
time: 283 us; the launch traced here: 282 us
  Pallas kernels  282 us (100%)
    pallas_call x1, Pallas kernels, balanced(): pl.pallas_call(functools.partial(main_kernel, count, cut), out_shape=[jax...  261 us
    pallas_call x1, Pallas kernels, balanced(): pl.pallas_call(functools.partial(last_kernel, cut), out_shape=[whole, who...  20.4 us

profile of v5, /device:TPU:0, one launch (start us, length us, event | category | flops | bytes accessed | tf_op | source)
XLA Modules:
  0.0 282.3 jit_solution(8037054590950017903)
XLA Ops:
  0.6 261.3 %shard_map.102 = (s32[32,128]{1,0:T(8,128)}, bf16[3584,1024]{1,0:T(8,128)(2,1)}, bf16[3584,1024]{1,0:T(8,128)(2,1)}, bf16[3584,768]{1,0:T(8,128)(2,1)}, f32[64,3...) custom-call(s32[28,128]{1,0:T(8,128)} %bitcast.2, ...), custom_call_target="tpu_custom_call" | custom-call | tf_op jit(solution)/shard_map/pallas_call | solution.py:423
  261.9 20.4 %shard_map.103 = (bf16[3584,1024]{1,0:T(8,128)(2,1)}, bf16[3584,1024]{1,0:T(8,128)(2,1)}, bf16[3584,1024]{1,0:T(8,128)(2,1)}, f32[64,3584]{1,0:T(8,128)}) custom-call(s32[32,128]{1,0:T(8,128)} %get-tuple-element.15.begins, bf16[3584,1024]{1,0:T(8,128)(2,1)} %get-tuple-element.16.up_ref, bf16[3584,1024]{1,0:T(8,128)(2,1)} %get-tuple-element.17.gate_ref, ...), custom_call_target="tpu_custom_call" | custom-call | tf_op jit(solution)/shard_map/pallas_call | solution.py:466

commit v6 on v4

--- a/solution.py
+++ b/solution.py
@@ -140,7 +140,10 @@
             )
     for copy in strips:
         copy.start()
-    loads = [pltpu.make_async_copy(ref, rows.at[n], load_sems.at[n]) for n, ref in enumerate((up_b, gate_b))]
+    loads = [
+        pltpu.make_async_copy(up_b, rows, load_sems.at[0]),
+        pltpu.make_async_copy(gate_b, means[1], load_sems.at[1]),
+    ]
     for copy in loads:
         copy.start()
 
@@ -169,7 +172,7 @@
     own.start()
     begin_ref[...] = first_of(slot[...], widths[3] // LANES)
     loads[0].wait()
-    spread_out(rows.at[0], spread)
+    spread_out(rows, spread)
     own.wait()
     for copy in asks:
         copy.wait()
@@ -252,7 +255,7 @@
                 copy.wait()
 
     loads[1].wait()
-    spread_out(rows.at[1], spread)
+    spread_out(means[1], spread)
     collect(1)
     push(AHEAD)
 
@@ -266,7 +269,8 @@
     def cost(j, carry):
         at = pl.ds(pl.multiple_of(j * COST_ROWS, COST_ROWS), COST_ROWS)
         both = [
-            lax.dot_general(wide[m], rows[m, at, :], OVER_LANES, preferred_element_type=jnp.float32) for m in range(2)
+            lax.dot_general(wide[m], ref[at, :], OVER_LANES, preferred_element_type=jnp.float32)
+            for m, ref in enumerate((rows, means[1]))
         ]
         value = both[0] + both[1]
         for k in range(PEERS):
@@ -282,25 +286,25 @@
     ]
     for copy in exchanged:
         copy.start()
-    load = pltpu.make_async_copy(down_b, rows.at[0], load_sems.at[0])
+    load = pltpu.make_async_copy(down_b, rows, load_sems.at[0])
     load.start()
     load.wait()
-    spread_out(rows.at[0], spread)
+    spread_out(rows, spread)
     collect(2, 3)
 
-    def place(a, initial, out):
-        width = widths[a]
+    def place(a, initial):
+        width, out = widths[a], means[a]
         tiles = width // LANES
         lanes = pl.ds(0, width)
         table[...] = first_of(slot[...], tiles)
         to_table = pltpu.make_async_copy(table, begins, own_sem)
         to_table.start()
-        ours = pltpu.make_async_copy(initial.at[:, lanes], rows.at[1, :, lanes], load_sems.at[1])
+        ours = pltpu.make_async_copy(initial.at[:, lanes], out, load_sems.at[1])
         ours.start()
-        own_rows = pltpu.make_async_copy(sent[a].at[0], rows.at[0, pl.ds(0, slots), lanes], stage_sems.at[0])
+        own_rows = pltpu.make_async_copy(sent[a].at[0], rows.at[pl.ds(0, slots), lanes], stage_sems.at[0])
         own_rows.start()
         fetched = [
-            pltpu.make_async_copy(moved[a].at[k], rows.at[0, pl.ds(k * slots, slots), lanes], strip_sems.at[k])
+            pltpu.make_async_copy(moved[a].at[k], rows.at[pl.ds(k * slots, slots), lanes], strip_sems.at[k])
             for k in range(1, PEERS)
         ]
         for copy in fetched:
@@ -308,7 +312,7 @@
         own_rows.wait()
         for copy in fetched:
             copy.wait()
-        spread_out(rows.at[0], spread, tiles)
+        spread_out(rows, spread, tiles)
         to_table.wait()
         ours.wait()
         read = table_reader(begins)
@@ -317,20 +321,16 @@
             for row, c, tile in rows_of(lambda s: read(j, s), spread, turn, tiles):
                 at = pl.ds(pl.multiple_of(j * ROWS + row, 16), 16)
                 columns = slice(c * LANES, (c + 1) * LANES)
-                mean = (rows[1, at, columns].astype(jnp.float32) + tile) * 0.5
-                rows[1, at, columns] = mean.astype(jnp.bfloat16)
+                out[at, columns] = ((out[at, columns].astype(jnp.float32) + tile) * 0.5).astype(jnp.bfloat16)
             return carry
 
         lax.fori_loop(0, count // ROWS, step, 0)
-        written = pltpu.make_async_copy(rows.at[1, :, lanes], out, load_sems.at[1])
-        written.start()
-        written.wait()
 
     held_back = 3 * len(ORDER)
     receive(len(ORDER), held_back)
-    place(0, up_a, means[0])
+    place(0, up_a)
     receive(2 * len(ORDER), held_back)
-    place(1, gate_a, means[1])
+    place(1, gate_a)
     for copy in exchanged:
         copy.wait()
     for block in range(PEERS):
@@ -343,14 +343,14 @@
     receive(held_back - 3, held_back)
     push(len(items))
     receive(held_back)
-    place(2, down_a, means[2])
+    place(2, down_a)
     receive(len(items))
     for a, k in items:
         item(a, k).wait_send()
 
 
-def last_kernel(cut, begins, up_ref, gate_ref, down_ref, costs_ref, own_ref, moved_ref, initial, *refs):
-    up_out, gate_out, down_out, costs_out, rows, ours, spread, turn, sems = refs
+def last_kernel(cut, begin_ref, up_ref, gate_ref, down_ref, costs_ref, own_ref, moved_ref, initial, *refs):
+    up_out, gate_out, down_out, costs_out, begins, rows, ours, spread, turn, sems, out_sems = refs
     count, features = initial.shape
     slots = count // PEERS
     width = features - cut
@@ -361,14 +361,9 @@
         pltpu.make_async_copy(moved_ref.at[k], rows.at[pl.ds(k * slots, slots)], sems.at[k]) for k in range(1, PEERS)
     ]
     fetched.append(pltpu.make_async_copy(initial.at[:, right], ours, sems.at[PEERS]))
-    handed = []
-    piece = count // PARTS
-    for n in range(PARTS):
-        at = pl.ds(n * piece, piece)
-        pairs = ((up_ref, up_out.at[at]), (gate_ref, gate_out.at[at]), (down_ref, down_out.at[at, left]))
-        for m, (src, dst) in enumerate(pairs):
-            handed.append(pltpu.make_async_copy(src.at[at], dst, sems.at[PEERS + 1 + 3 * n + m]))
-    handed.append(pltpu.make_async_copy(costs_ref, costs_out, sems.at[PEERS + 1 + 3 * PARTS]))
+    fetched.append(pltpu.make_async_copy(begin_ref, begins, sems.at[PEERS + 1]))
+    ways = ((up_ref, up_out), (gate_ref, gate_out), (down_ref, down_out.at[:, left]), (costs_ref, costs_out))
+    handed = [pltpu.make_async_copy(src, dst, out_sems.at[n]) for n, (src, dst) in enumerate(ways)]
     for copy in fetched + handed:
         copy.start()
     for copy in fetched:
@@ -383,12 +378,16 @@
             ours[at, columns] = ((ours[at, columns].astype(jnp.float32) + tile) * 0.5).astype(jnp.bfloat16)
         return carry
 
-    lax.fori_loop(0, count // ROWS, step, 0)
-    written = pltpu.make_async_copy(ours, down_out.at[:, right], sems.at[0])
-    written.start()
-    for copy in handed:
-        copy.wait()
-    written.wait()
+    piece = count // PARTS
+    steps = piece // ROWS
+    written = []
+    for n in range(PARTS):
+        lax.fori_loop(n * steps, (n + 1) * steps, step, 0)
+        at = pl.ds(n * piece, piece)
+        written.append(pltpu.make_async_copy(ours.at[at], down_out.at[at, right], sems.at[n]))
+        written[n].start()
+    for copy in handed + written:
+        copy.wait()
 
 
 def balanced(up_a, gate_a, down_a, up_b, gate_b, down_b, perm):
@@ -400,19 +399,18 @@
     slots = count // PEERS
     lanes = -(-slots // LANES) * LANES
     tiles = features // LANES
-    vmem, smem = pl.BlockSpec(memory_space=pltpu.VMEM), pl.BlockSpec(memory_space=pltpu.SMEM)
-    hbm = pl.BlockSpec(memory_space=pltpu.HBM)
+    vmem, hbm = pl.BlockSpec(memory_space=pltpu.VMEM), pl.BlockSpec(memory_space=pltpu.HBM)
     bf16, f32, i32 = jnp.bfloat16, jnp.float32, jnp.int32
     group = A_DEV // cols
-    whole = jax.ShapeDtypeStruct((count, features), bf16)
+    whole, kept = jax.ShapeDtypeStruct((count, features), bf16), pltpu.VMEM((count, features), bf16)
     costs_shape = jax.ShapeDtypeStruct((group * PEERS, count), f32)
     lists = [jax.ShapeDtypeStruct((PEERS, slots, size), bf16) for size in (features, features, cut, features - cut)]
     begins, *parts = pl.pallas_call(
         functools.partial(main_kernel, count, cut),
-        out_shape=[jax.ShapeDtypeStruct((pad, LANES), i32), whole, whole, jax.ShapeDtypeStruct((count, cut), bf16), costs_shape]
+        out_shape=[pltpu.VMEM((pad, LANES), i32), kept, kept, pltpu.VMEM((count, cut), bf16), pltpu.VMEM(costs_shape.shape, f32)]
         + lists * 2,
         in_specs=[vmem] + [hbm] * 6,
-        out_specs=[vmem] + [hbm] * 3 + [vmem] + [hbm] * 8,
+        out_specs=[vmem] * 5 + [hbm] * 8,
         scratch_shapes=[
             pltpu.VMEM((slots, count), bf16),
             pltpu.VMEM((2 * PEERS, count), bf16),
@@ -427,7 +425,7 @@
             pltpu.VMEM((2 * A_DEV, features), bf16),
             pltpu.VMEM((PEERS, 2 * A_DEV, features), bf16),
             pltpu.VMEM((2, A_DEV * PEERS, features), bf16),
-            pltpu.VMEM((2, count, features), bf16),
+            pltpu.VMEM((count, features), bf16),
             pltpu.VMEM(((count + 8) * tiles, LANES), f32),
             pltpu.VMEM(((ROWS + 8) * tiles, LANES), f32),
             pltpu.VMEM((2, slots, features), bf16),
@@ -444,26 +442,28 @@
             pltpu.SemaphoreType.DMA,
         ],
         compiler_params=pltpu.CompilerParams(
-            collective_id=0, has_side_effects=True, vmem_limit_bytes=62 * 1024 * 1024
+            collective_id=0, has_side_effects=True, vmem_limit_bytes=40 * 1024 * 1024
         ),
     )(perm.reshape(used, LANES), up_a, gate_a, down_a, up_b, gate_b, down_b)
-    up_part, gate_part, down_part, costs_part = parts[:4]
-    own, moved = parts[7], parts[11]
+    near = [pltpu.with_memory_space_constraint(part, pltpu.VMEM) for part in (begins, *parts[:4])]
+    own, moved, initial = (pltpu.with_memory_space_constraint(part, pltpu.HBM) for part in (parts[7], parts[11], down_a))
     width = features - cut
     up_mean, gate_mean, down_mean, costs = pl.pallas_call(
         functools.partial(last_kernel, cut),
         out_shape=[whole, whole, whole, costs_shape],
-        in_specs=[smem] + [hbm] * 7,
+        in_specs=[vmem] * 5 + [hbm] * 3,
         out_specs=[hbm] * 4,
         scratch_shapes=[
+            pltpu.SMEM((pad, LANES), i32),
             pltpu.VMEM((count, width), bf16),
             pltpu.VMEM((count, width), bf16),
             pltpu.VMEM(((count + 8) * width // LANES, LANES), f32),
             pltpu.VMEM(((ROWS + 8) * width // LANES, LANES), f32),
-            pltpu.SemaphoreType.DMA((PEERS + 2 + 3 * PARTS,)),
+            pltpu.SemaphoreType.DMA((PEERS + 2,)),
+            pltpu.SemaphoreType.DMA((4,)),
         ],
-        compiler_params=pltpu.CompilerParams(vmem_limit_bytes=62 * 1024 * 1024),
-    )(begins, up_part, gate_part, down_part, costs_part, own, moved, down_a)
+        compiler_params=pltpu.CompilerParams(vmem_limit_bytes=12 * 1024 * 1024),
+    )(*near, own, moved, initial)
     return (costs.T, up_mean, gate_mean, down_mean)
 
 
@@ -529,7 +529,7 @@
     def local(up_a, *rest):
         row_count, features = up_a.shape
         even = mesh.shape["rows"] == PEERS and row_count % (PEERS * 16) == 0 and row_count % (A_DEV * 16) == 0
-        even = even and row_count % COST_ROWS == 0 and row_count % (16 * PARTS) == 0 and row_count % (PEERS * ROWS) == 0
+        even = even and row_count % COST_ROWS == 0 and row_count % (ROWS * PARTS) == 0 and row_count % (PEERS * ROWS) == 0
         even = even and features == 8 * LANES and mesh.shape["cols"] == A_DEV // 8
         return (balanced if even else general)(up_a, *rest)
 

time: 904 us -> 278 us (0.31)
  Pallas kernels: 903 us -> 277 us
    pallas_call x1, Pallas kernels: 641 us -> 16.7 us  [balanced(): pl.pallas_call(functools.partial(last_kernel, cut), out_shape=[whole, who...]
where the time goes in v6:
time: 278 us
  Pallas kernels  277 us (100%)
    pallas_call x1, Pallas kernels, balanced(): pl.pallas_call(functools.partial(main_kernel, count, cut), out_shape=[plt...  260 us
    pallas_call x1, Pallas kernels, balanced(): pl.pallas_call(functools.partial(last_kernel, cut), out_shape=[whole, who...  16.7 us

profile of v6, /device:TPU:0, one launch (start us, length us, event | category | flops | bytes accessed | tf_op | source)
XLA Modules:
  0.0 277.7 jit_solution(9596773098108181311)
XLA Ops:
  0.6 260.3 %shard_map.102 = (s32[32,128]{1,0:T(8,128)S(1)}, bf16[3584,1024]{1,0:T(8,128)(2,1)S(1)}, bf16[3584,1024]{1,0:T(8,128)(2,1)S(1)}, bf16[3584,768]{1,0:T(8,128)(2,1...) custom-call(s32[28,128]{1,0:T(8,128)} %bitcast.2, ...), custom_call_target="tpu_custom_call" | custom-call | tf_op jit(solution)/shard_map/pallas_call | solution.py:408
  261.0 16.7 %shard_map.103 = (bf16[3584,1024]{1,0:T(8,128)(2,1)}, bf16[3584,1024]{1,0:T(8,128)(2,1)}, bf16[3584,1024]{1,0:T(8,128)(2,1)}, f32[64,3584]{1,0:T(8,128)}) custom-call(s32[32,128]{1,0:T(8,128)S(1)} %get-tuple-element.15.begin_ref, bf16[3584,1024]{1,0:T(8,128)(2,1)S(1)} %get-tuple-element.16.up_ref, bf16[3584,1024]{1,0:T(8,128)(2,1)S(1)} %get-tuple-element.17.gate_ref, ...), custom_call_target="tpu_custom_call" | custom-call | tf_op jit(solution)/shard_map/pallas_call | solution.py:451

commit v7 on v6

--- a/solution.py
+++ b/solution.py
@@ -104,6 +104,15 @@
             yield h * 16, c, jnp.concatenate(both, axis=0)
 
 
+def paired(begin):
+    return begin | lax.shift_left(pltpu.roll(begin, begin.shape[1] - 1, 1), 16)
+
+
+def half(read, s):
+    word = read(s // 2 * 2)
+    return lax.shift_right_logical(word, 16) if s % 2 else word & 0xFFFF
+
+
 def table_reader(table):
     per = LANES // ROWS
 
@@ -147,29 +156,28 @@
     for copy in loads:
         copy.start()
 
+    def remote(src, dst, send, recv, peer, axis="rows"):
+        return pltpu.make_async_remote_copy(
+            src_ref=src, dst_ref=dst, send_sem=send, recv_sem=recv, device_id={axis: peer}, device_id_type=MESH
+        )
+
+    count_ranks(count, me, perm_ref, slot, hot, halves, padded, ask)
+    pl.semaphore_wait(barrier, PEERS - 1 + cols - 1)
+    asks = [remote(ask.at[me ^ k], got.at[k], ask_send.at[k], ask_recv.at[k], me ^ k) for k in ORDER]
+    for copy in asks:
+        copy.start()
+    own = pltpu.make_async_copy(ask.at[me], got.at[0], own_sem)
+    own.start()
     for copy in strips:
         copy.wait()
     shape = (2 * A_DEV, 32 * A_DEV)
     first = lax.broadcasted_iota(jnp.int32, shape, 0) * 16 == lax.broadcasted_iota(jnp.int32, shape, 1)
     window[...] = matmul(one_hot(first), held[...]).astype(jnp.bfloat16)
     windows[0] = window[...]
-    pl.semaphore_wait(barrier, PEERS - 1 + cols - 1)
-
-    def remote(src, dst, send, recv, peer, axis="rows"):
-        return pltpu.make_async_remote_copy(
-            src_ref=src, dst_ref=dst, send_sem=send, recv_sem=recv, device_id={axis: peer}, device_id_type=MESH
-        )
-
     across = [remote(window, windows.at[k], win_send.at[k], win_recv.at[k], me ^ k) for k in (6, 2, 4)]
     for copy in across:
         copy.start()
 
-    count_ranks(count, me, perm_ref, slot, hot, halves, padded, ask)
-    asks = [remote(ask.at[me ^ k], got.at[k], ask_send.at[k], ask_recv.at[k], me ^ k) for k in ORDER]
-    for copy in asks:
-        copy.start()
-    own = pltpu.make_async_copy(ask.at[me], got.at[0], own_sem)
-    own.start()
     begin_ref[...] = first_of(slot[...], widths[3] // LANES)
     loads[0].wait()
     spread_out(rows, spread)
@@ -350,7 +358,7 @@
 
 
 def last_kernel(cut, begin_ref, up_ref, gate_ref, down_ref, costs_ref, own_ref, moved_ref, initial, *refs):
-    up_out, gate_out, down_out, costs_out, begins, rows, ours, spread, turn, sems, out_sems = refs
+    up_out, gate_out, down_out, costs_out, table, begins, rows, ours, spread, turn, sems, out_sems = refs
     count, features = initial.shape
     slots = count // PEERS
     width = features - cut
@@ -361,7 +369,8 @@
         pltpu.make_async_copy(moved_ref.at[k], rows.at[pl.ds(k * slots, slots)], sems.at[k]) for k in range(1, PEERS)
     ]
     fetched.append(pltpu.make_async_copy(initial.at[:, right], ours, sems.at[PEERS]))
-    fetched.append(pltpu.make_async_copy(begin_ref, begins, sems.at[PEERS + 1]))
+    table[...] = paired(begin_ref[...])
+    fetched.append(pltpu.make_async_copy(table, begins, sems.at[PEERS + 1]))
     ways = ((up_ref, up_out), (gate_ref, gate_out), (down_ref, down_out.at[:, left]), (costs_ref, costs_out))
     handed = [pltpu.make_async_copy(src, dst, out_sems.at[n]) for n, (src, dst) in enumerate(ways)]
     for copy in fetched + handed:
@@ -372,7 +381,7 @@
     read = table_reader(begins)
 
     def step(j, carry):
-        for row, c, tile in rows_of(lambda s: read(j, s), spread, turn, tiles):
+        for row, c, tile in rows_of(lambda s: half(lambda even: read(j, even), s), spread, turn, tiles):
             at = pl.ds(pl.multiple_of(j * ROWS + row, 16), 16)
             columns = slice(c * LANES, (c + 1) * LANES)
             ours[at, columns] = ((ours[at, columns].astype(jnp.float32) + tile) * 0.5).astype(jnp.bfloat16)
@@ -454,6 +463,7 @@
         in_specs=[vmem] * 5 + [hbm] * 3,
         out_specs=[hbm] * 4,
         scratch_shapes=[
+            pltpu.VMEM((pad, LANES), i32),
             pltpu.SMEM((pad, LANES), i32),
             pltpu.VMEM((count, width), bf16),
             pltpu.VMEM((count, width), bf16),
@@ -530,7 +540,7 @@
         row_count, features = up_a.shape
         even = mesh.shape["rows"] == PEERS and row_count % (PEERS * 16) == 0 and row_count % (A_DEV * 16) == 0
         even = even and row_count % COST_ROWS == 0 and row_count % (ROWS * PARTS) == 0 and row_count % (PEERS * ROWS) == 0
-        even = even and features == 8 * LANES and mesh.shape["cols"] == A_DEV // 8
+        even = even and features == 8 * LANES and mesh.shape["cols"] == A_DEV // 8 and row_count * 8 < 2**15
         return (balanced if even else general)(up_a, *rest)
 
     placed = (P("rows", "cols"),) * 6 + (P("rows"),)

time: 278 us -> 272 us (0.978)
  Pallas kernels: 277 us -> 271 us
    pallas_call x1, Pallas kernels: 260 us -> 256 us  [balanced(): pl.pallas_call(functools.partial(main_kernel, count, cut), out_shape=[plt...]
where the time goes in v7:
time: 272 us
  Pallas kernels  271 us (100%)
    pallas_call x1, Pallas kernels, balanced(): pl.pallas_call(functools.partial(main_kernel, count, cut), out_shape=[plt...  256 us
    pallas_call x1, Pallas kernels, balanced(): pl.pallas_call(functools.partial(last_kernel, cut), out_shape=[whole, who...  15.2 us

profile of v7, /device:TPU:0, one launch (start us, length us, event | category | flops | bytes accessed | tf_op | source)
XLA Modules:
  0.0 272.0 jit_solution(3780752263245351979)
XLA Ops:
  0.6 256.2 %shard_map.102 = (s32[32,128]{1,0:T(8,128)S(1)}, bf16[3584,1024]{1,0:T(8,128)(2,1)S(1)}, bf16[3584,1024]{1,0:T(8,128)(2,1)S(1)}, bf16[3584,768]{1,0:T(8,128)(2,1...) custom-call(s32[28,128]{1,0:T(8,128)} %bitcast.2, ...), custom_call_target="tpu_custom_call" | custom-call | tf_op jit(solution)/shard_map/pallas_call | solution.py:417
  256.8 15.2 %shard_map.103 = (bf16[3584,1024]{1,0:T(8,128)(2,1)}, bf16[3584,1024]{1,0:T(8,128)(2,1)}, bf16[3584,1024]{1,0:T(8,128)(2,1)}, f32[64,3584]{1,0:T(8,128)}) custom-call(s32[32,128]{1,0:T(8,128)S(1)} %get-tuple-element.15.begin_ref, bf16[3584,1024]{1,0:T(8,128)(2,1)S(1)} %get-tuple-element.16.up_ref, bf16[3584,1024]{1,0:T(8,128)(2,1)S(1)} %get-tuple-element.17.gate_ref, ...), custom_call_target="tpu_custom_call" | custom-call | tf_op jit(solution)/shard_map/pallas_call | solution.py:460

commit v8 on v7

--- a/solution.py
+++ b/solution.py
@@ -373,10 +373,12 @@
     fetched.append(pltpu.make_async_copy(table, begins, sems.at[PEERS + 1]))
     ways = ((up_ref, up_out), (gate_ref, gate_out), (down_ref, down_out.at[:, left]), (costs_ref, costs_out))
     handed = [pltpu.make_async_copy(src, dst, out_sems.at[n]) for n, (src, dst) in enumerate(ways)]
-    for copy in fetched + handed:
-        copy.start()
     for copy in fetched:
-        copy.wait()
+        copy.start()
+    for copy in fetched:
+        copy.wait()
+    for copy in handed:
+        copy.start()
     spread_out(rows, spread)
     read = table_reader(begins)
 

time: 272 us -> 269 us (0.989)
  Pallas kernels: 271 us -> 268 us
    pallas_call x1, Pallas kernels: 15.2 us -> 12.2 us  [balanced(): pl.pallas_call(functools.partial(last_kernel, cut), out_shape=[whole, who...]
where the time goes in v8:
time: 269 us
  Pallas kernels  268 us (100%)
    pallas_call x1, Pallas kernels, balanced(): pl.pallas_call(functools.partial(main_kernel, count, cut), out_shape=[plt...  256 us
    pallas_call x1, Pallas kernels, balanced(): pl.pallas_call(functools.partial(last_kernel, cut), out_shape=[whole, who...  12.2 us

profile of v8, /device:TPU:0, one launch (start us, length us, event | category | flops | bytes accessed | tf_op | source)
XLA Modules:
  0.0 269.0 jit_solution(15775692761566754689)
XLA Ops:
  0.6 256.2 %shard_map.102 = (s32[32,128]{1,0:T(8,128)S(1)}, bf16[3584,1024]{1,0:T(8,128)(2,1)S(1)}, bf16[3584,1024]{1,0:T(8,128)(2,1)S(1)}, bf16[3584,768]{1,0:T(8,128)(2,1...) custom-call(s32[28,128]{1,0:T(8,128)} %bitcast.2, ...), custom_call_target="tpu_custom_call" | custom-call | tf_op jit(solution)/shard_map/pallas_call | solution.py:419
  256.8 12.2 %shard_map.103 = (bf16[3584,1024]{1,0:T(8,128)(2,1)}, bf16[3584,1024]{1,0:T(8,128)(2,1)}, bf16[3584,1024]{1,0:T(8,128)(2,1)}, f32[64,3584]{1,0:T(8,128)}) custom-call(s32[32,128]{1,0:T(8,128)S(1)} %get-tuple-element.15.begin_ref, bf16[3584,1024]{1,0:T(8,128)(2,1)S(1)} %get-tuple-element.16.up_ref, bf16[3584,1024]{1,0:T(8,128)(2,1)S(1)} %get-tuple-element.17.gate_ref, ...), custom_call_target="tpu_custom_call" | custom-call | tf_op jit(solution)/shard_map/pallas_call | solution.py:462
